TPU v7x, 256 devices: a whole 4x4x8 slice. The times are simulated.
256 devices in a mesh: row: 32 (over z, x), col: 8 (over y, core).
Axes of the slice: x: 4, y: 4, z: 8, core: 2. Of those that a mesh axis runs over, the one named last changes fastest.
Arguments:
- right_side: float32 [15, 512, 512], P(None, 'row'), may hold values from -6 to 6
- off_blocks: float32 [8, 512, 2176], P('col', 'row'), may hold values from -0.09375 to 0.09375
- diag_inverse: float32 [8, 512, 960], P('col', 'row'), as said below
Outputs:
- forward_solution: float32 [8, 960, 512], P('col')
- solution: float32 [8, 4, 512, 512], P('col', None, 'row')
Inputs may be any that keep to these rules, and one draw needn't show every extreme that they name: `diag_inverse`: read through the block map of the first step, each block D(n) is lower triangular with a positive diagonal between 0.5 and 2.
All inputs are finite; a program needn't handle non-finite values.
Results may differ from a plain program's by a relative error of at most 0.00011.
Values sent between devices are 32-bit elements; how exact they have to be, the bound alone decides.
No kernel may reach another device: no remote copies, remote signals or barrier semaphores. Data moves between devices by JAX's collectives and lax.ppermute only.
A program may use at most 64 MiB of HBM per device.

v0:
```python
import functools

import jax
import jax.numpy as jnp
import numpy as np
from jax import lax
from jax.experimental import pallas as pl
from jax.experimental.pallas import tpu as pltpu
from jax.sharding import Mesh, PartitionSpec as P

SIZES = {"z": 8, "x": 4, "y": 4, "core": 2}
F32, BF16 = jnp.float32, jnp.bfloat16


def shift(value, axis, by):
    size = SIZES[axis]
    return lax.ppermute(value, axis, [(i, (i + by) % size) for i in range(size)])


def swap(value, axis, mask):
    return lax.ppermute(value, axis, [(i, i ^ mask) for i in range(SIZES[axis])])


def ring_z(block):
    half = block.shape[0] // 2
    parts = [block] + [None] * 7
    up = down = block
    for step in range(1, 4):
        up, down = shift(up, "z", 1), shift(down, "z", -1)
        parts[step], parts[8 - step] = up, down
    parts[4] = (shift(up[:half], "z", 1), shift(down[half:], "z", -1))
    return parts


def ring_x(block):
    half = block.shape[0] // 2
    up, down = shift(block, "x", 1), shift(block, "x", -1)
    return [block, up, (shift(up[:half], "x", 1), shift(down[half:], "x", -1)), down]


def cut(array, start, width):
    return lax.slice_in_dim(array, start, start + width, axis=1)


def parts_of(value):
    high = value.astype(BF16)
    return high, (value - high.astype(F32)).astype(BF16)


def times(value, high, low, dims):
    vh, vl = parts_of(value)
    dot = functools.partial(lax.dot_general, dimension_numbers=((dims, ((), ()))), preferred_element_type=F32)
    return dot(vh, high) + (dot(vl, high) + dot(vh, low))


def mm(value, matrix):
    return times(value, *matrix, ((1,), (0,)))


def mmt(value, matrix):
    return times(value, *matrix, ((1,), (1,)))


def whole(ref, columns):
    return ref[0, :, columns], ref[1, :, columns]


def rows_of_a(refs):
    order = [(0, 64), (64, 64), (128, 64), (192, 64), (256, 32), (288, 32), (320, 64), (384, 64), (448, 64)]
    return [(start, size, ref) for (start, size), ref in zip(order, refs)]


def rows_of_b(refs):
    found = []
    for k, first, count, ref in ((0, 0, 8, refs[0]), (1, 0, 8, refs[1]), (2, 0, 4, refs[2]), (2, 4, 4, refs[3]),
                                 (3, 0, 8, refs[4])):
        found += [((first + s) * 64 + k * 16, s, ref) for s in range(count)]
    return found


def mine_kernel(*refs):
    out = refs[14]
    for start, size, ref in rows_of_a(refs[:9]):
        out[start:start + size, 0:512] = ref[:, 1536:2048]
    for start, s, ref in rows_of_b(refs[9:14]):
        out[start:start + 16, 512:1536] = ref[s, :, 512:1536]


def level3_kernel(core_ref, *refs):
    a_refs, b_refs = rows_of_a(refs[:9]), rows_of_b(refs[9:14])
    mat, y3_out, y3t_out, kept_out, given_out, b2t_out, b1t_out, b0t_out, rhs, up = refs[14:]
    for start, size, ref in a_refs:
        rhs[start:start + size, 0:320] = ref[:, 2048:2368]
        high, low = parts_of(ref[:, 0:1536])
        mat[0, start:start + size, 0:1536] = high
        mat[1, start:start + size, 0:1536] = low
    for start, s, ref in b_refs:
        high, low = parts_of(ref[s, :, 0:512])
        mat[0, start:start + 16, 1536:2048] = high
        mat[1, start:start + 16, 1536:2048] = low
    rhs[:, 320:384] = jnp.zeros((512, 64), F32)
    b3t = rhs[:, 0:128].T
    b21t = rhs[:, 128:256].T
    b2t_out[...] = b21t[0:64]
    b1t_out[...] = b21t[64:128]
    b0t_out[...] = rhs[:, 256:384].T[0:64]
    y3t = mm(b3t, whole(mat, slice(1536, 2048)))
    y3t_out[...] = y3t
    y3_out[...] = y3t.T
    for at, column in ((0, 1024), (512, 512), (1024, 0)):
        up[:, at:at + 512] = mmt(y3t, whole(mat, slice(column, column + 512)))
    core = core_ref[0]
    kept_out[...] = up[pl.ds(pl.multiple_of(64 * core, 64), 64), :]
    given_out[...] = up[pl.ds(pl.multiple_of(64 * (1 - core), 64), 64), :]


def level2_kernel(mine, theirs, kept, got, b2t, mat, y2t_out, up_out):
    for i in range(6):
        for j, ref in ((0, mine), (256, theirs)):
            high, low = parts_of(ref[:, 256 * i:256 * i + 256])
            mat[0, :, 512 * i + j:512 * i + j + 256] = high
            mat[1, :, 512 * i + j:512 * i + j + 256] = low
    up3 = kept[...] + got[...]
    y2t = mm(b2t[...] - up3[:, 0:512], whole(mat, slice(1024, 1536)))
    y2t_out[...] = y2t
    up_out[:, 0:512] = up3[:, 512:1024] + mmt(y2t, whole(mat, slice(512, 1024)))
    up_out[:, 512:1024] = up3[:, 1024:1536] + mmt(y2t, whole(mat, slice(0, 512)))


def level1_kernel(up_ref, got, b1t, mat, y1t_out, up_out):
    y1t = mm(b1t[...] - (up_ref[:, 0:512] + got[:, 0:512]), whole(mat, slice(2048, 2560)))
    y1t_out[...] = y1t
    up_out[...] = (up_ref[:, 512:1024] + got[:, 512:1024]) + mmt(y1t, whole(mat, slice(1536, 2048)))


def level0_kernel(up_ref, got, b0t, y2t, y1t, mat, y0t_out, low_out):
    l02, l12, d2, l01, d1, d0 = (whole(mat, slice(512 * i, 512 * i + 512)) for i in range(6))
    y0t = mm(b0t[...] - (up_ref[...] + got[...]), d0)
    y0t_out[...] = y0t
    x0t = mmt(y0t, d0)
    low_out[:, 0:512] = x0t
    x1t = mmt(y1t[...] - mm(x0t, l01), d1)
    low_out[:, 512:1024] = x1t
    low_out[:, 1024:1536] = mmt(y2t[...] - mm(x0t, l02) - mm(x1t, l12), d2)


def last_kernel(core_ref, low, got, y3t, mat, x_out, both, tops):
    core = core_ref[0]
    both[pl.ds(pl.multiple_of(64 * core, 64), 64), :] = low[...]
    both[pl.ds(pl.multiple_of(64 * (1 - core), 64), 64), :] = got[...]
    rest = y3t[...]
    for k in range(3):
        rest = rest - mm(both[:, 512 * k:512 * k + 512], whole(mat, slice(512 * k, 512 * k + 512)))
        tops[:, 64 * k:64 * k + 64] = both[:, 512 * k:512 * k + 64]
    tops[:, 192:256] = mmt(rest, (mat[0, 0:64, 1536:2048], mat[1, 0:64, 1536:2048]))
    x_out[...] = tops[...].T


def rows_kernel(core_ref, y0t, y1t, y2t, got, out, both):
    core = core_ref[0]
    here, there = pl.multiple_of(64 * core, 64), pl.multiple_of(64 * (1 - core), 64)
    both[pl.ds(here, 64), 0:64] = y0t[:, 0:64]
    both[pl.ds(here, 64), 64:192] = y1t[:, 0:128]
    both[pl.ds(here, 64), 192:448] = y2t[:, 0:256]
    both[pl.ds(there, 64), 0:448] = got[...]
    both[:, 448:512] = jnp.zeros((128, 64), F32)
    out[...] = both[...].T[0:448]


def call(kernel, name, outs, *args, scalars=0, scratch=()):
    in_specs = [pl.BlockSpec(memory_space=pltpu.SMEM)] * scalars
    in_specs += [pl.BlockSpec(memory_space=pltpu.VMEM)] * (len(args) - scalars)
    return pl.pallas_call(
        kernel,
        name=name,
        out_shape=[jax.ShapeDtypeStruct(shape, kind) for shape, kind in outs],
        in_specs=in_specs,
        out_specs=[pl.BlockSpec(memory_space=pltpu.VMEM)] * len(outs),
        scratch_shapes=list(scratch),
        compiler_params=pltpu.CompilerParams(vmem_limit_bytes=40 * 2**20),
    )(*args)


def per_device(right_side, off_blocks, diag_inverse):
    off, diag = off_blocks[0], diag_inverse[0]
    x, y, core = lax.axis_index("x"), lax.axis_index("y"), lax.axis_index("core")
    column = 2 * y + core
    core_at = jnp.reshape(core, (1,)).astype(jnp.int32)

    chain = [lax.dynamic_index_in_dim(right_side, 2**k - 1 + (column >> (3 - k)), 0, keepdims=False)
             for k in range(4)]
    stream_a = jnp.concatenate([cut(off, 640, 1536), cut(off, 128, 512)], axis=1)
    rows_a = []
    for k in range(4):
        target = lax.rem(x + k, 4) * 128
        pieces = [lax.dynamic_slice(chain[3], (0, target), (16, 128))]
        pieces += [lax.dynamic_slice(chain[m], (0, target + 64 * core), (16, 64)) for m in (2, 1, 0)]
        block = jnp.concatenate([stream_a] + pieces, axis=1)
        rows_a.append(shift(block, "x", k) if k else block)
    blocks_a = ring_z(jnp.concatenate(rows_a, axis=0))
    blocks_a = blocks_a[:4] + list(blocks_a[4]) + blocks_a[5:]

    small = jnp.concatenate([cut(off, 0, 128), cut(diag, 0, 192)], axis=1)
    other = swap(small, "y", 1)
    pair_d0 = jnp.concatenate([cut(small, 128, 64), cut(other, 128, 64)], axis=1)
    stream_b = jnp.concatenate(
        [cut(diag, 448, 512), cut(diag, 192, 256),
         cut(small, 0, 128), cut(other, 0, 128), cut(small, 192, 128), cut(other, 192, 128),
         pair_d0, swap(pair_d0, "y", 2)], axis=1)
    rows_b = ring_z(stream_b)
    rows_b[4] = jnp.concatenate(rows_b[4], axis=0)
    blocks_b = ring_x(jnp.stack(rows_b, axis=0))
    blocks_b = blocks_b[:2] + list(blocks_b[2]) + blocks_b[3:]

    (mine,) = call(mine_kernel, "mine", [((512, 1536), F32)], *blocks_a, *blocks_b)
    theirs = swap(mine, "core", 1)

    mat3, y3, y3t, kept, given, b2t, b1t, b0t = call(
        level3_kernel, "level3",
        [((2, 512, 2048), BF16), ((512, 128), F32), ((128, 512), F32), ((64, 1536), F32), ((64, 1536), F32),
         ((64, 512), F32), ((64, 512), F32), ((64, 512), F32)],
        core_at, *blocks_a, *blocks_b, scalars=1,
        scratch=[pltpu.VMEM((512, 384), F32), pltpu.VMEM((128, 1536), F32)])
    got = swap(given, "core", 1)
    mat, y2t, up = call(level2_kernel, "level2",
                        [((2, 512, 3072), BF16), ((64, 512), F32), ((64, 1024), F32)], mine, theirs, kept, got, b2t)
    got = swap(up, "y", 1)
    y1t, up = call(level1_kernel, "level1", [((64, 512), F32), ((64, 512), F32)], up, got, b1t, mat)
    got = swap(up, "y", 2)
    y0t, low = call(level0_kernel, "level0", [((64, 512), F32), ((64, 1536), F32)], up, got, b0t, y2t, y1t, mat)

    x_all = call(last_kernel, "last", [((256, 128), F32)], core_at, low, swap(low, "core", 1), y3t, mat3, scalars=1,
                 scratch=[pltpu.VMEM((128, 1536), F32), pltpu.VMEM((128, 256), F32)])[0]
    chain_x = x_all.reshape(4, 4, 16, 128)
    backward = jnp.zeros((4, 16, 512), F32)
    for k in range(4):
        part = chain_x[:, k]
        part = shift(part, "x", -k) if k else part
        backward = lax.dynamic_update_slice(backward, part, (0, 0, lax.rem(x + k, 4) * 128))

    got = swap(jnp.concatenate([y0t[:, 256:320], y1t[:, 256:384], y2t[:, 256:512]], axis=1), "core", 1)
    (low_rows,) = call(rows_kernel, "rows", [((448, 128), F32)], core_at, y0t, y1t, y2t, got, scalars=1,
                       scratch=[pltpu.VMEM((128, 512), F32)])
    forward = jnp.zeros((960, 512), F32)
    for first, piece in ((448, y3), (0, low_rows)):
        for k in range(4):
            part = shift(piece, "x", k) if k else piece
            forward = lax.dynamic_update_slice(forward, part, (first, lax.rem(x + 4 - k, 4) * 128))
    return forward[None], backward[None]


def solution(mesh):
    split = Mesh(np.asarray(mesh.devices).reshape(8, 4, 4, 2), ("z", "x", "y", "core"))
    row, col = ("z", "x"), ("y", "core")
    return jax.shard_map(
        per_device,
        mesh=split,
        in_specs=(P(None, row, None), P(col, row, None), P(col, row, None)),
        out_specs=(P(col, None, None), P(col, None, row, None)),
        check_vma=False,
    )
```

profile of v0, /device:TPU:1, one launch (start us, length us, event | category | flops | bytes accessed | tf_op | source)
XLA Modules:
  0.0 161.5 jit_solution(6034328121404918091)
XLA Ops:
  16.1 2.6 %collective-permute-start.12 = (f32[16,128]{1,0:T(8,128)S(1)}, f32[16,128]{1,0:T(8,128)S(1)}, u32[]{:S(2)}, u32[]{:S(2)}) collective-permute-start(f32[16,128]{1,0:T(8,128)S(1)} %pad_maximum_fusion.3), channel_id=1, source_target_pairs={{0,4},{2,6},{4,0},{6,2},{1,5},{3,7},{5,1},{7,3},{8,12},{10,14},{12... | collective-permute-start | bytes 24584 | tf_op jit(solution)/shard_map/ppermute | solution.py:21
  21.9 4.0 %collective-permute-start.17 = (f32[16,1536]{1,0:T(8,128)S(1)}, f32[16,1536]{1,0:T(8,128)S(1)}, u32[]{:S(2)}, u32[]{:S(2)}) collective-permute-start(f32[16,1536]{1,0:T(8,128)S(1)} %concatenate.43), channel_id=1, source_target_pairs={{0,224},{32,0},{64,32},{96,64},{128,96},{160,128},{192,160},{224,1... | collective-permute-start | bytes 294920 | tf_op jit(solution)/shard_map/ppermute | solution.py:17
  27.9 2.8 %collective-permute-start.18 = (f32[16,1536]{1,0:T(8,128)S(1)}, f32[16,1536]{1,0:T(8,128)S(1)}, u32[]{:S(2)}, u32[]{:S(2)}) collective-permute-start(f32[16,1536]{1,0:T(8,128)S(1)} %collective-permute-done.17), channel_id=1, source_target_pairs={{0,224},{32,0},{64,32},{96,64},{128,96},{160,128},{192,160},{224,1... | collective-permute-start | bytes 294920 | tf_op jit(solution)/shard_map/ppermute | solution.py:17
  32.5 2.8 %collective-permute-start.19 = (f32[16,1536]{1,0:T(8,128)S(1)}, f32[16,1536]{1,0:T(8,128)S(1)}, u32[]{:S(2)}, u32[]{:S(2)}) collective-permute-start(f32[16,1536]{1,0:T(8,128)S(1)} %collective-permute-done.18), channel_id=1, source_target_pairs={{0,224},{32,0},{64,32},{96,64},{128,96},{160,128},{192,160},{224,1... | collective-permute-start | bytes 294920 | tf_op jit(solution)/shard_map/ppermute | solution.py:17
  35.3 10.7 %collective-permute-done.15 = f32[16,1536]{1,0:T(8,128)S(1)} collective-permute-done((f32[16,1536]{1,0:T(8,128)S(1)}, f32[16,1536]{1,0:T(8,128)S(1)}, u32[]{:S(2)}, u32[]{:S(2)}) %collective-permute-start.15) | collective-permute-done | bytes 98336 | tf_op jit(solution)/shard_map/ppermute | solution.py:17
  56.0 5.0 %collective-permute-done.8.refs_7_ = f32[64,2368]{1,0:T(8,128)S(1)} collective-permute-done((f32[64,2368]{1,0:T(8,128)S(1)}, f32[64,2368]{1,0:T(8,128)S(1)}, u32[]{:S(2)}, u32[]{:S(2)}) %collective-permute-start.8) | collective-permute-done | bytes 606240 | tf_op jit(solution)/shard_map/ppermute | solution.py:17
  61.0 3.1 %collective-permute-start.9 = (f32[64,2368]{1,0:T(8,128)S(1)}, f32[64,2368]{1,0:T(8,128)S(1)}, u32[]{:S(2)}, u32[]{:S(2)}) collective-permute-start(f32[64,2368]{1,0:T(8,128)S(1)} %collective-permute-done.8.refs_7_), channel_id=1, source_target_pairs={{0,224},{32,0},{64,32},{96,64},{128,96},{160,128},{192,160},{224,1... | collective-permute-start | bytes 1818632 | tf_op jit(solution)/shard_map/ppermute | solution.py:17
  65.5 2.9 %collective-permute-start.24 = (f32[4,16,1536]{2,1,0:T(8,128)S(1)}, f32[4,16,1536]{2,1,0:T(8,128)S(1)}, u32[]{:S(2)}, u32[]{:S(2)}) collective-permute-start(f32[4,16,1536]{2,1,0:T(8,128)S(1)} %slice.114), channel_id=1, source_target_pairs={{0,24},{8,0},{16,8},{24,16},{1,25},{9,1},{17,9},{25,17},{2,26},{10... | collective-permute-start | bytes 1179656 | tf_op jit(solution)/shard_map/ppermute | solution.py:17
  68.5 7.5 %collective-permute-done.9.refs_6_ = f32[64,2368]{1,0:T(8,128)S(1)} collective-permute-done((f32[64,2368]{1,0:T(8,128)S(1)}, f32[64,2368]{1,0:T(8,128)S(1)}, u32[]{:S(2)}, u32[]{:S(2)}) %collective-permute-start.9) | collective-permute-done | bytes 606240 | tf_op jit(solution)/shard_map/ppermute | solution.py:17
  75.9 3.5 %collective-permute-start.10 = (f32[32,2368]{1,0:T(8,128)S(1)}, f32[32,2368]{1,0:T(8,128)S(1)}, u32[]{:S(2)}, u32[]{:S(2)}) collective-permute-start(f32[32,2368]{1,0:T(8,128)S(1)} %slice.101), channel_id=1, source_target_pairs={{0,224},{32,0},{64,32},{96,64},{128,96},{160,128},{192,160},{224,1... | collective-permute-start | bytes 909320 | tf_op jit(solution)/shard_map/ppermute | solution.py:17
  79.6 7.1 %collective-permute-done.10.refs_5_ = f32[32,2368]{1,0:T(8,128)S(1)} collective-permute-done((f32[32,2368]{1,0:T(8,128)S(1)}, f32[32,2368]{1,0:T(8,128)S(1)}, u32[]{:S(2)}, u32[]{:S(2)}) %collective-permute-start.10) | collective-permute-done | bytes 303136 | tf_op jit(solution)/shard_map/ppermute | solution.py:17
  86.6 3.5 %collective-permute-done.6.refs_4_ = f32[32,2368]{1,0:T(8,128)S(1)} collective-permute-done((f32[32,2368]{1,0:T(8,128)S(1)}, f32[32,2368]{1,0:T(8,128)S(1)}, u32[]{:S(2)}, u32[]{:S(2)}) %collective-permute-start.6) | collective-permute-done | bytes 303136 | tf_op jit(solution)/shard_map/ppermute | solution.py:17
  90.3 11.2 %collective-permute-start.28 = (f32[512,1536]{1,0:T(8,128)S(1)}, f32[512,1536]{1,0:T(8,128)}, u32[]{:S(2)}, u32[]{:S(2)}) collective-permute-start(f32[512,1536]{1,0:T(8,128)S(1)} %mine.1), channel_id=1, source_target_pairs={{0,1},{1,0},{2,3},{3,2},{4,5},{5,4},{6,7},{7,6},{8,9},{9,8},{10,11... | collective-permute-start | bytes 9437192 | tf_op jit(solution)/shard_map/ppermute | solution.py:21
  101.5 3.0 %level3.1 = (bf16[2,512,2048]{2,1,0:T(8,128)(2,1)S(1)}, f32[512,128]{1,0:T(8,128)}, f32[128,512]{1,0:T(8,128)S(1)}, f32[64,1536]{1,0:T(8,128)S(1)}, f32[64,1536]...) custom-call(s32[1]{0:T(128)} %bitcast.core_ref, ...), custom_call_target="tpu_custom_call" | custom-call | tf_op jit(solution)/shard_map/level3/pallas_call | solution.py:173
  112.8 4.5 %level2.1 = (bf16[2,512,3072]{2,1,0:T(8,128)(2,1)S(1)}, f32[64,512]{1,0:T(8,128)S(1)}, f32[64,1024]{1,0:T(8,128)S(1)}) custom-call(f32[512,1536]{1,0:T(8,128)S(1)} %mine.1, f32[512,1536]{1,0:T(8,128)} %collective-permute-done.28.theirs, f32[64,1536]{1,0:T(8,128)S(1)} %get-tuple-element.18.kept, f32[64,1536]{1,0:T(8,128)} %collective-permute-done.29.got, ...), custom_call_target="tpu_custom_call" | custom-call | tf_op jit(solution)/shard_map/level2/pallas_call | solution.py:173
  118.8 4.9 %collective-permute-done.25 = f32[512,128]{1,0:T(8,128)} collective-permute-done((f32[512,128]{1,0:T(8,128)}, f32[512,128]{1,0:T(8,128)}, u32[]{:S(2)}, u32[]{:S(2)}) %collective-permute-start.25) | collective-permute-done | bytes 262176 | tf_op jit(solution)/shard_map/ppermute | solution.py:17
  125.7 2.7 %collective-permute-start.31 = (f32[64,512]{1,0:T(8,128)S(1)}, f32[64,512]{1,0:T(8,128)S(1)}, u32[]{:S(2)}, u32[]{:S(2)}) collective-permute-start(f32[64,512]{1,0:T(8,128)S(1)} %get-tuple-element.24.up_ref), channel_id=1, source_target_pairs={{0,4},{2,6},{4,0},{6,2},{1,5},{3,7},{5,1},{7,3},{8,12},{10,14},{12... | collective-permute-start | bytes 393224 | tf_op jit(solution)/shard_map/ppermute | solution.py:21
  128.4 2.6 %collective-permute-done.31.got = f32[64,512]{1,0:T(8,128)S(1)} collective-permute-done((f32[64,512]{1,0:T(8,128)S(1)}, f32[64,512]{1,0:T(8,128)S(1)}, u32[]{:S(2)}, u32[]{:S(2)}) %collective-permute-start.31) | collective-permute-done | bytes 131104 | tf_op jit(solution)/shard_map/ppermute | solution.py:21
  131.1 2.8 %level0.1 = (f32[64,512]{1,0:T(8,128)S(1)}, f32[64,1536]{1,0:T(8,128)S(1)}) custom-call(f32[64,512]{1,0:T(8,128)S(1)} %get-tuple-element.24.up_ref, f32[64,512]{1,0:T(8,128)S(1)} %collective-permute-done.31.got, f32[64,512]{1,0:T(8,128)S(1)} %copy-done.7, f32[64,512]{1,0:T(8,128)S(1)} %get-tuple-element.26.y2t, f32[64,512]{1,0:T(8,128)S(1)} %get-tuple-element.27.y1t, ...), custom_call_target="tpu_custom_call" | custom-call | tf_op jit(solution)/shard_map/level0/pallas_call | solution.py:173
  134.0 2.6 %collective-permute-start.32 = (f32[64,448]{1,0:T(8,128)S(1)}, f32[64,448]{1,0:T(8,128)S(1)}, u32[]{:S(2)}, u32[]{:S(2)}) collective-permute-start(f32[64,448]{1,0:T(8,128)S(1)} %pad_maximum_fusion.1), channel_id=1, source_target_pairs={{0,1},{1,0},{2,3},{3,2},{4,5},{5,4},{6,7},{7,6},{8,9},{9,8},{10,11... | collective-permute-start | bytes 344072 | tf_op jit(solution)/shard_map/ppermute | solution.py:21
  142.4 3.6 %collective-permute-done.33 = f32[448,128]{1,0:T(8,128)S(1)} collective-permute-done((f32[448,128]{1,0:T(8,128)S(1)}, f32[448,128]{1,0:T(8,128)S(1)}, u32[]{:S(2)}, u32[]{:S(2)}) %collective-permute-start.33) | collective-permute-done | bytes 229408 | tf_op jit(solution)/shard_map/ppermute | solution.py:17
  146.1 4.9 %collective-permute-done.34 = f32[448,128]{1,0:T(8,128)S(1)} collective-permute-done((f32[448,128]{1,0:T(8,128)S(1)}, f32[448,128]{1,0:T(8,128)S(1)}, u32[]{:S(2)}, u32[]{:S(2)}) %collective-permute-start.34) | collective-permute-done | bytes 229408 | tf_op jit(solution)/shard_map/ppermute | solution.py:17
  152.7 3.4 %collective-permute-start.37 = (f32[4,16,128]{2,1,0:T(8,128)S(1)}, f32[4,16,128]{2,1,0:T(8,128)S(1)}, u32[]{:S(2)}, u32[]{:S(2)}) collective-permute-start(f32[4,16,128]{2,1,0:T(8,128)S(1)} %get-tuple-element.50), channel_id=1, source_target_pairs={{0,24},{8,0},{16,8},{24,16},{1,25},{9,1},{17,9},{25,17},{2,26},{10... | collective-permute-start | bytes 98312 | tf_op jit(solution)/shard_map/ppermute | solution.py:17
  157.1 3.4 %collective-permute-done.38 = f32[4,16,128]{2,1,0:T(8,128)S(1)} collective-permute-done((f32[4,16,128]{2,1,0:T(8,128)S(1)}, f32[4,16,128]{2,1,0:T(8,128)S(1)}, u32[]{:S(2)}, u32[]{:S(2)}) %collective-permute-start.38) | collective-permute-done | bytes 32800 | tf_op jit(solution)/shard_map/ppermute | solution.py:17
  (140 shorter events, 55.4 us)
Async XLA Ops:
  2.1 14.0 %collective-permute-start.11 = (f32[16,320]{1,0:T(8,128)S(1)}, f32[16,320]{1,0:T(8,128)S(1)}, u32[]{:S(2)}, u32[]{:S(2)}) collective-permute-start(f32[16,320]{1,0:T(8,128)S(1)} %pad_maximum_fusion.2), channel_id=1, source_target_pairs={{0,2},{2,0},{4,6},{6,4},{1,3},{3,1},{5,7},{7,5},{8,10},{10,8},{12,... | collective-permute-start | bytes 61448 | tf_op jit(solution)/shard_map/ppermute | solution.py:21
  7.8 22.8 %collective-permute-start = (f32[16,2368]{1,0:T(8,128)S(1)}, f32[16,2368]{1,0:T(8,128)S(1)}, u32[]{:S(2)}, u32[]{:S(2)}) collective-permute-start(f32[16,2368]{1,0:T(8,128)S(1)} %concatenate.37), channel_id=1, source_target_pairs={{0,8},{8,16},{16,24},{24,0},{1,9},{9,17},{17,25},{25,1},{2,10},{10... | collective-permute-start | bytes 454664 | tf_op jit(solution)/shard_map/ppermute | solution.py:17
  9.1 21.5 %collective-permute-start.1 = (f32[16,2368]{1,0:T(8,128)S(1)}, f32[16,2368]{1,0:T(8,128)S(1)}, u32[]{:S(2)}, u32[]{:S(2)}) collective-permute-start(f32[16,2368]{1,0:T(8,128)S(1)} %concatenate.38), channel_id=1, source_target_pairs={{0,16},{8,24},{16,0},{24,8},{1,17},{9,25},{17,1},{25,9},{2,18},{10... | collective-permute-start | bytes 454664 | tf_op jit(solution)/shard_map/ppermute | solution.py:17
  11.7 19.0 %collective-permute-start.2 = (f32[16,2368]{1,0:T(8,128)S(1)}, f32[16,2368]{1,0:T(8,128)S(1)}, u32[]{:S(2)}, u32[]{:S(2)}) collective-permute-start(f32[16,2368]{1,0:T(8,128)S(1)} %concatenate.39), channel_id=1, source_target_pairs={{0,24},{8,0},{16,8},{24,16},{1,25},{9,1},{17,9},{25,17},{2,26},{10... | collective-permute-start | bytes 454664 | tf_op jit(solution)/shard_map/ppermute | solution.py:17
  30.7 20.4 %collective-permute-start.7 = (f32[64,2368]{1,0:T(8,128)S(1)}, f32[64,2368]{1,0:T(8,128)S(1)}, u32[]{:S(2)}, u32[]{:S(2)}) collective-permute-start(f32[64,2368]{1,0:T(8,128)S(1)} %pad_maximum_fusion.refs_0_), channel_id=1, source_target_pairs={{0,224},{32,0},{64,32},{96,64},{128,96},{160,128},{192,160},{224,1... | collective-permute-start | bytes 1818632 | tf_op jit(solution)/shard_map/ppermute | solution.py:17
  31.0 22.2 %collective-permute-start.3 = (f32[64,2368]{1,0:T(8,128)S(1)}, f32[64,2368]{1,0:T(8,128)S(1)}, u32[]{:S(2)}, u32[]{:S(2)}) collective-permute-start(f32[64,2368]{1,0:T(8,128)S(1)} %pad_maximum_fusion.refs_0_), channel_id=1, source_target_pairs={{0,32},{32,64},{64,96},{96,128},{128,160},{160,192},{192,224},{224... | collective-permute-start | bytes 1818632 | tf_op jit(solution)/shard_map/ppermute | solution.py:17
  32.5 13.5 %collective-permute-start.15 = (f32[16,1536]{1,0:T(8,128)S(1)}, f32[16,1536]{1,0:T(8,128)S(1)}, u32[]{:S(2)}, u32[]{:S(2)}) collective-permute-start(f32[16,1536]{1,0:T(8,128)S(1)} %collective-permute-done.14), channel_id=1, source_target_pairs={{0,32},{32,64},{64,96},{96,128},{128,160},{160,192},{192,224},{224... | collective-permute-start | bytes 294920 | tf_op jit(solution)/shard_map/ppermute | solution.py:17
  32.5 14.0 %collective-permute-start.19 = (f32[16,1536]{1,0:T(8,128)S(1)}, f32[16,1536]{1,0:T(8,128)S(1)}, u32[]{:S(2)}, u32[]{:S(2)}) collective-permute-start(f32[16,1536]{1,0:T(8,128)S(1)} %collective-permute-done.18), channel_id=1, source_target_pairs={{0,224},{32,0},{64,32},{96,64},{128,96},{160,128},{192,160},{224,1... | collective-permute-start | bytes 294920 | tf_op jit(solution)/shard_map/ppermute | solution.py:17
  53.2 10.8 %collective-permute-start.4 = (f32[64,2368]{1,0:T(8,128)S(1)}, f32[64,2368]{1,0:T(8,128)S(1)}, u32[]{:S(2)}, u32[]{:S(2)}) collective-permute-start(f32[64,2368]{1,0:T(8,128)S(1)} %collective-permute-done.3.refs_1_), channel_id=1, source_target_pairs={{0,32},{32,64},{64,96},{96,128},{128,160},{160,192},{192,224},{224... | collective-permute-start | bytes 1818632 | tf_op jit(solution)/shard_map/ppermute | solution.py:17
  53.2 12.1 %collective-permute-start.21 = (f32[8,16,1536]{2,1,0:T(8,128)S(1)}, f32[8,16,1536]{2,1,0:T(8,128)S(1)}, u32[]{:S(2)}, u32[]{:S(2)}) collective-permute-start(f32[8,16,1536]{2,1,0:T(8,128)S(1)} %bitcast_dynamic-update-slice_fusion.8.refs_9_), channel_id=1, source_target_pairs={{0,8},{8,16},{16,24},{24,0},{1,9},{9,17},{17,25},{25,1},{2,10},{10... | collective-permute-start | bytes 2359304 | tf_op jit(solution)/shard_map/ppermute | solution.py:17
  53.6 11.9 %collective-permute-start.23 = (f32[8,16,1536]{2,1,0:T(8,128)S(1)}, f32[8,16,1536]{2,1,0:T(8,128)S(1)}, u32[]{:S(2)}, u32[]{:S(2)}) collective-permute-start(f32[8,16,1536]{2,1,0:T(8,128)S(1)} %bitcast_dynamic-update-slice_fusion.8.refs_9_), channel_id=1, source_target_pairs={{0,24},{8,0},{16,8},{24,16},{1,25},{9,1},{17,9},{25,17},{2,26},{10... | collective-permute-start | bytes 2359304 | tf_op jit(solution)/shard_map/ppermute | solution.py:17
  61.0 14.9 %collective-permute-start.9 = (f32[64,2368]{1,0:T(8,128)S(1)}, f32[64,2368]{1,0:T(8,128)S(1)}, u32[]{:S(2)}, u32[]{:S(2)}) collective-permute-start(f32[64,2368]{1,0:T(8,128)S(1)} %collective-permute-done.8.refs_7_), channel_id=1, source_target_pairs={{0,224},{32,0},{64,32},{96,64},{128,96},{160,128},{192,160},{224,1... | collective-permute-start | bytes 1818632 | tf_op jit(solution)/shard_map/ppermute | solution.py:17
  64.1 15.4 %collective-permute-start.5 = (f32[64,2368]{1,0:T(8,128)S(1)}, f32[64,2368]{1,0:T(8,128)S(1)}, u32[]{:S(2)}, u32[]{:S(2)}) collective-permute-start(f32[64,2368]{1,0:T(8,128)S(1)} %collective-permute-done.4.refs_2_), channel_id=1, source_target_pairs={{0,32},{32,64},{64,96},{96,128},{128,160},{160,192},{192,224},{224... | collective-permute-start | bytes 1818632 | tf_op jit(solution)/shard_map/ppermute | solution.py:17
  65.4 14.2 %collective-permute-start.22 = (f32[4,16,1536]{2,1,0:T(8,128)S(1)}, f32[4,16,1536]{2,1,0:T(8,128)S(1)}, u32[]{:S(2)}, u32[]{:S(2)}) collective-permute-start(f32[4,16,1536]{2,1,0:T(8,128)S(1)} %slice.113), channel_id=1, source_target_pairs={{0,8},{8,16},{16,24},{24,0},{1,9},{9,17},{17,25},{25,1},{2,10},{10... | collective-permute-start | bytes 1179656 | tf_op jit(solution)/shard_map/ppermute | solution.py:17
  65.5 14.0 %collective-permute-start.24 = (f32[4,16,1536]{2,1,0:T(8,128)S(1)}, f32[4,16,1536]{2,1,0:T(8,128)S(1)}, u32[]{:S(2)}, u32[]{:S(2)}) collective-permute-start(f32[4,16,1536]{2,1,0:T(8,128)S(1)} %slice.114), channel_id=1, source_target_pairs={{0,24},{8,0},{16,8},{24,16},{1,25},{9,1},{17,9},{25,17},{2,26},{10... | collective-permute-start | bytes 1179656 | tf_op jit(solution)/shard_map/ppermute | solution.py:17
  75.9 10.7 %collective-permute-start.10 = (f32[32,2368]{1,0:T(8,128)S(1)}, f32[32,2368]{1,0:T(8,128)S(1)}, u32[]{:S(2)}, u32[]{:S(2)}) collective-permute-start(f32[32,2368]{1,0:T(8,128)S(1)} %slice.101), channel_id=1, source_target_pairs={{0,224},{32,0},{64,32},{96,64},{128,96},{160,128},{192,160},{224,1... | collective-permute-start | bytes 909320 | tf_op jit(solution)/shard_map/ppermute | solution.py:17
  79.5 10.6 %collective-permute-start.6 = (f32[32,2368]{1,0:T(8,128)S(1)}, f32[32,2368]{1,0:T(8,128)S(1)}, u32[]{:S(2)}, u32[]{:S(2)}) collective-permute-start(f32[32,2368]{1,0:T(8,128)S(1)} %slice.100), channel_id=1, source_target_pairs={{0,32},{32,64},{64,96},{96,128},{128,160},{160,192},{192,224},{224... | collective-permute-start | bytes 909320 | tf_op jit(solution)/shard_map/ppermute | solution.py:17
  90.3 21.6 %collective-permute-start.28 = (f32[512,1536]{1,0:T(8,128)S(1)}, f32[512,1536]{1,0:T(8,128)}, u32[]{:S(2)}, u32[]{:S(2)}) collective-permute-start(f32[512,1536]{1,0:T(8,128)S(1)} %mine.1), channel_id=1, source_target_pairs={{0,1},{1,0},{2,3},{3,2},{4,5},{5,4},{6,7},{7,6},{8,9},{9,8},{10,11... | collective-permute-start | bytes 9437192 | tf_op jit(solution)/shard_map/ppermute | solution.py:21
  109.2 14.5 %collective-permute-start.25 = (f32[512,128]{1,0:T(8,128)}, f32[512,128]{1,0:T(8,128)}, u32[]{:S(2)}, u32[]{:S(2)}) collective-permute-start(f32[512,128]{1,0:T(8,128)} %get-tuple-element.17), channel_id=1, source_target_pairs={{0,8},{8,16},{16,24},{24,0},{1,9},{9,17},{17,25},{25,1},{2,10},{10... | collective-permute-start | bytes 786440 | tf_op jit(solution)/shard_map/ppermute | solution.py:17
  109.5 18.9 %collective-permute-start.26 = (f32[512,128]{1,0:T(8,128)}, f32[512,128]{1,0:T(8,128)S(1)}, u32[]{:S(2)}, u32[]{:S(2)}) collective-permute-start(f32[512,128]{1,0:T(8,128)} %get-tuple-element.17), channel_id=1, source_target_pairs={{0,16},{8,24},{16,0},{24,8},{1,17},{9,25},{17,1},{25,9},{2,18},{10... | collective-permute-start | bytes 786440 | tf_op jit(solution)/shard_map/ppermute | solution.py:17
  110.0 26.6 %collective-permute-start.27 = (f32[512,128]{1,0:T(8,128)}, f32[512,128]{1,0:T(8,128)S(1)}, u32[]{:S(2)}, u32[]{:S(2)}) collective-permute-start(f32[512,128]{1,0:T(8,128)} %get-tuple-element.17), channel_id=1, source_target_pairs={{0,24},{8,0},{16,8},{24,16},{1,25},{9,1},{17,9},{25,17},{2,26},{10... | collective-permute-start | bytes 786440 | tf_op jit(solution)/shard_map/ppermute | solution.py:17
  136.7 14.6 %collective-permute-start.36 = (f32[64,1536]{1,0:T(8,128)S(1)}, f32[64,1536]{1,0:T(8,128)S(1)}, u32[]{:S(2)}, u32[]{:S(2)}) collective-permute-start(f32[64,1536]{1,0:T(8,128)S(1)} %get-tuple-element.29.low), channel_id=1, source_target_pairs={{0,1},{1,0},{2,3},{3,2},{4,5},{5,4},{6,7},{7,6},{8,9},{9,8},{10,11... | collective-permute-start | bytes 1179656 | tf_op jit(solution)/shard_map/ppermute | solution.py:21
  138.5 12.4 %collective-permute-start.34 = (f32[448,128]{1,0:T(8,128)S(1)}, f32[448,128]{1,0:T(8,128)S(1)}, u32[]{:S(2)}, u32[]{:S(2)}) collective-permute-start(f32[448,128]{1,0:T(8,128)S(1)} %rows.1), channel_id=1, source_target_pairs={{0,16},{8,24},{16,0},{24,8},{1,17},{9,25},{17,1},{25,9},{2,18},{10... | collective-permute-start | bytes 688136 | tf_op jit(solution)/shard_map/ppermute | solution.py:17
  140.4 10.8 %collective-permute-start.35 = (f32[448,128]{1,0:T(8,128)S(1)}, f32[448,128]{1,0:T(8,128)S(1)}, u32[]{:S(2)}, u32[]{:S(2)}) collective-permute-start(f32[448,128]{1,0:T(8,128)S(1)} %rows.1), channel_id=1, source_target_pairs={{0,24},{8,0},{16,8},{24,16},{1,25},{9,1},{17,9},{25,17},{2,26},{10... | collective-permute-start | bytes 688136 | tf_op jit(solution)/shard_map/ppermute | solution.py:17
  (28 other events, 145.5 us)
where the time goes:
time: 163 us; the launch traced here: 162 us
  starting transfers between devices  68 us (42%)
  waiting for transfers between devices  62 us (38%)
  local copies, waits for them, and re-layouts  17.3 us (11%)
  Pallas kernels  13 us (8%)
    ppermute x32, waiting for transfers between devices, shift(): lax.ppermute(value, axis, [(i, (i + by) % size) for i in range(size)])  57.2 us
    ppermute x32, starting transfers between devices, shift(): lax.ppermute(value, axis, [(i, (i + by) % size) for i in range(size)])  46.2 us
    ppermute x8, starting transfers between devices, swap(): lax.ppermute(value, axis, [(i, i ^ mask) for i in range(SIZES[axis])])  21.7 us
    pallas_call x7, Pallas kernels, call(): pl.pallas_call(kernel, name=name, out_shape=[jax.ShapeDtypeStruct(shape,...  13 us
    slice x10, local copies, waits for them, and re-layouts, cut(): return lax.slice_in_dim(array, start, start + width, axis=1)  6.31 us
    unnamed x30, local copies, waits for them, and re-layouts  6.28 us
    ppermute x8, waiting for transfers between devices, swap(): lax.ppermute(value, axis, [(i, i ^ mask) for i in range(SIZES[axis])])  4.8 us
  transfers between devices with their start and end apart: 40, of which 19 were waited for; matrix products, arithmetic and copies ran while one was open for 6% of the time, Pallas kernels for 7%

commit v1 on v0

v1 whole, which is shorter than its diff:
```python
import functools

import jax
import jax.numpy as jnp
import numpy as np
from jax import lax
from jax.experimental import pallas as pl
from jax.experimental.pallas import tpu as pltpu
from jax.sharding import Mesh, PartitionSpec as P

SIZES = {"z": 8, "x": 4, "y": 4, "core": 2}
F32, BF16 = jnp.float32, jnp.bfloat16


def shift(value, axis, by):
    size = SIZES[axis]
    return lax.ppermute(value, axis, [(i, (i + by) % size) for i in range(size)])


def swap(value, axis, mask):
    return lax.ppermute(value, axis, [(i, i ^ mask) for i in range(SIZES[axis])])


def ring_z(block, *held):
    half = block.shape[0] // 2
    parts = [block] + [None] * 7
    up = down = block
    for step in range(1, 4):
        if held and step == 3:
            up, down = lax.optimization_barrier((up, down) + held)[:2]
        up, down = shift(up, "z", 1), shift(down, "z", -1)
        parts[step], parts[8 - step] = up, down
    parts[4] = (shift(up[:half], "z", 1), shift(down[half:], "z", -1))
    return parts


def ring_x(block):
    half = block.shape[0] // 2
    up, down = shift(block, "x", 1), shift(block, "x", -1)
    return [block, up, (shift(up[:half], "x", 1), shift(down[half:], "x", -1)), down]


def cut(array, start, width):
    return lax.slice_in_dim(array, start, start + width, axis=1)


def parts_of(value):
    high = value.astype(BF16)
    return high, (value - high.astype(F32)).astype(BF16)


def times(value, high, low, dims):
    count = value.shape[0]
    vh, vl = parts_of(value)
    dot = functools.partial(lax.dot_general, dimension_numbers=((dims, ((), ()))), preferred_element_type=F32)
    main = dot(jnp.concatenate([vh, vl], axis=0), high)
    return main[:count] + (main[count:] + dot(vh, low))


def mm(value, matrix):
    return times(value, *matrix, ((1,), (0,)))


def mmt(value, matrix):
    return times(value, *matrix, ((1,), (1,)))


def whole(ref, columns):
    return ref[0, :, columns], ref[1, :, columns]


def rows_of_a(refs):
    order = [(0, 64), (64, 64), (128, 64), (192, 64), (256, 32), (288, 32), (320, 64), (384, 64), (448, 64)]
    return [(start, size, ref) for (start, size), ref in zip(order, refs)]


def rows_of_b(refs):
    found = []
    for k, first, count, ref in ((0, 0, 8, refs[0]), (1, 0, 8, refs[1]), (2, 0, 4, refs[2]), (2, 4, 4, refs[3]),
                                 (3, 0, 8, refs[4])):
        found += [((first + s) * 64 + k * 16, s, ref) for s in range(count)]
    return found


def put_parts(mat, rows, columns, value):
    high, low = parts_of(value)
    mat[0, rows, columns] = high
    mat[1, rows, columns] = low


def pack_kernel(place, right, off, diag, b_out, *a_outs):
    b_out[:, 1280:1408] = off[:, 0:128]
    b_out[:, 1408:1536] = diag[:, 64:192]
    b_out[:, 1536:1600] = diag[:, 0:64]
    b_out[:, 0:768] = diag[:, 192:960]
    b_out[:, 768:1280] = off[:, 128:640]
    x, core = place[1], place[3]
    column = 2 * place[2] + core
    for k in range(4):
        out = a_outs[k]
        at = pl.ds(pl.multiple_of(lax.rem(x + k, 4) * 128, 128), 128)
        out[:, 0:1536] = off[:, 640:2176]
        out[:, 1536:1664] = right[7 + column, :, at]
        for m in (2, 1, 0):
            both = right[2**m - 1 + lax.shift_right_logical(column, 3 - m), :, at]
            to = 1664 + 64 * (2 - m)
            out[:, to:to + 64] = jnp.where(core == 0, both[:, 0:64], both[:, 64:128])


def column_blocks_kernel(*refs):
    main, low = refs[9], refs[10]
    for at, first, size in zip((0, 1, 2, 3, 4, 4, 5, 6, 7), (0, 0, 0, 0, 0, 8, 0, 0, 0), (16, 16, 16, 16, 8, 8, 16, 16, 16)):
        ref = refs[at + (first > 0) if at <= 4 else at + 1]
        main[at, first:first + size, :] = ref[:, 0:1280]
        low[at, first:first + size, :] = ref[:, 1280:1600]


def low_rows_kernel(b0, b1, b2, b3, out):
    for k, ref in enumerate((b0, b1, b2, b3)):
        for s in range(8):
            at = s * 64 + k * 16
            out[at:at + 16, :] = ref[s, :, 0:128]
            out[512 + at:528 + at, :] = ref[s, :, 128:256]
            out[1024 + at % 256:1040 + at % 256, at // 256 * 64:at // 256 * 64 + 64] = ref[s, :, 256:320]


def pair_kernel(own, other, out):
    for i, ref in enumerate((own, other)):
        out[0:256, 64 * i:64 * i + 64] = ref[1024:1280, 0:64]
        out[256:512, 64 * i:64 * i + 64] = ref[1024:1280, 64:128]


def low_mine_kernel(own, other, pair, far, out):
    out[:, 0:128] = own[0:512]
    out[:, 128:256] = other[0:512]
    out[:, 256:384] = own[512:1024]
    out[:, 384:512] = other[512:1024]
    out[:, 512:640] = pair[...]
    out[:, 640:768] = far[...]


def mine_kernel(*refs):
    out = refs[5]
    for start, s, ref in rows_of_b(refs[:5]):
        out[start:start + 16, 0:256] = ref[s, :, 0:256]
        out[start:start + 16, 256:768] = ref[s, :, 768:1280]


def level3_kernel(place, *refs):
    a_refs, b_refs = rows_of_a(refs[:9]), rows_of_b(refs[9:14])
    mat, keep, y3_out, kept_out, given_out, b2t_out, rhs, up = refs[14:]
    for start, size, ref in a_refs:
        rhs[start:start + size, 0:320] = ref[:, 1536:1856]
        put_parts(mat, slice(start, start + size), slice(0, 1536), ref[:, 0:1536])
    for start, s, ref in b_refs:
        put_parts(mat, slice(start, start + 16), slice(1536, 2048), ref[s, :, 256:768])
    rhs[:, 320:384] = jnp.zeros((512, 64), F32)
    b3t = rhs[:, 0:128].T
    b21t = rhs[:, 128:256].T
    b2t_out[...] = b21t[0:64]
    keep[128:192] = b21t[64:128]
    keep[192:256] = rhs[:, 256:384].T[0:64]
    y3t = mm(b3t, whole(mat, slice(1536, 2048)))
    keep[0:128] = y3t
    y3_out[...] = y3t.T
    for at, column in ((0, 1024), (512, 512), (1024, 0)):
        up[:, at:at + 512] = mmt(y3t, whole(mat, slice(column, column + 512)))
    core = place[3]
    kept_out[...] = up[pl.ds(pl.multiple_of(64 * core, 64), 64), :]
    given_out[...] = up[pl.ds(pl.multiple_of(64 * (1 - core), 64), 64), :]


def level2_kernel(mine, theirs, kept, got, b2t, mat, y2t_out, up_out):

    @pl.loop(0, 8)
    def _(s):
        at = pl.ds(pl.multiple_of(64 * s, 64), 64)
        for i in range(3):
            for j, ref in ((0, mine), (256, theirs)):
                put_parts(mat, at, slice(512 * i + j, 512 * i + j + 256), ref[at, 256 * i:256 * i + 256])

    up3 = kept[...] + got[...]
    y2t = mm(b2t[...] - up3[:, 0:512], whole(mat, slice(0, 512)))
    y2t_out[...] = y2t
    up_out[:, 0:512] = up3[:, 512:1024] + mmt(y2t, whole(mat, slice(1024, 1536)))
    up_out[:, 512:1024] = up3[:, 1024:1536] + mmt(y2t, whole(mat, slice(512, 1024)))


def low_matrices_kernel(mine, theirs, mat):
    @pl.loop(0, 8)
    def _(s):
        at = pl.ds(pl.multiple_of(64 * s, 64), 64)
        for i in range(3):
            for j, ref in ((0, mine), (256, theirs)):
                put_parts(mat, at, slice(512 * i + j, 512 * i + j + 256), ref[at, 256 * i:256 * i + 256])


def level1_kernel(up_ref, got, y2t, mat, keep, y1t_out, up_out, give_out):
    y1t = mm(keep[128:192] - (up_ref[:, 0:512] + got[:, 0:512]), whole(mat, slice(512, 1024)))
    y1t_out[...] = y1t
    up_out[...] = (up_ref[:, 512:1024] + got[:, 512:1024]) + mmt(y1t, whole(mat, slice(0, 512)))
    give_out[:, 0:128] = y1t[:, 256:384]
    give_out[:, 128:384] = y2t[:, 256:512]


def level0_kernel(up_ref, got, y2t, y1t, mat2, mat, keep, y0t_out, low_out):
    d2, l02, l12 = (whole(mat2, slice(512 * i, 512 * i + 512)) for i in range(3))
    l01, d1, d0 = (whole(mat, slice(512 * i, 512 * i + 512)) for i in range(3))
    y0t = mm(keep[192:256] - (up_ref[...] + got[...]), d0)
    y0t_out[...] = y0t
    low_out[:, 1536:1600] = y0t[:, 256:320]
    x0t = mmt(y0t, d0)
    low_out[:, 0:512] = x0t
    x1t = mmt(y1t[...] - mm(x0t, l01), d1)
    low_out[:, 512:1024] = x1t
    low_out[:, 1024:1536] = mmt(y2t[...] - mm(x0t, l02) - mm(x1t, l12), d2)


def halves(place):
    core = place[3]
    return pl.ds(pl.multiple_of(64 * core, 64), 64), pl.ds(pl.multiple_of(64 * (1 - core), 64), 64)


def rows_kernel(place, y1t, y2t, got, out, both):
    here, there = halves(place)
    both[here, 0:128] = y1t[:, 0:128]
    both[here, 128:384] = y2t[:, 0:256]
    both[there, :] = got[...]
    out[...] = both[...].T


def last_kernel(place, low, got, y0t, keep, mat, *refs):
    outs, both, tops = refs[:4], refs[4], refs[5]
    here, there = halves(place)
    both[here, :] = low[:, 0:1536]
    both[there, :] = got[:, 0:1536]
    tops[here, 0:64] = y0t[:, 0:64]
    tops[there, 0:64] = got[:, 1536:1600]
    rest = keep[0:128]
    for k in range(3):
        rest = rest - mm(both[:, 512 * k:512 * k + 512], whole(mat, slice(512 * k, 512 * k + 512)))
        tops[:, 64 * k + 64:64 * k + 128] = both[:, 512 * k:512 * k + 64]
    tops[:, 256:320] = mmt(rest, (mat[0, 0:64, 1536:2048], mat[1, 0:64, 1536:2048]))
    tops[:, 320:384] = jnp.zeros((128, 64), F32)
    rows = tops[...].T
    for k in range(4):
        outs[k][0:64, :] = rows[0:64]
        for n in range(4):
            at = 64 + 64 * n + 16 * ((4 - k) % 4)
            outs[k][64 + 16 * n:80 + 16 * n, :] = rows[at:at + 16]


def forward_kernel(place, *refs):
    out = refs[8]
    for k in range(4):
        at = pl.ds(pl.multiple_of(lax.rem(place[1] + 4 - k, 4) * 128, 128), 128)
        out[0:64, at] = jnp.zeros((64, 128), F32)
        out[64:448, at] = refs[k][...]
        out[448:960, at] = refs[4 + k][...]


def final_kernel(place, m0, m1, m2, m3, forward_in, forward_out, x_out, top, sem):
    del forward_in
    for k, ref in enumerate((m0, m1, m2, m3)):
        at = pl.ds(pl.multiple_of(lax.rem(place[1] + 4 - k, 4) * 128, 128), 128)
        top[:, at] = ref[0:64, :]
        for n in range(4):
            x_out[n, :, at] = ref[64 + 16 * n:80 + 16 * n, :]
    copy = pltpu.make_async_copy(top, forward_out.at[0:64], sem)
    copy.start()
    copy.wait()


VMEM, SMEM, ANY = (pl.BlockSpec(memory_space=m) for m in (pltpu.VMEM, pltpu.SMEM, pl.ANY))


def call(kernel, name, outs, *args, scalars=1, scratch=(), in_specs=None, out_specs=None, aliases=None, limit=6):
    return pl.pallas_call(
        kernel,
        name=name,
        out_shape=[jax.ShapeDtypeStruct(shape, kind) for shape, kind in outs],
        in_specs=in_specs or [SMEM] * scalars + [VMEM] * (len(args) - scalars),
        out_specs=out_specs or [VMEM] * len(outs),
        scratch_shapes=list(scratch),
        input_output_aliases=aliases or {},
        compiler_params=pltpu.CompilerParams(vmem_limit_bytes=limit * 2**20),
    )(*args)


def after(value, *others):
    return lax.optimization_barrier((value,) + others)[0]


def per_device(right_side, off_blocks, diag_inverse):
    place = jnp.stack([lax.axis_index(a) for a in ("z", "x", "y", "core")]).astype(jnp.int32)

    stream_b, *stream_a = call(
        pack_kernel, "pack", [((16, 1600), F32)] + [((16, 1856), F32)] * 4,
        place, right_side, off_blocks[0], diag_inverse[0], limit=8)

    rows_a = [stream_a[0]] + [shift(stream_a[k], "x", k) for k in (1, 2, 3)]
    block_a = jnp.concatenate(rows_a, axis=0)
    blocks_a = ring_z(block_a)
    blocks_a = blocks_a[:4] + list(blocks_a[4]) + blocks_a[5:]

    rows_b = ring_z(stream_b, block_a)
    rows_b = rows_b[:4] + list(rows_b[4]) + rows_b[5:]
    rows_b[0] = after(rows_b[0], blocks_a[1], blocks_a[8])
    main, low_block = call(column_blocks_kernel, "column_blocks", [((8, 16, 1280), F32), ((8, 16, 320), F32)],
                           *rows_b, scalars=0)
    low_blocks = [shift(low_block, "x", k) for k in (1, 2, 3)]
    low_block = after(low_block, blocks_a[2], blocks_a[7])
    (own,) = call(low_rows_kernel, "low_rows", [((1280, 128), F32)], low_block, *low_blocks, scalars=0)
    other = after(swap(own, "y", 1), blocks_a[3], blocks_a[6])
    (pair,) = call(pair_kernel, "pair", [((512, 128), F32)], own, other, scalars=0)
    (low_mine,) = call(low_mine_kernel, "low_mine", [((512, 768), F32)], own, other, pair,
                       after(swap(pair, "y", 2), blocks_a[4], blocks_a[5]), scalars=0)
    low_theirs = swap(low_mine, "core", 1)
    blocks_b = ring_x(main)
    blocks_b = blocks_b[:2] + list(blocks_b[2]) + blocks_b[3:]

    (mine,) = call(mine_kernel, "mine", [((512, 768), F32)], *blocks_b, scalars=0, limit=6)
    theirs = swap(mine, "core", 1)

    mat3, keep, y3, kept, given, b2t = call(
        level3_kernel, "level3",
        [((2, 512, 2048), BF16), ((256, 512), F32), ((512, 128), F32), ((64, 1536), F32), ((64, 1536), F32),
         ((64, 512), F32)],
        place, *blocks_a, *blocks_b,
        scratch=[pltpu.VMEM((512, 384), F32), pltpu.VMEM((128, 1536), F32)])
    got = swap(given, "core", 1)
    mat2, y2t, up = call(
        level2_kernel, "level2", [((2, 512, 1536), BF16), ((64, 512), F32), ((64, 1024), F32)],
        mine, theirs, kept, got, b2t, scalars=0)
    got = swap(up, "y", 1)
    y3 = after(y3, up)
    top_parts = [y3] + [shift(y3, "x", k) for k in (1, 2, 3)]
    (mat1,) = call(low_matrices_kernel, "low_matrices", [((2, 512, 1536), BF16)], low_mine, low_theirs, scalars=0)
    y1t, up, give = call(
        level1_kernel, "level1", [((64, 512), F32), ((64, 512), F32), ((64, 384), F32)],
        up, got, y2t, mat1, keep, scalars=0)
    got = swap(up, "y", 2)
    (rows,) = call(rows_kernel, "rows", [((384, 128), F32)], place, y1t, y2t, swap(give, "core", 1),
                   scratch=[pltpu.VMEM((128, 384), F32)], limit=4)
    got = after(got, rows, *top_parts)
    mid_parts = [rows] + [shift(rows, "x", k) for k in (1, 2, 3)]
    y0t, low = call(level0_kernel, "level0", [((64, 512), F32), ((64, 1600), F32)],
                    up, got, y2t, y1t, mat2, mat1, keep, scalars=0)

    messages = call(last_kernel, "last", [((128, 128), F32)] * 4, place, low, swap(low, "core", 1), y0t, keep, mat3,
                    scratch=[pltpu.VMEM((128, 1536), F32), pltpu.VMEM((128, 384), F32)])
    held = lax.optimization_barrier(tuple(mid_parts + top_parts) + (messages[0],))[:8]
    (forward,) = call(forward_kernel, "forward", [((960, 512), F32)], place, *held, limit=8)
    arrived = [messages[0]] + [shift(after(messages[k], *mid_parts), "x", k) for k in (1, 2, 3)]
    forward, backward = call(
        final_kernel, "final", [((960, 512), F32), ((4, 16, 512), F32)], place, *arrived, forward,
        in_specs=[SMEM] + [VMEM] * 4 + [ANY], out_specs=[ANY, VMEM], aliases={5: 0},
        scratch=[pltpu.VMEM((64, 512), F32), pltpu.SemaphoreType.DMA], limit=4)
    return forward[None], backward[None]


def solution(mesh):
    split = Mesh(np.asarray(mesh.devices).reshape(8, 4, 4, 2), ("z", "x", "y", "core"))
    row, col = ("z", "x"), ("y", "core")
    return jax.shard_map(
        per_device,
        mesh=split,
        in_specs=(P(None, row, None), P(col, row, None), P(col, row, None)),
        out_specs=(P(col, None, None), P(col, None, row, None)),
        check_vma=False,
    )
```

time: 163 us -> 158 us (0.969)
  local copies, waits for them, and re-layouts: 17.3 us -> 2.91 us
  waiting for transfers between devices: 62 us -> 66.9 us
  starting transfers between devices: 68 us -> 71.6 us
    slice x13 -> x0, local copies, waits for them, and re-layouts: 6.33 us -> none  [the longest x10 6.31 us: cut(): return lax.slice_in_dim(array, start, start + width, axis=1)]
    ppermute x32 -> x35, starting transfers between devices: 46.2 us -> 50.4 us  [shift(): lax.ppermute(value, axis, [(i, (i + by) % size) for i in range(size)])]
    unnamed x30 -> x9, local copies, waits for them, and re-layouts: 6.28 us -> 2.81 us
    ppermute x32 -> x35, waiting for transfers between devices: 57.2 us -> 60.4 us  [shift(): lax.ppermute(value, axis, [(i, (i + by) % size) for i in range(size)])]
    dynamic_update_slice x12 -> x0, local copies, waits for them, and re-layouts: 2.1 us -> none  [the longest x8 2.07 us: per_device(): lax.dynamic_update_slice(forward, part, (first, lax.rem(x + 4 - k, 4) * 1...]
    dynamic_slice x2 -> x0, local copies, waits for them, and re-layouts: 1.85 us -> none  [the longest x1 0.96 us: per_device(): lax.dynamic_slice(chain[m], (0, target + 64 * core), (16, 64))]
    ppermute x8 -> x9, waiting for transfers between devices: 4.8 us -> 6.47 us  [swap(): lax.ppermute(value, axis, [(i, i ^ mask) for i in range(SIZES[axis])])]
    pallas_call x7 -> x15, Pallas kernels: 13 us -> 14.5 us  [call(): pl.pallas_call(kernel, name=name, out_shape=[jax.ShapeDtypeStruct(shape,...]
  transfers between devices with their start and end apart: 40 -> 44, of which waited for: 19 -> 18; matrix products, arithmetic and copies ran while one was open for 6% -> 0% of each run, Pallas kernels for 7% -> 6%
where the time goes in v1:
time: 158 us; the launch traced here: 157 us
  starting transfers between devices  71.6 us (45%)
  waiting for transfers between devices  66.9 us (42%)
  Pallas kernels  14.5 us (9%)
  local copies, waits for them, and re-layouts  2.91 us (2%)
    ppermute x35, waiting for transfers between devices, shift(): lax.ppermute(value, axis, [(i, (i + by) % size) for i in range(size)])  60.4 us
    ppermute x35, starting transfers between devices, shift(): lax.ppermute(value, axis, [(i, (i + by) % size) for i in range(size)])  50.4 us
    ppermute x9, starting transfers between devices, swap(): lax.ppermute(value, axis, [(i, i ^ mask) for i in range(SIZES[axis])])  21.2 us
    pallas_call x15, Pallas kernels, call(): pl.pallas_call(kernel, name=name, out_shape=[jax.ShapeDtypeStruct(shape,...  14.5 us
    ppermute x9, waiting for transfers between devices, swap(): lax.ppermute(value, axis, [(i, i ^ mask) for i in range(SIZES[axis])])  6.47 us
  transfers between devices with their start and end apart: 44, of which 18 were waited for; matrix products, arithmetic and copies ran while one was open for 0% of the time, Pallas kernels for 6%

profile of v1, /device:TPU:1, one launch (start us, length us, event | category | flops | bytes accessed | tf_op | source)
XLA Modules:
  0.0 156.9 jit_solution(13364458352288908231)
XLA Ops:
  6.3 2.5 %collective-permute-start.1 = (f32[16,1856]{1,0:T(8,128)S(1)}, f32[16,1856]{1,0:T(8,128)S(1)}, u32[]{:S(2)}, u32[]{:S(2)}) collective-permute-start(f32[16,1856]{1,0:T(8,128)S(1)} %get-tuple-element.51), channel_id=1, source_target_pairs={{0,16},{8,24},{16,0},{24,8},{1,17},{9,25},{17,1},{25,9},{2,18},{10... | collective-permute-start | bytes 356360 | tf_op jit(solution)/shard_map/ppermute | solution.py:17
  9.9 4.2 %collective-permute-done.1 = f32[16,1856]{1,0:T(8,128)S(1)} collective-permute-done((f32[16,1856]{1,0:T(8,128)S(1)}, f32[16,1856]{1,0:T(8,128)S(1)}, u32[]{:S(2)}, u32[]{:S(2)}) %collective-permute-start.1) | collective-permute-done | bytes 118816 | tf_op jit(solution)/shard_map/ppermute | solution.py:17
  15.9 4.0 %collective-permute-start.4 = (f32[64,1856]{1,0:T(8,128)S(1)}, f32[64,1856]{1,0:T(8,128)S(1)}, u32[]{:S(2)}, u32[]{:S(2)}) collective-permute-start(f32[64,1856]{1,0:T(8,128)S(1)} %constant_dynamic-update-slice_fusion.refs_0_), channel_id=1, source_target_pairs={{0,224},{32,0},{64,32},{96,64},{128,96},{160,128},{192,160},{224,1... | collective-permute-start | bytes 1425416 | tf_op jit(solution)/shard_map/ppermute | solution.py:17
  19.9 2.7 %collective-permute-start.7 = (f32[16,1600]{1,0:T(8,128)S(1)}, f32[16,1600]{1,0:T(8,128)S(1)}, u32[]{:S(2)}, u32[]{:S(2)}) collective-permute-start(f32[16,1600]{1,0:T(8,128)S(1)} %get-tuple-element.53.refs_0_), channel_id=1, source_target_pairs={{0,224},{32,0},{64,32},{96,64},{128,96},{160,128},{192,160},{224,1... | collective-permute-start | bytes 307208 | tf_op jit(solution)/shard_map/ppermute | solution.py:17
  22.6 7.2 %collective-permute-done.3.refs_1_ = f32[64,1856]{1,0:T(8,128)S(1)} collective-permute-done((f32[64,1856]{1,0:T(8,128)S(1)}, f32[64,1856]{1,0:T(8,128)S(1)}, u32[]{:S(2)}, u32[]{:S(2)}) %collective-permute-start.3) | collective-permute-done | bytes 475168 | tf_op jit(solution)/shard_map/ppermute | solution.py:17
  29.8 2.7 %collective-permute-start.21 = (f32[64,1856]{1,0:T(8,128)S(1)}, f32[64,1856]{1,0:T(8,128)S(1)}, u32[]{:S(2)}, u32[]{:S(2)}) collective-permute-start(f32[64,1856]{1,0:T(8,128)S(1)} %collective-permute-done.4.refs_8_), channel_id=1, source_target_pairs={{0,224},{32,0},{64,32},{96,64},{128,96},{160,128},{192,160},{224,1... | collective-permute-start | bytes 1425416 | tf_op jit(solution)/shard_map/ppermute | solution.py:17
  32.5 2.7 %collective-permute-start.8 = (f32[16,1600]{1,0:T(8,128)S(1)}, f32[16,1600]{1,0:T(8,128)S(1)}, u32[]{:S(2)}, u32[]{:S(2)}) collective-permute-start(f32[16,1600]{1,0:T(8,128)S(1)} %collective-permute-done.7.refs_8_), channel_id=1, source_target_pairs={{0,224},{32,0},{64,32},{96,64},{128,96},{160,128},{192,160},{224,1... | collective-permute-start | bytes 307208 | tf_op jit(solution)/shard_map/ppermute | solution.py:17
  35.1 7.8 %collective-permute-done.6.refs_2_ = f32[16,1600]{1,0:T(8,128)S(1)} collective-permute-done((f32[16,1600]{1,0:T(8,128)S(1)}, f32[16,1600]{1,0:T(8,128)S(1)}, u32[]{:S(2)}, u32[]{:S(2)}) %collective-permute-start.6) | collective-permute-done | bytes 102432 | tf_op jit(solution)/shard_map/ppermute | solution.py:17
  43.0 2.7 %collective-permute-start.11 = (f32[16,1600]{1,0:T(8,128)S(1)}, f32[16,1600]{1,0:T(8,128)S(1)}, u32[]{:S(2)}, u32[]{:S(2)}) collective-permute-start(f32[16,1600]{1,0:T(8,128)S(1)} %collective-permute-done.8.refs_7_), channel_id=1, source_target_pairs={{0,224},{32,0},{64,32},{96,64},{128,96},{160,128},{192,160},{224,1... | collective-permute-start | bytes 307208 | tf_op jit(solution)/shard_map/ppermute | solution.py:17
  47.8 2.7 %collective-permute-start.12 = (f32[8,1600]{1,0:T(8,128)S(1)}, f32[8,1600]{1,0:T(8,128)S(1)}, u32[]{:S(2)}, u32[]{:S(2)}) collective-permute-start(f32[8,1600]{1,0:T(8,128)S(1)} %slice.25), channel_id=1, source_target_pairs={{0,224},{32,0},{64,32},{96,64},{128,96},{160,128},{192,160},{224,1... | collective-permute-start | bytes 153608 | tf_op jit(solution)/shard_map/ppermute | solution.py:17
  55.8 2.4 %collective-permute-start.27 = (f32[8,16,320]{2,1,0:T(8,128)S(1)}, f32[8,16,320]{2,1,0:T(8,128)S(1)}, u32[]{:S(2)}, u32[]{:S(2)}) collective-permute-start(f32[8,16,320]{2,1,0:T(8,128)S(1)} %get-tuple-element.63.b0), channel_id=1, source_target_pairs={{0,16},{8,24},{16,0},{24,8},{1,17},{9,25},{17,1},{25,9},{2,18},{10... | collective-permute-start | bytes 491528 | tf_op jit(solution)/shard_map/ppermute | solution.py:17
  58.8 9.9 %collective-permute-done.26.b1 = f32[8,16,320]{2,1,0:T(8,128)S(1)} collective-permute-done((f32[8,16,320]{2,1,0:T(8,128)S(1)}, f32[8,16,320]{2,1,0:T(8,128)S(1)}, u32[]{:S(2)}, u32[]{:S(2)}) %collective-permute-start.26) | collective-permute-done | bytes 163872 | tf_op jit(solution)/shard_map/ppermute | solution.py:17
  68.7 4.9 %collective-permute-done.27.b2 = f32[8,16,320]{2,1,0:T(8,128)S(1)} collective-permute-done((f32[8,16,320]{2,1,0:T(8,128)S(1)}, f32[8,16,320]{2,1,0:T(8,128)S(1)}, u32[]{:S(2)}, u32[]{:S(2)}) %collective-permute-start.27) | collective-permute-done | bytes 163872 | tf_op jit(solution)/shard_map/ppermute | solution.py:17
  75.0 2.7 %collective-permute-start.22 = (f32[64,1856]{1,0:T(8,128)S(1)}, f32[64,1856]{1,0:T(8,128)S(1)}, u32[]{:S(2)}, u32[]{:S(2)}) collective-permute-start(f32[64,1856]{1,0:T(8,128)S(1)} %collective-permute-done.21.refs_7_), channel_id=1, source_target_pairs={{0,224},{32,0},{64,32},{96,64},{128,96},{160,128},{192,160},{224,1... | collective-permute-start | bytes 1425416 | tf_op jit(solution)/shard_map/ppermute | solution.py:17
  77.9 2.7 %collective-permute-start.16 = (f32[4,16,1280]{2,1,0:T(8,128)S(1)}, f32[4,16,1280]{2,1,0:T(8,128)S(1)}, u32[]{:S(2)}, u32[]{:S(2)}) collective-permute-start(f32[4,16,1280]{2,1,0:T(8,128)S(1)} %slice.27), channel_id=1, source_target_pairs={{0,24},{8,0},{16,8},{24,16},{1,25},{9,1},{17,9},{25,17},{2,26},{10... | collective-permute-start | bytes 983048 | tf_op jit(solution)/shard_map/ppermute | solution.py:17
  80.6 3.3 %collective-permute-done.19.refs_3_ = f32[64,1856]{1,0:T(8,128)S(1)} collective-permute-done((f32[64,1856]{1,0:T(8,128)S(1)}, f32[64,1856]{1,0:T(8,128)S(1)}, u32[]{:S(2)}, u32[]{:S(2)}) %collective-permute-start.19) | collective-permute-done | bytes 475168 | tf_op jit(solution)/shard_map/ppermute | solution.py:17
  84.1 2.7 %collective-permute-start.30 = (f32[512,128]{1,0:T(8,128)S(1)}, f32[512,128]{1,0:T(8,128)S(1)}, u32[]{:S(2)}, u32[]{:S(2)}) collective-permute-start(f32[512,128]{1,0:T(8,128)S(1)} %pair.1), channel_id=1, source_target_pairs={{0,4},{2,6},{4,0},{6,2},{1,5},{3,7},{5,1},{7,3},{8,12},{10,14},{12... | collective-permute-start | bytes 786440 | tf_op jit(solution)/shard_map/ppermute | solution.py:21
  86.9 11.2 %collective-permute-start.17 = (f32[512,768]{1,0:T(8,128)S(1)}, f32[512,768]{1,0:T(8,128)S(1)}, u32[]{:S(2)}, u32[]{:S(2)}) collective-permute-start(f32[512,768]{1,0:T(8,128)S(1)} %mine.1), channel_id=1, source_target_pairs={{0,1},{1,0},{2,3},{3,2},{4,5},{5,4},{6,7},{7,6},{8,9},{9,8},{10,11... | collective-permute-start | bytes 4718600 | tf_op jit(solution)/shard_map/ppermute | solution.py:21
  102.6 6.2 %collective-permute-done.20.refs_4_ = f32[32,1856]{1,0:T(8,128)S(1)} collective-permute-done((f32[32,1856]{1,0:T(8,128)S(1)}, f32[32,1856]{1,0:T(8,128)S(1)}, u32[]{:S(2)}, u32[]{:S(2)}) %collective-permute-start.20) | collective-permute-done | bytes 237600 | tf_op jit(solution)/shard_map/ppermute | solution.py:17
  109.6 2.3 %level3.1 = (bf16[2,512,2048]{2,1,0:T(8,128)(2,1)S(1)}, f32[256,512]{1,0:T(8,128)S(1)}, f32[512,128]{1,0:T(8,128)S(1)}, f32[64,1536]{1,0:T(8,128)S(1)}, f32[64,1536]{1,0:T(8,128)S(1)}, /*index=5*/f32[64,512]{1,0:T(8,128)S(1)}) custom-call(s32[4]{0:T(128)S(1)} %pad_add_fusion.place, f32[64,1856]{1,0:T(8,128)S(1)} %constant_dynamic-update-slice_fusion.refs_0_, ...), custom_call_target="tpu_custom_call" | custom-call | tf_op jit(solution)/shard_map/level3/pallas_call | solution.py:278
  119.3 3.8 %collective-permute-done.25.got = f32[64,1024]{1,0:T(8,128)S(1)} collective-permute-done((f32[64,1024]{1,0:T(8,128)S(1)}, f32[64,1024]{1,0:T(8,128)S(1)}, u32[]{:S(2)}, u32[]{:S(2)}) %collective-permute-start.25) | collective-permute-done | bytes 262176 | tf_op jit(solution)/shard_map/ppermute | solution.py:21
  134.5 3.2 %collective-permute-start.39 = (f32[384,128]{1,0:T(8,128)S(1)}, f32[384,128]{1,0:T(8,128)S(1)}, u32[]{:S(2)}, u32[]{:S(2)}) collective-permute-start(f32[384,128]{1,0:T(8,128)S(1)} %rows.1.refs_0_), channel_id=1, source_target_pairs={{0,16},{8,24},{16,0},{24,8},{1,17},{9,25},{17,1},{25,9},{2,18},{10... | collective-permute-start | bytes 589832 | tf_op jit(solution)/shard_map/ppermute | solution.py:17
  141.8 5.1 %collective-permute-done.39.refs_2_ = f32[384,128]{1,0:T(8,128)S(1)} collective-permute-done((f32[384,128]{1,0:T(8,128)S(1)}, f32[384,128]{1,0:T(8,128)S(1)}, u32[]{:S(2)}, u32[]{:S(2)}) %collective-permute-start.39) | collective-permute-done | bytes 196640 | tf_op jit(solution)/shard_map/ppermute | solution.py:17
  146.9 2.5 %collective-permute-start.43 = (f32[128,128]{1,0:T(8,128)S(1)}, f32[128,128]{1,0:T(8,128)S(1)}, u32[]{:S(2)}, u32[]{:S(2)}) collective-permute-start(f32[128,128]{1,0:T(8,128)S(1)} %get-tuple-element.83), channel_id=1, source_target_pairs={{0,24},{8,0},{16,8},{24,16},{1,25},{9,1},{17,9},{25,17},{2,26},{10... | collective-permute-start | bytes 196616 | tf_op jit(solution)/shard_map/ppermute | solution.py:17
  (96 shorter events, 53.9 us)
Async XLA Ops:
  14.1 15.6 %collective-permute-start.3 = (f32[64,1856]{1,0:T(8,128)S(1)}, f32[64,1856]{1,0:T(8,128)S(1)}, u32[]{:S(2)}, u32[]{:S(2)}) collective-permute-start(f32[64,1856]{1,0:T(8,128)S(1)} %constant_dynamic-update-slice_fusion.refs_0_), channel_id=1, source_target_pairs={{0,32},{32,64},{64,96},{96,128},{128,160},{160,192},{192,224},{224... | collective-permute-start | bytes 1425416 | tf_op jit(solution)/shard_map/ppermute | solution.py:17
  15.9 13.9 %collective-permute-start.4 = (f32[64,1856]{1,0:T(8,128)S(1)}, f32[64,1856]{1,0:T(8,128)S(1)}, u32[]{:S(2)}, u32[]{:S(2)}) collective-permute-start(f32[64,1856]{1,0:T(8,128)S(1)} %constant_dynamic-update-slice_fusion.refs_0_), channel_id=1, source_target_pairs={{0,224},{32,0},{64,32},{96,64},{128,96},{160,128},{192,160},{224,1... | collective-permute-start | bytes 1425416 | tf_op jit(solution)/shard_map/ppermute | solution.py:17
  19.9 12.6 %collective-permute-start.5 = (f32[16,1600]{1,0:T(8,128)S(1)}, f32[16,1600]{1,0:T(8,128)S(1)}, u32[]{:S(2)}, u32[]{:S(2)}) collective-permute-start(f32[16,1600]{1,0:T(8,128)S(1)} %get-tuple-element.53.refs_0_), channel_id=1, source_target_pairs={{0,32},{32,64},{64,96},{96,128},{128,160},{160,192},{192,224},{224... | collective-permute-start | bytes 307208 | tf_op jit(solution)/shard_map/ppermute | solution.py:17
  19.9 12.6 %collective-permute-start.7 = (f32[16,1600]{1,0:T(8,128)S(1)}, f32[16,1600]{1,0:T(8,128)S(1)}, u32[]{:S(2)}, u32[]{:S(2)}) collective-permute-start(f32[16,1600]{1,0:T(8,128)S(1)} %get-tuple-element.53.refs_0_), channel_id=1, source_target_pairs={{0,224},{32,0},{64,32},{96,64},{128,96},{160,128},{192,160},{224,1... | collective-permute-start | bytes 307208 | tf_op jit(solution)/shard_map/ppermute | solution.py:17
  29.8 26.0 %collective-permute-start.18 = (f32[64,1856]{1,0:T(8,128)S(1)}, f32[64,1856]{1,0:T(8,128)S(1)}, u32[]{:S(2)}, u32[]{:S(2)}) collective-permute-start(f32[64,1856]{1,0:T(8,128)S(1)} %collective-permute-done.3.refs_1_), channel_id=1, source_target_pairs={{0,32},{32,64},{64,96},{96,128},{128,160},{160,192},{192,224},{224... | collective-permute-start | bytes 1425416 | tf_op jit(solution)/shard_map/ppermute | solution.py:17
  29.8 28.4 %collective-permute-start.21 = (f32[64,1856]{1,0:T(8,128)S(1)}, f32[64,1856]{1,0:T(8,128)S(1)}, u32[]{:S(2)}, u32[]{:S(2)}) collective-permute-start(f32[64,1856]{1,0:T(8,128)S(1)} %collective-permute-done.4.refs_8_), channel_id=1, source_target_pairs={{0,224},{32,0},{64,32},{96,64},{128,96},{160,128},{192,160},{224,1... | collective-permute-start | bytes 1425416 | tf_op jit(solution)/shard_map/ppermute | solution.py:17
  32.5 10.5 %collective-permute-start.6 = (f32[16,1600]{1,0:T(8,128)S(1)}, f32[16,1600]{1,0:T(8,128)S(1)}, u32[]{:S(2)}, u32[]{:S(2)}) collective-permute-start(f32[16,1600]{1,0:T(8,128)S(1)} %collective-permute-done.5.refs_1_), channel_id=1, source_target_pairs={{0,32},{32,64},{64,96},{96,128},{128,160},{160,192},{192,224},{224... | collective-permute-start | bytes 307208 | tf_op jit(solution)/shard_map/ppermute | solution.py:17
  32.5 10.5 %collective-permute-start.8 = (f32[16,1600]{1,0:T(8,128)S(1)}, f32[16,1600]{1,0:T(8,128)S(1)}, u32[]{:S(2)}, u32[]{:S(2)}) collective-permute-start(f32[16,1600]{1,0:T(8,128)S(1)} %collective-permute-done.7.refs_8_), channel_id=1, source_target_pairs={{0,224},{32,0},{64,32},{96,64},{128,96},{160,128},{192,160},{224,1... | collective-permute-start | bytes 307208 | tf_op jit(solution)/shard_map/ppermute | solution.py:17
  52.9 24.9 %collective-permute-start.13 = (f32[8,16,1280]{2,1,0:T(8,128)S(1)}, f32[8,16,1280]{2,1,0:T(8,128)S(1)}, u32[]{:S(2)}, u32[]{:S(2)}) collective-permute-start(f32[8,16,1280]{2,1,0:T(8,128)S(1)} %get-tuple-element.56.refs_0_.refs_9_), channel_id=1, source_target_pairs={{0,8},{8,16},{16,24},{24,0},{1,9},{9,17},{17,25},{25,1},{2,10},{10... | collective-permute-start | bytes 1966088 | tf_op jit(solution)/shard_map/ppermute | solution.py:17
  54.1 23.7 %collective-permute-start.15 = (f32[8,16,1280]{2,1,0:T(8,128)S(1)}, f32[8,16,1280]{2,1,0:T(8,128)S(1)}, u32[]{:S(2)}, u32[]{:S(2)}) collective-permute-start(f32[8,16,1280]{2,1,0:T(8,128)S(1)} %get-tuple-element.56.refs_0_.refs_9_), channel_id=1, source_target_pairs={{0,24},{8,0},{16,8},{24,16},{1,25},{9,1},{17,9},{25,17},{2,26},{10... | collective-permute-start | bytes 1966088 | tf_op jit(solution)/shard_map/ppermute | solution.py:17
  55.8 12.9 %collective-permute-start.26 = (f32[8,16,320]{2,1,0:T(8,128)S(1)}, f32[8,16,320]{2,1,0:T(8,128)S(1)}, u32[]{:S(2)}, u32[]{:S(2)}) collective-permute-start(f32[8,16,320]{2,1,0:T(8,128)S(1)} %get-tuple-element.63.b0), channel_id=1, source_target_pairs={{0,8},{8,16},{16,24},{24,0},{1,9},{9,17},{17,25},{25,1},{2,10},{10... | collective-permute-start | bytes 491528 | tf_op jit(solution)/shard_map/ppermute | solution.py:17
  55.8 17.7 %collective-permute-start.27 = (f32[8,16,320]{2,1,0:T(8,128)S(1)}, f32[8,16,320]{2,1,0:T(8,128)S(1)}, u32[]{:S(2)}, u32[]{:S(2)}) collective-permute-start(f32[8,16,320]{2,1,0:T(8,128)S(1)} %get-tuple-element.63.b0), channel_id=1, source_target_pairs={{0,16},{8,24},{16,0},{24,8},{1,17},{9,25},{17,1},{25,9},{2,18},{10... | collective-permute-start | bytes 491528 | tf_op jit(solution)/shard_map/ppermute | solution.py:17
  58.2 15.4 %collective-permute-start.28 = (f32[8,16,320]{2,1,0:T(8,128)S(1)}, f32[8,16,320]{2,1,0:T(8,128)S(1)}, u32[]{:S(2)}, u32[]{:S(2)}) collective-permute-start(f32[8,16,320]{2,1,0:T(8,128)S(1)} %get-tuple-element.63.b0), channel_id=1, source_target_pairs={{0,24},{8,0},{16,8},{24,16},{1,25},{9,1},{17,9},{25,17},{2,26},{10... | collective-permute-start | bytes 491528 | tf_op jit(solution)/shard_map/ppermute | solution.py:17
  73.7 10.3 %collective-permute-start.29 = (f32[1280,128]{1,0:T(8,128)S(1)}, f32[1280,128]{1,0:T(8,128)S(1)}, u32[]{:S(2)}, u32[]{:S(2)}) collective-permute-start(f32[1280,128]{1,0:T(8,128)S(1)} %low_rows.1.own), channel_id=1, source_target_pairs={{0,2},{2,0},{4,6},{6,4},{1,3},{3,1},{5,7},{7,5},{8,10},{10,8},{12,... | collective-permute-start | bytes 1966088 | tf_op jit(solution)/shard_map/ppermute | solution.py:21
  77.7 9.0 %collective-permute-start.14 = (f32[4,16,1280]{2,1,0:T(8,128)S(1)}, f32[4,16,1280]{2,1,0:T(8,128)S(1)}, u32[]{:S(2)}, u32[]{:S(2)}) collective-permute-start(f32[4,16,1280]{2,1,0:T(8,128)S(1)} %slice.26), channel_id=1, source_target_pairs={{0,8},{8,16},{16,24},{24,0},{1,9},{9,17},{17,25},{25,1},{2,10},{10... | collective-permute-start | bytes 983048 | tf_op jit(solution)/shard_map/ppermute | solution.py:17
  84.1 24.7 %collective-permute-start.30 = (f32[512,128]{1,0:T(8,128)S(1)}, f32[512,128]{1,0:T(8,128)S(1)}, u32[]{:S(2)}, u32[]{:S(2)}) collective-permute-start(f32[512,128]{1,0:T(8,128)S(1)} %pair.1), channel_id=1, source_target_pairs={{0,4},{2,6},{4,0},{6,2},{1,5},{3,7},{5,1},{7,3},{8,12},{10,14},{12... | collective-permute-start | bytes 786440 | tf_op jit(solution)/shard_map/ppermute | solution.py:21
  86.9 27.0 %collective-permute-start.17 = (f32[512,768]{1,0:T(8,128)S(1)}, f32[512,768]{1,0:T(8,128)S(1)}, u32[]{:S(2)}, u32[]{:S(2)}) collective-permute-start(f32[512,768]{1,0:T(8,128)S(1)} %mine.1), channel_id=1, source_target_pairs={{0,1},{1,0},{2,3},{3,2},{4,5},{5,4},{6,7},{7,6},{8,9},{9,8},{10,11... | collective-permute-start | bytes 4718600 | tf_op jit(solution)/shard_map/ppermute | solution.py:21
  98.1 10.6 %collective-permute-start.20 = (f32[32,1856]{1,0:T(8,128)S(1)}, f32[32,1856]{1,0:T(8,128)S(1)}, u32[]{:S(2)}, u32[]{:S(2)}) collective-permute-start(f32[32,1856]{1,0:T(8,128)S(1)} %slice.28), channel_id=1, source_target_pairs={{0,32},{32,64},{64,96},{96,128},{128,160},{160,192},{192,224},{224... | collective-permute-start | bytes 712712 | tf_op jit(solution)/shard_map/ppermute | solution.py:17
  108.9 10.0 %collective-permute-start.31 = (f32[512,768]{1,0:T(8,128)S(1)}, f32[512,768]{1,0:T(8,128)S(1)}, u32[]{:S(2)}, u32[]{:S(2)}) collective-permute-start(f32[512,768]{1,0:T(8,128)S(1)} %low_mine.1.mine), channel_id=1, source_target_pairs={{0,1},{1,0},{2,3},{3,2},{4,5},{5,4},{6,7},{7,6},{8,9},{9,8},{10,11... | collective-permute-start | bytes 4718600 | tf_op jit(solution)/shard_map/ppermute | solution.py:21
  115.9 14.3 %collective-permute-start.34 = (f32[512,128]{1,0:T(8,128)S(1)}, f32[512,128]{1,0:T(8,128)S(1)}, u32[]{:S(2)}, u32[]{:S(2)}) collective-permute-start(f32[512,128]{1,0:T(8,128)S(1)} %get-tuple-element.88.refs_4_), channel_id=1, source_target_pairs={{0,8},{8,16},{16,24},{24,0},{1,9},{9,17},{17,25},{25,1},{2,10},{10... | collective-permute-start | bytes 786440 | tf_op jit(solution)/shard_map/ppermute | solution.py:17
  115.9 14.3 %collective-permute-start.35 = (f32[512,128]{1,0:T(8,128)S(1)}, f32[512,128]{1,0:T(8,128)S(1)}, u32[]{:S(2)}, u32[]{:S(2)}) collective-permute-start(f32[512,128]{1,0:T(8,128)S(1)} %get-tuple-element.88.refs_4_), channel_id=1, source_target_pairs={{0,16},{8,24},{16,0},{24,8},{1,17},{9,25},{17,1},{25,9},{2,18},{10... | collective-permute-start | bytes 786440 | tf_op jit(solution)/shard_map/ppermute | solution.py:17
  116.9 13.6 %collective-permute-start.36 = (f32[512,128]{1,0:T(8,128)S(1)}, f32[512,128]{1,0:T(8,128)S(1)}, u32[]{:S(2)}, u32[]{:S(2)}) collective-permute-start(f32[512,128]{1,0:T(8,128)S(1)} %get-tuple-element.88.refs_4_), channel_id=1, source_target_pairs={{0,24},{8,0},{16,8},{24,16},{1,25},{9,1},{17,9},{25,17},{2,26},{10... | collective-permute-start | bytes 786440 | tf_op jit(solution)/shard_map/ppermute | solution.py:17
  134.5 12.4 %collective-permute-start.39 = (f32[384,128]{1,0:T(8,128)S(1)}, f32[384,128]{1,0:T(8,128)S(1)}, u32[]{:S(2)}, u32[]{:S(2)}) collective-permute-start(f32[384,128]{1,0:T(8,128)S(1)} %rows.1.refs_0_), channel_id=1, source_target_pairs={{0,16},{8,24},{16,0},{24,8},{1,17},{9,25},{17,1},{25,9},{2,18},{10... | collective-permute-start | bytes 589832 | tf_op jit(solution)/shard_map/ppermute | solution.py:17
  137.7 9.2 %collective-permute-start.40 = (f32[384,128]{1,0:T(8,128)S(1)}, f32[384,128]{1,0:T(8,128)S(1)}, u32[]{:S(2)}, u32[]{:S(2)}) collective-permute-start(f32[384,128]{1,0:T(8,128)S(1)} %rows.1.refs_0_), channel_id=1, source_target_pairs={{0,24},{8,0},{16,8},{24,16},{1,25},{9,1},{17,9},{25,17},{2,26},{10... | collective-permute-start | bytes 589832 | tf_op jit(solution)/shard_map/ppermute | solution.py:17
  (23 other events, 123.0 us)

commit v2 on v1

--- a/solution.py
+++ b/solution.py
@@ -19,29 +19,6 @@
 
 def swap(value, axis, mask):
     return lax.ppermute(value, axis, [(i, i ^ mask) for i in range(SIZES[axis])])
-
-
-def ring_z(block, *held):
-    half = block.shape[0] // 2
-    parts = [block] + [None] * 7
-    up = down = block
-    for step in range(1, 4):
-        if held and step == 3:
-            up, down = lax.optimization_barrier((up, down) + held)[:2]
-        up, down = shift(up, "z", 1), shift(down, "z", -1)
-        parts[step], parts[8 - step] = up, down
-    parts[4] = (shift(up[:half], "z", 1), shift(down[half:], "z", -1))
-    return parts
-
-
-def ring_x(block):
-    half = block.shape[0] // 2
-    up, down = shift(block, "x", 1), shift(block, "x", -1)
-    return [block, up, (shift(up[:half], "x", 1), shift(down[half:], "x", -1)), down]
-
-
-def cut(array, start, width):
-    return lax.slice_in_dim(array, start, start + width, axis=1)
 
 
 def parts_of(value):
@@ -108,35 +85,36 @@
 
 
 def column_blocks_kernel(*refs):
-    main, low = refs[9], refs[10]
-    for at, first, size in zip((0, 1, 2, 3, 4, 4, 5, 6, 7), (0, 0, 0, 0, 0, 8, 0, 0, 0), (16, 16, 16, 16, 8, 8, 16, 16, 16)):
-        ref = refs[at + (first > 0) if at <= 4 else at + 1]
-        main[at, first:first + size, :] = ref[:, 0:1280]
-        low[at, first:first + size, :] = ref[:, 1280:1600]
-
-
-def low_rows_kernel(b0, b1, b2, b3, out):
-    for k, ref in enumerate((b0, b1, b2, b3)):
-        for s in range(8):
-            at = s * 64 + k * 16
-            out[at:at + 16, :] = ref[s, :, 0:128]
-            out[512 + at:528 + at, :] = ref[s, :, 128:256]
-            out[1024 + at % 256:1040 + at % 256, at // 256 * 64:at // 256 * 64 + 64] = ref[s, :, 256:320]
+    main, low = refs[8], refs[9]
+    size = 16
+    for first, ref in zip(range(0, 128, 16), refs):
+        main[first // 16, :, :] = ref[:, 0:1280]
+        low[first:first + size, :] = ref[:, 1280:1408]
+        low[128 + first:128 + first + size, :] = ref[:, 1408:1536]
+        at = first // 64 * 64
+        low[256 + first % 64:256 + first % 64 + size, at:at + 64] = ref[:, 1536:1600]
 
 
 def pair_kernel(own, other, out):
     for i, ref in enumerate((own, other)):
-        out[0:256, 64 * i:64 * i + 64] = ref[1024:1280, 0:64]
-        out[256:512, 64 * i:64 * i + 64] = ref[1024:1280, 64:128]
-
-
-def low_mine_kernel(own, other, pair, far, out):
-    out[:, 0:128] = own[0:512]
-    out[:, 128:256] = other[0:512]
-    out[:, 256:384] = own[512:1024]
-    out[:, 384:512] = other[512:1024]
+        out[0:64, 64 * i:64 * i + 64] = ref[256:320, 0:64]
+        out[64:128, 64 * i:64 * i + 64] = ref[256:320, 64:128]
+
+
+def slab_kernel(own, other, pair, far, out):
+    out[:, 0:128] = own[0:128]
+    out[:, 128:256] = other[0:128]
+    out[:, 256:384] = own[128:256]
+    out[:, 384:512] = other[128:256]
     out[:, 512:640] = pair[...]
     out[:, 640:768] = far[...]
+
+
+def low_rows_kernel(b0, b1, b2, b2_low, b3, out):
+    for k, refs in enumerate(((b0,), (b1,), (b2, b2_low), (b3,))):
+        for s in range(8):
+            ref, at = refs[s // 4 if len(refs) > 1 else 0], 16 * (s % 4 if len(refs) > 1 else s)
+            out[s * 64 + k * 16:s * 64 + k * 16 + 16, :] = ref[at:at + 16, :]
 
 
 def mine_kernel(*refs):
@@ -298,26 +276,39 @@
         pack_kernel, "pack", [((16, 1600), F32)] + [((16, 1856), F32)] * 4,
         place, right_side, off_blocks[0], diag_inverse[0], limit=8)
 
-    rows_a = [stream_a[0]] + [shift(stream_a[k], "x", k) for k in (1, 2, 3)]
-    block_a = jnp.concatenate(rows_a, axis=0)
-    blocks_a = ring_z(block_a)
-    blocks_a = blocks_a[:4] + list(blocks_a[4]) + blocks_a[5:]
-
-    rows_b = ring_z(stream_b, block_a)
-    rows_b = rows_b[:4] + list(rows_b[4]) + rows_b[5:]
-    rows_b[0] = after(rows_b[0], blocks_a[1], blocks_a[8])
-    main, low_block = call(column_blocks_kernel, "column_blocks", [((8, 16, 1280), F32), ((8, 16, 320), F32)],
-                           *rows_b, scalars=0)
-    low_blocks = [shift(low_block, "x", k) for k in (1, 2, 3)]
-    low_block = after(low_block, blocks_a[2], blocks_a[7])
-    (own,) = call(low_rows_kernel, "low_rows", [((1280, 128), F32)], low_block, *low_blocks, scalars=0)
-    other = after(swap(own, "y", 1), blocks_a[3], blocks_a[6])
-    (pair,) = call(pair_kernel, "pair", [((512, 128), F32)], own, other, scalars=0)
-    (low_mine,) = call(low_mine_kernel, "low_mine", [((512, 768), F32)], own, other, pair,
-                       after(swap(pair, "y", 2), blocks_a[4], blocks_a[5]), scalars=0)
-    low_theirs = swap(low_mine, "core", 1)
-    blocks_b = ring_x(main)
-    blocks_b = blocks_b[:2] + list(blocks_b[2]) + blocks_b[3:]
+    wait = lax.optimization_barrier
+
+    def both_ways(up, down, axis):
+        return shift(up, axis, 1), shift(down, axis, -1)
+
+    b1 = both_ways(stream_b, stream_b, "z")
+    *b1, a_1, a_2, a_3 = wait((*b1, *stream_a[1:]))
+    b2 = both_ways(*b1, "z")
+    across = [shift(a_1, "x", 1), shift(a_2, "x", 2), shift(a_3, "x", 3)]
+    b3 = both_ways(*b2, "z")
+    b4 = shift(b3[0], "z", 1)
+    b4, *b3, across1, across2, across3 = wait((b4, *b3, *across))
+    block_a = jnp.concatenate([stream_a[0], across1, across2, across3], axis=0)
+    a1 = both_ways(block_a, block_a, "z")
+    main, low = call(column_blocks_kernel, "column_blocks", [((8, 16, 1280), F32), ((320, 128), F32)],
+                     stream_b, b1[0], b2[0], b3[0], b4, b3[1], b2[1], b1[1], scalars=0)
+    c1_up, c1_down = both_ways(main, main, "x")
+    other = swap(low, "y", 1)
+    other, a1_up, a1_down = wait((other, *a1))
+    a2 = both_ways(a1_up, a1_down, "z")
+    (pair,) = call(pair_kernel, "pair", [((128, 128), F32)], low, other, scalars=0)
+    far = swap(pair, "y", 2)
+    c2 = both_ways(c1_up[:4], c1_down[4:], "x")
+    a2_up, a2_down, far = wait((*a2, far))
+    a3 = both_ways(a2_up, a2_down, "z")
+    (slab,) = call(slab_kernel, "slab", [((128, 768), F32)], low, other, pair, far, scalars=0)
+    e1 = both_ways(slab, slab, "x")
+    a3_up, a3_down, c2_up, c2_down, e1_up, e1_down = wait((*a3, *c2, *e1))
+    a4 = both_ways(a3_up[:32], a3_down[32:], "z")
+    e2 = both_ways(e1_up[:64], e1_down[64:], "x")
+    *a4, e2_up, e2_down = wait((*a4, *e2))
+    blocks_b = [main, c1_up, c2_up, c2_down, c1_down]
+    blocks_a = [block_a, a1_up, a2_up, a3_up, a4[0], a4[1], a3_down, a2_down, a1_down]
 
     (mine,) = call(mine_kernel, "mine", [((512, 768), F32)], *blocks_b, scalars=0, limit=6)
     theirs = swap(mine, "core", 1)
@@ -329,10 +320,13 @@
         place, *blocks_a, *blocks_b,
         scratch=[pltpu.VMEM((512, 384), F32), pltpu.VMEM((128, 1536), F32)])
     got = swap(given, "core", 1)
+    slab, _ = wait((slab, given))
+    (low_mine,) = call(low_rows_kernel, "low_rows", [((512, 768), F32)], slab, e1_up, e2_up, e2_down, e1_down, scalars=0)
     mat2, y2t, up = call(
         level2_kernel, "level2", [((2, 512, 1536), BF16), ((64, 512), F32), ((64, 1024), F32)],
         mine, theirs, kept, got, b2t, scalars=0)
     got = swap(up, "y", 1)
+    low_theirs = swap(wait((low_mine, up))[0], "core", 1)
     y3 = after(y3, up)
     top_parts = [y3] + [shift(y3, "x", k) for k in (1, 2, 3)]
     (mat1,) = call(low_matrices_kernel, "low_matrices", [((2, 512, 1536), BF16)], low_mine, low_theirs, scalars=0)
@@ -351,7 +345,7 @@
                     scratch=[pltpu.VMEM((128, 1536), F32), pltpu.VMEM((128, 384), F32)])
     held = lax.optimization_barrier(tuple(mid_parts + top_parts) + (messages[0],))[:8]
     (forward,) = call(forward_kernel, "forward", [((960, 512), F32)], place, *held, limit=8)
-    arrived = [messages[0]] + [shift(after(messages[k], *mid_parts), "x", k) for k in (1, 2, 3)]
+    arrived = [messages[0]] + [shift(messages[k], "x", k) for k in (1, 2, 3)]
     forward, backward = call(
         final_kernel, "final", [((960, 512), F32), ((4, 16, 512), F32)], place, *arrived, forward,
         in_specs=[SMEM] + [VMEM] * 4 + [ANY], out_specs=[ANY, VMEM], aliases={5: 0},

time: 158 us -> 133 us (0.84)
  waiting for transfers between devices: 66.9 us -> 40.5 us
  starting transfers between devices: 71.6 us -> 74.2 us
    ppermute x35, waiting for transfers between devices: 60.4 us -> 34.8 us  [shift(): lax.ppermute(value, axis, [(i, (i + by) % size) for i in range(size)])]
    ppermute x9, starting transfers between devices: 21.2 us -> 25.8 us  [swap(): lax.ppermute(value, axis, [(i, i ^ mask) for i in range(SIZES[axis])])]
    ppermute x35, starting transfers between devices: 50.4 us -> 48.4 us  [shift(): lax.ppermute(value, axis, [(i, (i + by) % size) for i in range(size)])]
  transfers between devices with their start and end apart: 44 -> 44, of which waited for: 18 -> 20; matrix products, arithmetic and copies ran while one was open for 0% -> 0% of each run, Pallas kernels for 6% -> 6%
where the time goes in v2:
time: 133 us
  starting transfers between devices  74.2 us (56%)
  waiting for transfers between devices  40.5 us (30%)
  Pallas kernels  14.3 us (11%)
  local copies, waits for them, and re-layouts  2.92 us (2%)
    ppermute x35, starting transfers between devices, shift(): lax.ppermute(value, axis, [(i, (i + by) % size) for i in range(size)])  48.4 us
    ppermute x35, waiting for transfers between devices, shift(): lax.ppermute(value, axis, [(i, (i + by) % size) for i in range(size)])  34.8 us
    ppermute x9, starting transfers between devices, swap(): lax.ppermute(value, axis, [(i, i ^ mask) for i in range(SIZES[axis])])  25.8 us
    pallas_call x15, Pallas kernels, call(): pl.pallas_call(kernel, name=name, out_shape=[jax.ShapeDtypeStruct(shape,...  14.3 us
    ppermute x9, waiting for transfers between devices, swap(): lax.ppermute(value, axis, [(i, i ^ mask) for i in range(SIZES[axis])])  5.67 us
    unnamed x9, local copies, waits for them, and re-layouts  2.81 us
  transfers between devices with their start and end apart: 44, of which 20 were waited for; matrix products, arithmetic and copies ran while one was open for 0% of the time, Pallas kernels for 6%

profile of v2, /device:TPU:1, one launch (start us, length us, event | category | flops | bytes accessed | tf_op | source)
XLA Modules:
  0.0 133.0 jit_solution(5718473778686590020)
XLA Ops:
  4.2 2.5 %collective-permute-start = (f32[16,1600]{1,0:T(8,128)S(1)}, f32[16,1600]{1,0:T(8,128)S(1)}, u32[]{:S(2)}, u32[]{:S(2)}) collective-permute-start(f32[16,1600]{1,0:T(8,128)S(1)} %get-tuple-element.68.refs_0_), channel_id=1, source_target_pairs={{0,32},{32,64},{64,96},{96,128},{128,160},{160,192},{192,224},{224... | collective-permute-start | bytes 307208 | tf_op jit(solution)/shard_map/ppermute | solution.py:17
  6.7 4.0 %collective-permute-start.1 = (f32[16,1600]{1,0:T(8,128)S(1)}, f32[16,1600]{1,0:T(8,128)S(1)}, u32[]{:S(2)}, u32[]{:S(2)}) collective-permute-start(f32[16,1600]{1,0:T(8,128)S(1)} %get-tuple-element.68.refs_0_), channel_id=1, source_target_pairs={{0,224},{32,0},{64,32},{96,64},{128,96},{160,128},{192,160},{224,1... | collective-permute-start | bytes 307208 | tf_op jit(solution)/shard_map/ppermute | solution.py:17
  10.7 2.6 %collective-permute-done.refs_1_ = f32[16,1600]{1,0:T(8,128)S(1)} collective-permute-done((f32[16,1600]{1,0:T(8,128)S(1)}, f32[16,1600]{1,0:T(8,128)S(1)}, u32[]{:S(2)}, u32[]{:S(2)}) %collective-permute-start) | collective-permute-done | bytes 102432 | tf_op jit(solution)/shard_map/ppermute | solution.py:17
  13.4 2.7 %collective-permute-start.5 = (f32[16,1600]{1,0:T(8,128)S(1)}, f32[16,1600]{1,0:T(8,128)S(1)}, u32[]{:S(2)}, u32[]{:S(2)}) collective-permute-start(f32[16,1600]{1,0:T(8,128)S(1)} %collective-permute-done.1.refs_7_), channel_id=1, source_target_pairs={{0,224},{32,0},{64,32},{96,64},{128,96},{160,128},{192,160},{224,1... | collective-permute-start | bytes 307208 | tf_op jit(solution)/shard_map/ppermute | solution.py:17
  19.3 2.5 %collective-permute-start.8 = (f32[16,1856]{1,0:T(8,128)S(1)}, f32[16,1856]{1,0:T(8,128)S(1)}, u32[]{:S(2)}, u32[]{:S(2)}) collective-permute-start(f32[16,1856]{1,0:T(8,128)S(1)} %get-tuple-element.75), channel_id=1, source_target_pairs={{0,16},{8,24},{16,0},{24,8},{1,17},{9,25},{17,1},{25,9},{2,18},{10... | collective-permute-start | bytes 356360 | tf_op jit(solution)/shard_map/ppermute | solution.py:17
  22.9 2.7 %collective-permute-start.6 = (f32[16,1600]{1,0:T(8,128)S(1)}, f32[16,1600]{1,0:T(8,128)S(1)}, u32[]{:S(2)}, u32[]{:S(2)}) collective-permute-start(f32[16,1600]{1,0:T(8,128)S(1)} %collective-permute-done.5.refs_6_), channel_id=1, source_target_pairs={{0,224},{32,0},{64,32},{96,64},{128,96},{160,128},{192,160},{224,1... | collective-permute-start | bytes 307208 | tf_op jit(solution)/shard_map/ppermute | solution.py:17
  27.3 3.1 %collective-permute-done.4.refs_4_ = f32[16,1600]{1,0:T(8,128)S(1)} collective-permute-done((f32[16,1600]{1,0:T(8,128)S(1)}, f32[16,1600]{1,0:T(8,128)S(1)}, u32[]{:S(2)}, u32[]{:S(2)}) %collective-permute-start.4) | collective-permute-done | bytes 102432 | tf_op jit(solution)/shard_map/ppermute | solution.py:17
  30.5 2.7 %collective-permute-start.13 = (f32[64,1856]{1,0:T(8,128)S(1)}, f32[64,1856]{1,0:T(8,128)S(1)}, u32[]{:S(2)}, u32[]{:S(2)}) collective-permute-start(f32[64,1856]{1,0:T(8,128)S(1)} %constant_dynamic-update-slice_fusion.refs_0_), channel_id=1, source_target_pairs={{0,224},{32,0},{64,32},{96,64},{128,96},{160,128},{192,160},{224,1... | collective-permute-start | bytes 1425416 | tf_op jit(solution)/shard_map/ppermute | solution.py:17
  34.9 2.4 %collective-permute-start.20 = (f32[8,16,1280]{2,1,0:T(8,128)S(1)}, f32[8,16,1280]{2,1,0:T(8,128)S(1)}, u32[]{:S(2)}, u32[]{:S(2)}) collective-permute-start(f32[8,16,1280]{2,1,0:T(8,128)S(1)} %get-tuple-element.80.refs_0_.refs_9_), channel_id=1, source_target_pairs={{0,24},{8,0},{16,8},{24,16},{1,25},{9,1},{17,9},{25,17},{2,26},{10... | collective-permute-start | bytes 1966088 | tf_op jit(solution)/shard_map/ppermute | solution.py:17
  39.9 2.7 %collective-permute-start.15 = (f32[64,1856]{1,0:T(8,128)S(1)}, f32[64,1856]{1,0:T(8,128)S(1)}, u32[]{:S(2)}, u32[]{:S(2)}) collective-permute-start(f32[64,1856]{1,0:T(8,128)S(1)} %collective-permute-done.13.refs_8_), channel_id=1, source_target_pairs={{0,224},{32,0},{64,32},{96,64},{128,96},{160,128},{192,160},{224,1... | collective-permute-start | bytes 1425416 | tf_op jit(solution)/shard_map/ppermute | solution.py:17
  42.6 2.2 %collective-permute-done.10.refs_1_.refs_10_ = f32[8,16,1280]{2,1,0:T(8,128)S(1)} collective-permute-done((f32[8,16,1280]{2,1,0:T(8,128)S(1)}, f32[8,16,1280]{2,1,0:T(8,128)S(1)}, u32[]{:S(2)}, u32[]{:S(2)}) %collective-permute-start.10) | collective-permute-done | bytes 655392 | tf_op jit(solution)/shard_map/ppermute | solution.py:17
  45.0 3.0 %collective-permute-start.16 = (f32[128,128]{1,0:T(8,128)S(1)}, f32[128,128]{1,0:T(8,128)S(1)}, u32[]{:S(2)}, u32[]{:S(2)}) collective-permute-start(f32[128,128]{1,0:T(8,128)S(1)} %pair.1), channel_id=1, source_target_pairs={{0,4},{2,6},{4,0},{6,2},{1,5},{3,7},{5,1},{7,3},{8,12},{10,14},{12... | collective-permute-start | bytes 196616 | tf_op jit(solution)/shard_map/ppermute | solution.py:21
  50.9 2.7 %collective-permute-start.18 = (f32[64,1856]{1,0:T(8,128)S(1)}, f32[64,1856]{1,0:T(8,128)S(1)}, u32[]{:S(2)}, u32[]{:S(2)}) collective-permute-start(f32[64,1856]{1,0:T(8,128)S(1)} %collective-permute-done.15.refs_7_), channel_id=1, source_target_pairs={{0,224},{32,0},{64,32},{96,64},{128,96},{160,128},{192,160},{224,1... | collective-permute-start | bytes 1425416 | tf_op jit(solution)/shard_map/ppermute | solution.py:17
  54.0 2.4 %collective-permute-start.23 = (f32[128,768]{1,0:T(8,128)S(1)}, f32[128,768]{1,0:T(8,128)S(1)}, u32[]{:S(2)}, u32[]{:S(2)}) collective-permute-start(f32[128,768]{1,0:T(8,128)S(1)} %slab.1.b0), channel_id=1, source_target_pairs={{0,24},{8,0},{16,8},{24,16},{1,25},{9,1},{17,9},{25,17},{2,26},{10... | collective-permute-start | bytes 1179656 | tf_op jit(solution)/shard_map/ppermute | solution.py:17
  56.7 7.9 %collective-permute-done.21.refs_3_.refs_12_ = f32[4,16,1280]{2,1,0:T(8,128)S(1)} collective-permute-done((f32[4,16,1280]{2,1,0:T(8,128)S(1)}, f32[4,16,1280]{2,1,0:T(8,128)S(1)}, u32[]{:S(2)}, u32[]{:S(2)}) %collective-permute-start.21) | collective-permute-done | bytes 327712 | tf_op jit(solution)/shard_map/ppermute | solution.py:17
  65.1 12.7 %collective-permute-start.24 = (f32[512,768]{1,0:T(8,128)S(1)}, f32[512,768]{1,0:T(8,128)S(1)}, u32[]{:S(2)}, u32[]{:S(2)}) collective-permute-start(f32[512,768]{1,0:T(8,128)S(1)} %mine.1), channel_id=1, source_target_pairs={{0,1},{1,0},{2,3},{3,2},{4,5},{5,4},{6,7},{7,6},{8,9},{9,8},{10,11... | collective-permute-start | bytes 4718600 | tf_op jit(solution)/shard_map/ppermute | solution.py:21
  77.8 2.1 %collective-permute-start.25 = (f32[32,1856]{1,0:T(8,128)S(1)}, f32[32,1856]{1,0:T(8,128)S(1)}, u32[]{:S(2)}, u32[]{:S(2)}) collective-permute-start(f32[32,1856]{1,0:T(8,128)S(1)} %slice.20), channel_id=1, source_target_pairs={{0,32},{32,64},{64,96},{96,128},{128,160},{160,192},{192,224},{224... | collective-permute-start | bytes 712712 | tf_op jit(solution)/shard_map/ppermute | solution.py:17
  80.8 3.4 %collective-permute-start.28 = (f32[64,768]{1,0:T(8,128)S(1)}, f32[64,768]{1,0:T(8,128)S(1)}, u32[]{:S(2)}, u32[]{:S(2)}) collective-permute-start(f32[64,768]{1,0:T(8,128)S(1)} %slice.23), channel_id=1, source_target_pairs={{0,24},{8,0},{16,8},{24,16},{1,25},{9,1},{17,9},{25,17},{2,26},{10... | collective-permute-start | bytes 589832 | tf_op jit(solution)/shard_map/ppermute | solution.py:17
  84.1 4.6 %collective-permute-done.27.b2 = f32[64,768]{1,0:T(8,128)S(1)} collective-permute-done((f32[64,768]{1,0:T(8,128)S(1)}, f32[64,768]{1,0:T(8,128)S(1)}, u32[]{:S(2)}, u32[]{:S(2)}) %collective-permute-start.27) | collective-permute-done | bytes 196640 | tf_op jit(solution)/shard_map/ppermute | solution.py:17
  88.8 2.3 %level3.1 = (bf16[2,512,2048]{2,1,0:T(8,128)(2,1)S(1)}, f32[256,512]{1,0:T(8,128)S(1)}, f32[512,128]{1,0:T(8,128)S(1)}, f32[64,1536]{1,0:T(8,128)S(1)}, f32[64,1536]{1,0:T(8,128)S(1)}, /*index=5*/f32[64,512]{1,0:T(8,128)S(1)}) custom-call(s32[4]{0:T(128)S(1)} %pad_add_fusion.place, f32[64,1856]{1,0:T(8,128)S(1)} %constant_dynamic-update-slice_fusion.refs_0_, ...), custom_call_target="tpu_custom_call" | custom-call | tf_op jit(solution)/shard_map/level3/pallas_call | solution.py:256
  98.0 3.0 %collective-permute-start.35 = (f32[512,128]{1,0:T(8,128)S(1)}, f32[512,128]{1,0:T(8,128)S(1)}, u32[]{:S(2)}, u32[]{:S(2)}) collective-permute-start(f32[512,128]{1,0:T(8,128)S(1)} %get-tuple-element.128.refs_4_), channel_id=1, source_target_pairs={{0,16},{8,24},{16,0},{24,8},{1,17},{9,25},{17,1},{25,9},{2,18},{10... | collective-permute-start | bytes 786440 | tf_op jit(solution)/shard_map/ppermute | solution.py:17
  104.2 3.0 %collective-permute-start.32 = (f32[64,512]{1,0:T(8,128)S(1)}, f32[64,512]{1,0:T(8,128)S(1)}, u32[]{:S(2)}, u32[]{:S(2)}) collective-permute-start(f32[64,512]{1,0:T(8,128)S(1)} %get-tuple-element.110.up_ref), channel_id=1, source_target_pairs={{0,4},{2,6},{4,0},{6,2},{1,5},{3,7},{5,1},{7,3},{8,12},{10,14},{12... | collective-permute-start | bytes 393224 | tf_op jit(solution)/shard_map/ppermute | solution.py:21
  110.1 2.5 %collective-permute-done.35.refs_6_ = f32[512,128]{1,0:T(8,128)S(1)} collective-permute-done((f32[512,128]{1,0:T(8,128)S(1)}, f32[512,128]{1,0:T(8,128)S(1)}, u32[]{:S(2)}, u32[]{:S(2)}) %collective-permute-start.35) | collective-permute-done | bytes 262176 | tf_op jit(solution)/shard_map/ppermute | solution.py:17
  124.9 3.2 %collective-permute-done.42.refs_2_ = f32[384,128]{1,0:T(8,128)S(1)} collective-permute-done((f32[384,128]{1,0:T(8,128)S(1)}, f32[384,128]{1,0:T(8,128)S(1)}, u32[]{:S(2)}, u32[]{:S(2)}) %collective-permute-start.42) | collective-permute-done | bytes 196640 | tf_op jit(solution)/shard_map/ppermute | solution.py:17
  (96 shorter events, 49.3 us)
Async XLA Ops:
  4.2 9.2 %collective-permute-start = (f32[16,1600]{1,0:T(8,128)S(1)}, f32[16,1600]{1,0:T(8,128)S(1)}, u32[]{:S(2)}, u32[]{:S(2)}) collective-permute-start(f32[16,1600]{1,0:T(8,128)S(1)} %get-tuple-element.68.refs_0_), channel_id=1, source_target_pairs={{0,32},{32,64},{64,96},{96,128},{128,160},{160,192},{192,224},{224... | collective-permute-start | bytes 307208 | tf_op jit(solution)/shard_map/ppermute | solution.py:17
  13.4 9.6 %collective-permute-start.5 = (f32[16,1600]{1,0:T(8,128)S(1)}, f32[16,1600]{1,0:T(8,128)S(1)}, u32[]{:S(2)}, u32[]{:S(2)}) collective-permute-start(f32[16,1600]{1,0:T(8,128)S(1)} %collective-permute-done.1.refs_7_), channel_id=1, source_target_pairs={{0,224},{32,0},{64,32},{96,64},{128,96},{160,128},{192,160},{224,1... | collective-permute-start | bytes 307208 | tf_op jit(solution)/shard_map/ppermute | solution.py:17
  30.4 9.5 %collective-permute-start.12 = (f32[64,1856]{1,0:T(8,128)S(1)}, f32[64,1856]{1,0:T(8,128)S(1)}, u32[]{:S(2)}, u32[]{:S(2)}) collective-permute-start(f32[64,1856]{1,0:T(8,128)S(1)} %constant_dynamic-update-slice_fusion.refs_0_), channel_id=1, source_target_pairs={{0,32},{32,64},{64,96},{96,128},{128,160},{160,192},{192,224},{224... | collective-permute-start | bytes 1425416 | tf_op jit(solution)/shard_map/ppermute | solution.py:17
  30.5 9.4 %collective-permute-start.13 = (f32[64,1856]{1,0:T(8,128)S(1)}, f32[64,1856]{1,0:T(8,128)S(1)}, u32[]{:S(2)}, u32[]{:S(2)}) collective-permute-start(f32[64,1856]{1,0:T(8,128)S(1)} %constant_dynamic-update-slice_fusion.refs_0_), channel_id=1, source_target_pairs={{0,224},{32,0},{64,32},{96,64},{128,96},{160,128},{192,160},{224,1... | collective-permute-start | bytes 1425416 | tf_op jit(solution)/shard_map/ppermute | solution.py:17
  33.3 11.5 %collective-permute-start.10 = (f32[8,16,1280]{2,1,0:T(8,128)S(1)}, f32[8,16,1280]{2,1,0:T(8,128)S(1)}, u32[]{:S(2)}, u32[]{:S(2)}) collective-permute-start(f32[8,16,1280]{2,1,0:T(8,128)S(1)} %get-tuple-element.80.refs_0_.refs_9_), channel_id=1, source_target_pairs={{0,8},{8,16},{16,24},{24,0},{1,9},{9,17},{17,25},{25,1},{2,10},{10... | collective-permute-start | bytes 1966088 | tf_op jit(solution)/shard_map/ppermute | solution.py:17
  34.9 19.0 %collective-permute-start.20 = (f32[8,16,1280]{2,1,0:T(8,128)S(1)}, f32[8,16,1280]{2,1,0:T(8,128)S(1)}, u32[]{:S(2)}, u32[]{:S(2)}) collective-permute-start(f32[8,16,1280]{2,1,0:T(8,128)S(1)} %get-tuple-element.80.refs_0_.refs_9_), channel_id=1, source_target_pairs={{0,24},{8,0},{16,8},{24,16},{1,25},{9,1},{17,9},{25,17},{2,26},{10... | collective-permute-start | bytes 1966088 | tf_op jit(solution)/shard_map/ppermute | solution.py:17
  39.9 11.0 %collective-permute-start.14 = (f32[64,1856]{1,0:T(8,128)S(1)}, f32[64,1856]{1,0:T(8,128)S(1)}, u32[]{:S(2)}, u32[]{:S(2)}) collective-permute-start(f32[64,1856]{1,0:T(8,128)S(1)} %collective-permute-done.12.refs_1_), channel_id=1, source_target_pairs={{0,32},{32,64},{64,96},{96,128},{128,160},{160,192},{192,224},{224... | collective-permute-start | bytes 1425416 | tf_op jit(solution)/shard_map/ppermute | solution.py:17
  39.9 11.0 %collective-permute-start.15 = (f32[64,1856]{1,0:T(8,128)S(1)}, f32[64,1856]{1,0:T(8,128)S(1)}, u32[]{:S(2)}, u32[]{:S(2)}) collective-permute-start(f32[64,1856]{1,0:T(8,128)S(1)} %collective-permute-done.13.refs_8_), channel_id=1, source_target_pairs={{0,224},{32,0},{64,32},{96,64},{128,96},{160,128},{192,160},{224,1... | collective-permute-start | bytes 1425416 | tf_op jit(solution)/shard_map/ppermute | solution.py:17
  44.8 11.6 %collective-permute-start.19 = (f32[4,16,1280]{2,1,0:T(8,128)S(1)}, f32[4,16,1280]{2,1,0:T(8,128)S(1)}, u32[]{:S(2)}, u32[]{:S(2)}) collective-permute-start(f32[4,16,1280]{2,1,0:T(8,128)S(1)} %slice.24), channel_id=1, source_target_pairs={{0,8},{8,16},{16,24},{24,0},{1,9},{9,17},{17,25},{25,1},{2,10},{10... | collective-permute-start | bytes 983048 | tf_op jit(solution)/shard_map/ppermute | solution.py:17
  50.9 14.1 %collective-permute-start.17 = (f32[64,1856]{1,0:T(8,128)S(1)}, f32[64,1856]{1,0:T(8,128)S(1)}, u32[]{:S(2)}, u32[]{:S(2)}) collective-permute-start(f32[64,1856]{1,0:T(8,128)S(1)} %collective-permute-done.14.refs_2_), channel_id=1, source_target_pairs={{0,32},{32,64},{64,96},{96,128},{128,160},{160,192},{192,224},{224... | collective-permute-start | bytes 1425416 | tf_op jit(solution)/shard_map/ppermute | solution.py:17
  50.9 14.1 %collective-permute-start.18 = (f32[64,1856]{1,0:T(8,128)S(1)}, f32[64,1856]{1,0:T(8,128)S(1)}, u32[]{:S(2)}, u32[]{:S(2)}) collective-permute-start(f32[64,1856]{1,0:T(8,128)S(1)} %collective-permute-done.15.refs_7_), channel_id=1, source_target_pairs={{0,224},{32,0},{64,32},{96,64},{128,96},{160,128},{192,160},{224,1... | collective-permute-start | bytes 1425416 | tf_op jit(solution)/shard_map/ppermute | solution.py:17
  53.6 11.4 %collective-permute-start.22 = (f32[128,768]{1,0:T(8,128)S(1)}, f32[128,768]{1,0:T(8,128)S(1)}, u32[]{:S(2)}, u32[]{:S(2)}) collective-permute-start(f32[128,768]{1,0:T(8,128)S(1)} %slab.1.b0), channel_id=1, source_target_pairs={{0,8},{8,16},{16,24},{24,0},{1,9},{9,17},{17,25},{25,1},{2,10},{10... | collective-permute-start | bytes 1179656 | tf_op jit(solution)/shard_map/ppermute | solution.py:17
  54.0 11.0 %collective-permute-start.23 = (f32[128,768]{1,0:T(8,128)S(1)}, f32[128,768]{1,0:T(8,128)S(1)}, u32[]{:S(2)}, u32[]{:S(2)}) collective-permute-start(f32[128,768]{1,0:T(8,128)S(1)} %slab.1.b0), channel_id=1, source_target_pairs={{0,24},{8,0},{16,8},{24,16},{1,25},{9,1},{17,9},{25,17},{2,26},{10... | collective-permute-start | bytes 1179656 | tf_op jit(solution)/shard_map/ppermute | solution.py:17
  65.1 28.5 %collective-permute-start.24 = (f32[512,768]{1,0:T(8,128)S(1)}, f32[512,768]{1,0:T(8,128)S(1)}, u32[]{:S(2)}, u32[]{:S(2)}) collective-permute-start(f32[512,768]{1,0:T(8,128)S(1)} %mine.1), channel_id=1, source_target_pairs={{0,1},{1,0},{2,3},{3,2},{4,5},{5,4},{6,7},{7,6},{8,9},{9,8},{10,11... | collective-permute-start | bytes 4718600 | tf_op jit(solution)/shard_map/ppermute | solution.py:21
  77.8 11.0 %collective-permute-start.25 = (f32[32,1856]{1,0:T(8,128)S(1)}, f32[32,1856]{1,0:T(8,128)S(1)}, u32[]{:S(2)}, u32[]{:S(2)}) collective-permute-start(f32[32,1856]{1,0:T(8,128)S(1)} %slice.20), channel_id=1, source_target_pairs={{0,32},{32,64},{64,96},{96,128},{128,160},{160,192},{192,224},{224... | collective-permute-start | bytes 712712 | tf_op jit(solution)/shard_map/ppermute | solution.py:17
  80.0 8.8 %collective-permute-start.26 = (f32[32,1856]{1,0:T(8,128)S(1)}, f32[32,1856]{1,0:T(8,128)S(1)}, u32[]{:S(2)}, u32[]{:S(2)}) collective-permute-start(f32[32,1856]{1,0:T(8,128)S(1)} %slice.21), channel_id=1, source_target_pairs={{0,224},{32,0},{64,32},{96,64},{128,96},{160,128},{192,160},{224,1... | collective-permute-start | bytes 712712 | tf_op jit(solution)/shard_map/ppermute | solution.py:17
  97.0 13.0 %collective-permute-start.34 = (f32[512,128]{1,0:T(8,128)S(1)}, f32[512,128]{1,0:T(8,128)S(1)}, u32[]{:S(2)}, u32[]{:S(2)}) collective-permute-start(f32[512,128]{1,0:T(8,128)S(1)} %get-tuple-element.128.refs_4_), channel_id=1, source_target_pairs={{0,8},{8,16},{16,24},{24,0},{1,9},{9,17},{17,25},{25,1},{2,10},{10... | collective-permute-start | bytes 786440 | tf_op jit(solution)/shard_map/ppermute | solution.py:17
  98.0 14.6 %collective-permute-start.35 = (f32[512,128]{1,0:T(8,128)S(1)}, f32[512,128]{1,0:T(8,128)S(1)}, u32[]{:S(2)}, u32[]{:S(2)}) collective-permute-start(f32[512,128]{1,0:T(8,128)S(1)} %get-tuple-element.128.refs_4_), channel_id=1, source_target_pairs={{0,16},{8,24},{16,0},{24,8},{1,17},{9,25},{17,1},{25,9},{2,18},{10... | collective-permute-start | bytes 786440 | tf_op jit(solution)/shard_map/ppermute | solution.py:17
  101.0 11.6 %collective-permute-start.36 = (f32[512,128]{1,0:T(8,128)S(1)}, f32[512,128]{1,0:T(8,128)S(1)}, u32[]{:S(2)}, u32[]{:S(2)}) collective-permute-start(f32[512,128]{1,0:T(8,128)S(1)} %get-tuple-element.128.refs_4_), channel_id=1, source_target_pairs={{0,24},{8,0},{16,8},{24,16},{1,25},{9,1},{17,9},{25,17},{2,26},{10... | collective-permute-start | bytes 786440 | tf_op jit(solution)/shard_map/ppermute | solution.py:17
  104.2 8.4 %collective-permute-start.32 = (f32[64,512]{1,0:T(8,128)S(1)}, f32[64,512]{1,0:T(8,128)S(1)}, u32[]{:S(2)}, u32[]{:S(2)}) collective-permute-start(f32[64,512]{1,0:T(8,128)S(1)} %get-tuple-element.110.up_ref), channel_id=1, source_target_pairs={{0,4},{2,6},{4,0},{6,2},{1,5},{3,7},{5,1},{7,3},{8,12},{10,14},{12... | collective-permute-start | bytes 393224 | tf_op jit(solution)/shard_map/ppermute | solution.py:21
  116.8 11.4 %collective-permute-start.42 = (f32[384,128]{1,0:T(8,128)S(1)}, f32[384,128]{1,0:T(8,128)S(1)}, u32[]{:S(2)}, u32[]{:S(2)}) collective-permute-start(f32[384,128]{1,0:T(8,128)S(1)} %rows.1.refs_0_), channel_id=1, source_target_pairs={{0,16},{8,24},{16,0},{24,8},{1,17},{9,25},{17,1},{25,9},{2,18},{10... | collective-permute-start | bytes 589832 | tf_op jit(solution)/shard_map/ppermute | solution.py:17
  118.9 9.2 %collective-permute-start.43 = (f32[384,128]{1,0:T(8,128)S(1)}, f32[384,128]{1,0:T(8,128)S(1)}, u32[]{:S(2)}, u32[]{:S(2)}) collective-permute-start(f32[384,128]{1,0:T(8,128)S(1)} %rows.1.refs_0_), channel_id=1, source_target_pairs={{0,24},{8,0},{16,8},{24,16},{1,25},{9,1},{17,9},{25,17},{2,26},{10... | collective-permute-start | bytes 589832 | tf_op jit(solution)/shard_map/ppermute | solution.py:17
  121.9 8.4 %collective-permute-start.38 = (f32[128,128]{1,0:T(8,128)S(1)}, f32[128,128]{1,0:T(8,128)S(1)}, u32[]{:S(2)}, u32[]{:S(2)}) collective-permute-start(f32[128,128]{1,0:T(8,128)S(1)} %get-tuple-element.121), channel_id=1, source_target_pairs={{0,8},{8,16},{16,24},{24,0},{1,9},{9,17},{17,25},{25,1},{2,10},{10... | collective-permute-start | bytes 196616 | tf_op jit(solution)/shard_map/ppermute | solution.py:17
  122.2 8.7 %collective-permute-start.39 = (f32[128,128]{1,0:T(8,128)S(1)}, f32[128,128]{1,0:T(8,128)S(1)}, u32[]{:S(2)}, u32[]{:S(2)}) collective-permute-start(f32[128,128]{1,0:T(8,128)S(1)} %get-tuple-element.122), channel_id=1, source_target_pairs={{0,16},{8,24},{16,0},{24,8},{1,17},{9,25},{17,1},{25,9},{2,18},{10... | collective-permute-start | bytes 196616 | tf_op jit(solution)/shard_map/ppermute | solution.py:17
  (23 other events, 121.7 us)

commit v3 on v2

--- a/solution.py
+++ b/solution.py
@@ -228,25 +228,26 @@
             outs[k][64 + 16 * n:80 + 16 * n, :] = rows[at:at + 16]
 
 
-def forward_kernel(place, *refs):
-    out = refs[8]
-    for k in range(4):
+def forward_kernel(place, p0, p1, p2, p3, out):
+    for k, ref in enumerate((p0, p1, p2, p3)):
         at = pl.ds(pl.multiple_of(lax.rem(place[1] + 4 - k, 4) * 128, 128), 128)
-        out[0:64, at] = jnp.zeros((64, 128), F32)
-        out[64:448, at] = refs[k][...]
-        out[448:960, at] = refs[4 + k][...]
-
-
-def final_kernel(place, m0, m1, m2, m3, forward_in, forward_out, x_out, top, sem):
+        out[0:448, at] = jnp.zeros((448, 128), F32)
+        out[448:960, at] = ref[...]
+
+
+def final_kernel(place, m0, m1, m2, m3, r0, r1, r2, r3, forward_in, forward_out, x_hbm, top, x_out, sems):
     del forward_in
-    for k, ref in enumerate((m0, m1, m2, m3)):
+    for k, (ref, rows) in enumerate(((m0, r0), (m1, r1), (m2, r2), (m3, r3))):
         at = pl.ds(pl.multiple_of(lax.rem(place[1] + 4 - k, 4) * 128, 128), 128)
-        top[:, at] = ref[0:64, :]
+        top[0:64, at] = ref[0:64, :]
+        top[64:448, at] = rows[...]
         for n in range(4):
             x_out[n, :, at] = ref[64 + 16 * n:80 + 16 * n, :]
-    copy = pltpu.make_async_copy(top, forward_out.at[0:64], sem)
-    copy.start()
-    copy.wait()
+    copies = (pltpu.make_async_copy(top, forward_out.at[0:448], sems.at[0]), pltpu.make_async_copy(x_out, x_hbm, sems.at[1]))
+    for copy in copies:
+        copy.start()
+    for copy in copies:
+        copy.wait()
 
 
 VMEM, SMEM, ANY = (pl.BlockSpec(memory_space=m) for m in (pltpu.VMEM, pltpu.SMEM, pl.ANY))
@@ -282,11 +283,11 @@
         return shift(up, axis, 1), shift(down, axis, -1)
 
     b1 = both_ways(stream_b, stream_b, "z")
-    *b1, a_1, a_2, a_3 = wait((*b1, *stream_a[1:]))
+    *b1, a_1, a_2, a_3, far_b = wait((*b1, *stream_a[1:], stream_b))
     b2 = both_ways(*b1, "z")
+    b4 = shift(far_b, "z", 4)
     across = [shift(a_1, "x", 1), shift(a_2, "x", 2), shift(a_3, "x", 3)]
     b3 = both_ways(*b2, "z")
-    b4 = shift(b3[0], "z", 1)
     b4, *b3, across1, across2, across3 = wait((b4, *b3, *across))
     block_a = jnp.concatenate([stream_a[0], across1, across2, across3], axis=0)
     a1 = both_ways(block_a, block_a, "z")
@@ -343,13 +344,14 @@
 
     messages = call(last_kernel, "last", [((128, 128), F32)] * 4, place, low, swap(low, "core", 1), y0t, keep, mat3,
                     scratch=[pltpu.VMEM((128, 1536), F32), pltpu.VMEM((128, 384), F32)])
-    held = lax.optimization_barrier(tuple(mid_parts + top_parts) + (messages[0],))[:8]
+    held = wait(tuple(top_parts) + (messages[0],))[:4]
     (forward,) = call(forward_kernel, "forward", [((960, 512), F32)], place, *held, limit=8)
     arrived = [messages[0]] + [shift(messages[k], "x", k) for k in (1, 2, 3)]
     forward, backward = call(
-        final_kernel, "final", [((960, 512), F32), ((4, 16, 512), F32)], place, *arrived, forward,
-        in_specs=[SMEM] + [VMEM] * 4 + [ANY], out_specs=[ANY, VMEM], aliases={5: 0},
-        scratch=[pltpu.VMEM((64, 512), F32), pltpu.SemaphoreType.DMA], limit=4)
+        final_kernel, "final", [((960, 512), F32), ((4, 16, 512), F32)],
+        place, *arrived, *mid_parts, forward,
+        in_specs=[SMEM] + [VMEM] * 8 + [ANY], out_specs=[ANY, ANY], aliases={9: 0},
+        scratch=[pltpu.VMEM((448, 512), F32), pltpu.VMEM((4, 16, 512), F32), pltpu.SemaphoreType.DMA((2,))], limit=4)
     return forward[None], backward[None]
 
 

time: 133 us -> 131 us (0.985)
  waiting for transfers between devices: 40.5 us -> 34.8 us
  starting transfers between devices: 74.2 us -> 78 us
    ppermute x35, waiting for transfers between devices: 34.8 us -> 27.7 us  [shift(): lax.ppermute(value, axis, [(i, (i + by) % size) for i in range(size)])]
    ppermute x35, starting transfers between devices: 48.4 us -> 53.4 us  [shift(): lax.ppermute(value, axis, [(i, (i + by) % size) for i in range(size)])]
    ppermute x9, waiting for transfers between devices: 5.67 us -> 7.07 us  [swap(): lax.ppermute(value, axis, [(i, i ^ mask) for i in range(SIZES[axis])])]
  transfers between devices with their start and end apart: 44 -> 44, of which waited for: 20 -> 17; matrix products, arithmetic and copies ran while one was open for 0% -> 0% of each run, Pallas kernels for 6% -> 6%
where the time goes in v3:
time: 131 us
  starting transfers between devices  78 us (60%)
  waiting for transfers between devices  34.8 us (27%)
  Pallas kernels  14 us (11%)
  local copies, waits for them, and re-layouts  2.92 us (2%)
    ppermute x35, starting transfers between devices, shift(): lax.ppermute(value, axis, [(i, (i + by) % size) for i in range(size)])  53.4 us
    ppermute x35, waiting for transfers between devices, shift(): lax.ppermute(value, axis, [(i, (i + by) % size) for i in range(size)])  27.7 us
    ppermute x9, starting transfers between devices, swap(): lax.ppermute(value, axis, [(i, i ^ mask) for i in range(SIZES[axis])])  24.6 us
    pallas_call x15, Pallas kernels, call(): pl.pallas_call(kernel, name=name, out_shape=[jax.ShapeDtypeStruct(shape,...  14 us
    ppermute x9, waiting for transfers between devices, swap(): lax.ppermute(value, axis, [(i, i ^ mask) for i in range(SIZES[axis])])  7.07 us
    unnamed x9, local copies, waits for them, and re-layouts  2.81 us
  transfers between devices with their start and end apart: 44, of which 17 were waited for; matrix products, arithmetic and copies ran while one was open for 0% of the time, Pallas kernels for 6%

profile of v3, /device:TPU:1, one launch (start us, length us, event | category | flops | bytes accessed | tf_op | source)
XLA Modules:
  0.0 130.8 jit_solution(604596734369338917)
XLA Ops:
  4.2 2.5 %collective-permute-start = (f32[16,1600]{1,0:T(8,128)S(1)}, f32[16,1600]{1,0:T(8,128)S(1)}, u32[]{:S(2)}, u32[]{:S(2)}) collective-permute-start(f32[16,1600]{1,0:T(8,128)S(1)} %get-tuple-element.70.refs_0_), channel_id=1, source_target_pairs={{0,32},{32,64},{64,96},{96,128},{128,160},{160,192},{192,224},{224... | collective-permute-start | bytes 307208 | tf_op jit(solution)/shard_map/ppermute | solution.py:17
  6.7 4.0 %collective-permute-start.1 = (f32[16,1600]{1,0:T(8,128)S(1)}, f32[16,1600]{1,0:T(8,128)S(1)}, u32[]{:S(2)}, u32[]{:S(2)}) collective-permute-start(f32[16,1600]{1,0:T(8,128)S(1)} %get-tuple-element.70.refs_0_), channel_id=1, source_target_pairs={{0,224},{32,0},{64,32},{96,64},{128,96},{160,128},{192,160},{224,1... | collective-permute-start | bytes 307208 | tf_op jit(solution)/shard_map/ppermute | solution.py:17
  10.7 2.6 %collective-permute-done.refs_1_ = f32[16,1600]{1,0:T(8,128)S(1)} collective-permute-done((f32[16,1600]{1,0:T(8,128)S(1)}, f32[16,1600]{1,0:T(8,128)S(1)}, u32[]{:S(2)}, u32[]{:S(2)}) %collective-permute-start) | collective-permute-done | bytes 102432 | tf_op jit(solution)/shard_map/ppermute | solution.py:17
  13.4 2.7 %collective-permute-start.5 = (f32[16,1600]{1,0:T(8,128)S(1)}, f32[16,1600]{1,0:T(8,128)S(1)}, u32[]{:S(2)}, u32[]{:S(2)}) collective-permute-start(f32[16,1600]{1,0:T(8,128)S(1)} %collective-permute-done.1.refs_7_), channel_id=1, source_target_pairs={{0,224},{32,0},{64,32},{96,64},{128,96},{160,128},{192,160},{224,1... | collective-permute-start | bytes 307208 | tf_op jit(solution)/shard_map/ppermute | solution.py:17
  16.0 3.4 %collective-permute-start.3 = (f32[16,1600]{1,0:T(8,128)S(1)}, f32[16,1600]{1,0:T(8,128)S(1)}, u32[]{:S(2)}, u32[]{:S(2)}) collective-permute-start(f32[16,1600]{1,0:T(8,128)S(1)} %get-tuple-element.70.refs_0_), channel_id=1, source_target_pairs={{0,128},{32,160},{64,192},{96,224},{128,0},{160,32},{192,64},{224,... | collective-permute-start | bytes 307208 | tf_op jit(solution)/shard_map/ppermute | solution.py:17
  20.6 2.5 %collective-permute-start.8 = (f32[16,1856]{1,0:T(8,128)S(1)}, f32[16,1856]{1,0:T(8,128)S(1)}, u32[]{:S(2)}, u32[]{:S(2)}) collective-permute-start(f32[16,1856]{1,0:T(8,128)S(1)} %get-tuple-element.73), channel_id=1, source_target_pairs={{0,16},{8,24},{16,0},{24,8},{1,17},{9,25},{17,1},{25,9},{2,18},{10... | collective-permute-start | bytes 356360 | tf_op jit(solution)/shard_map/ppermute | solution.py:17
  24.4 3.2 %collective-permute-start.6 = (f32[16,1600]{1,0:T(8,128)S(1)}, f32[16,1600]{1,0:T(8,128)S(1)}, u32[]{:S(2)}, u32[]{:S(2)}) collective-permute-start(f32[16,1600]{1,0:T(8,128)S(1)} %collective-permute-done.5.refs_6_), channel_id=1, source_target_pairs={{0,224},{32,0},{64,32},{96,64},{128,96},{160,128},{192,160},{224,1... | collective-permute-start | bytes 307208 | tf_op jit(solution)/shard_map/ppermute | solution.py:17
  29.5 3.1 %collective-permute-start.13 = (f32[64,1856]{1,0:T(8,128)S(1)}, f32[64,1856]{1,0:T(8,128)S(1)}, u32[]{:S(2)}, u32[]{:S(2)}) collective-permute-start(f32[64,1856]{1,0:T(8,128)S(1)} %constant_dynamic-update-slice_fusion.refs_0_), channel_id=1, source_target_pairs={{0,224},{32,0},{64,32},{96,64},{128,96},{160,128},{192,160},{224,1... | collective-permute-start | bytes 1425416 | tf_op jit(solution)/shard_map/ppermute | solution.py:17
  39.8 2.7 %collective-permute-start.15 = (f32[64,1856]{1,0:T(8,128)S(1)}, f32[64,1856]{1,0:T(8,128)S(1)}, u32[]{:S(2)}, u32[]{:S(2)}) collective-permute-start(f32[64,1856]{1,0:T(8,128)S(1)} %collective-permute-done.13.refs_8_), channel_id=1, source_target_pairs={{0,224},{32,0},{64,32},{96,64},{128,96},{160,128},{192,160},{224,1... | collective-permute-start | bytes 1425416 | tf_op jit(solution)/shard_map/ppermute | solution.py:17
  42.4 3.2 %collective-permute-done.10.refs_1_.refs_10_ = f32[8,16,1280]{2,1,0:T(8,128)S(1)} collective-permute-done((f32[8,16,1280]{2,1,0:T(8,128)S(1)}, f32[8,16,1280]{2,1,0:T(8,128)S(1)}, u32[]{:S(2)}, u32[]{:S(2)}) %collective-permute-start.10) | collective-permute-done | bytes 655392 | tf_op jit(solution)/shard_map/ppermute | solution.py:17
  46.7 3.0 %collective-permute-start.16 = (f32[128,128]{1,0:T(8,128)S(1)}, f32[128,128]{1,0:T(8,128)S(1)}, u32[]{:S(2)}, u32[]{:S(2)}) collective-permute-start(f32[128,128]{1,0:T(8,128)S(1)} %pair.1), channel_id=1, source_target_pairs={{0,4},{2,6},{4,0},{6,2},{1,5},{3,7},{5,1},{7,3},{8,12},{10,14},{12... | collective-permute-start | bytes 196616 | tf_op jit(solution)/shard_map/ppermute | solution.py:21
  51.4 2.7 %collective-permute-start.18 = (f32[64,1856]{1,0:T(8,128)S(1)}, f32[64,1856]{1,0:T(8,128)S(1)}, u32[]{:S(2)}, u32[]{:S(2)}) collective-permute-start(f32[64,1856]{1,0:T(8,128)S(1)} %collective-permute-done.15.refs_7_), channel_id=1, source_target_pairs={{0,224},{32,0},{64,32},{96,64},{128,96},{160,128},{192,160},{224,1... | collective-permute-start | bytes 1425416 | tf_op jit(solution)/shard_map/ppermute | solution.py:17
  54.6 2.3 %collective-permute-start.23 = (f32[128,768]{1,0:T(8,128)S(1)}, f32[128,768]{1,0:T(8,128)S(1)}, u32[]{:S(2)}, u32[]{:S(2)}) collective-permute-start(f32[128,768]{1,0:T(8,128)S(1)} %slab.1.b0), channel_id=1, source_target_pairs={{0,24},{8,0},{16,8},{24,16},{1,25},{9,1},{17,9},{25,17},{2,26},{10... | collective-permute-start | bytes 1179656 | tf_op jit(solution)/shard_map/ppermute | solution.py:17
  57.6 7.6 %collective-permute-done.21.refs_3_.refs_12_ = f32[4,16,1280]{2,1,0:T(8,128)S(1)} collective-permute-done((f32[4,16,1280]{2,1,0:T(8,128)S(1)}, f32[4,16,1280]{2,1,0:T(8,128)S(1)}, u32[]{:S(2)}, u32[]{:S(2)}) %collective-permute-start.21) | collective-permute-done | bytes 327712 | tf_op jit(solution)/shard_map/ppermute | solution.py:17
  65.2 11.0 %collective-permute-start.24 = (f32[512,768]{1,0:T(8,128)S(1)}, f32[512,768]{1,0:T(8,128)S(1)}, u32[]{:S(2)}, u32[]{:S(2)}) collective-permute-start(f32[512,768]{1,0:T(8,128)S(1)} %mine.1), channel_id=1, source_target_pairs={{0,1},{1,0},{2,3},{3,2},{4,5},{5,4},{6,7},{7,6},{8,9},{9,8},{10,11... | collective-permute-start | bytes 4718600 | tf_op jit(solution)/shard_map/ppermute | solution.py:21
  82.0 4.3 %collective-permute-done.27.b2 = f32[64,768]{1,0:T(8,128)S(1)} collective-permute-done((f32[64,768]{1,0:T(8,128)S(1)}, f32[64,768]{1,0:T(8,128)S(1)}, u32[]{:S(2)}, u32[]{:S(2)}) %collective-permute-start.27) | collective-permute-done | bytes 196640 | tf_op jit(solution)/shard_map/ppermute | solution.py:17
  86.4 2.3 %level3.1 = (bf16[2,512,2048]{2,1,0:T(8,128)(2,1)S(1)}, f32[256,512]{1,0:T(8,128)S(1)}, f32[512,128]{1,0:T(8,128)S(1)}, f32[64,1536]{1,0:T(8,128)S(1)}, f32[64,1536]{1,0:T(8,128)S(1)}, /*index=5*/f32[64,512]{1,0:T(8,128)S(1)}) custom-call(s32[4]{0:T(128)S(1)} %pad_add_fusion.place, f32[64,1856]{1,0:T(8,128)S(1)} %constant_dynamic-update-slice_fusion.refs_0_, ...), custom_call_target="tpu_custom_call" | custom-call | tf_op jit(solution)/shard_map/level3/pallas_call | solution.py:257
  96.3 2.6 %collective-permute-start.35 = (f32[512,128]{1,0:T(8,128)S(1)}, f32[512,128]{1,0:T(8,128)S(1)}, u32[]{:S(2)}, u32[]{:S(2)}) collective-permute-start(f32[512,128]{1,0:T(8,128)S(1)} %get-tuple-element.122.p0), channel_id=1, source_target_pairs={{0,16},{8,24},{16,0},{24,8},{1,17},{9,25},{17,1},{25,9},{2,18},{10... | collective-permute-start | bytes 786440 | tf_op jit(solution)/shard_map/ppermute | solution.py:17
  102.3 3.0 %collective-permute-start.32 = (f32[64,512]{1,0:T(8,128)S(1)}, f32[64,512]{1,0:T(8,128)S(1)}, u32[]{:S(2)}, u32[]{:S(2)}) collective-permute-start(f32[64,512]{1,0:T(8,128)S(1)} %get-tuple-element.108.up_ref), channel_id=1, source_target_pairs={{0,4},{2,6},{4,0},{6,2},{1,5},{3,7},{5,1},{7,3},{8,12},{10,14},{12... | collective-permute-start | bytes 393224 | tf_op jit(solution)/shard_map/ppermute | solution.py:21
  108.1 2.4 %collective-permute-done.35.p2 = f32[512,128]{1,0:T(8,128)S(1)} collective-permute-done((f32[512,128]{1,0:T(8,128)S(1)}, f32[512,128]{1,0:T(8,128)S(1)}, u32[]{:S(2)}, u32[]{:S(2)}) %collective-permute-start.35) | collective-permute-done | bytes 262176 | tf_op jit(solution)/shard_map/ppermute | solution.py:17
  110.5 2.0 %level0.1 = (f32[64,512]{1,0:T(8,128)S(1)}, f32[64,1600]{1,0:T(8,128)S(1)}) custom-call(f32[64,512]{1,0:T(8,128)S(1)} %get-tuple-element.108.up_ref, f32[64,512]{1,0:T(8,128)S(1)} %collective-permute-done.32.got, f32[64,512]{1,0:T(8,128)S(1)} %get-tuple-element.102.y2t, f32[64,512]{1,0:T(8,128)S(1)} %get-tuple-element.109.y1t, ...), custom_call_target="tpu_custom_call" | custom-call | tf_op jit(solution)/shard_map/level0/pallas_call | solution.py:257
  114.8 2.1 %collective-permute-start.42 = (f32[384,128]{1,0:T(8,128)S(1)}, f32[384,128]{1,0:T(8,128)S(1)}, u32[]{:S(2)}, u32[]{:S(2)}) collective-permute-start(f32[384,128]{1,0:T(8,128)S(1)} %rows.1.r0), channel_id=1, source_target_pairs={{0,16},{8,24},{16,0},{24,8},{1,17},{9,25},{17,1},{25,9},{2,18},{10... | collective-permute-start | bytes 589832 | tf_op jit(solution)/shard_map/ppermute | solution.py:17
  122.8 2.1 %forward.1.forward_in = f32[960,512]{1,0:T(8,128)} custom-call(s32[4]{0:T(128)S(1)} %pad_add_fusion.place, f32[512,128]{1,0:T(8,128)S(1)} %get-tuple-element.122.p0, f32[512,128]{1,0:T(8,128)S(1)} %collective-permute-done.34.p1, f32[512,128]{1,0:T(8,128)S(1)} %collective-permute-done.35.p2, f32[512,128]{1,0:T(8,128)S(1)} %collective-permute-done.36.p3), custom_call_target="tpu_custom_call" | custom-call | tf_op jit(solution)/shard_map/forward/pallas_call | solution.py:257
  126.1 2.1 %collective-permute-done.38.m1 = f32[128,128]{1,0:T(8,128)S(1)} collective-permute-done((f32[128,128]{1,0:T(8,128)S(1)}, f32[128,128]{1,0:T(8,128)S(1)}, u32[]{:S(2)}, u32[]{:S(2)}) %collective-permute-start.38) | collective-permute-done | bytes 65568 | tf_op jit(solution)/shard_map/ppermute | solution.py:17
  (96 shorter events, 50.6 us)
Async XLA Ops:
  4.2 9.2 %collective-permute-start = (f32[16,1600]{1,0:T(8,128)S(1)}, f32[16,1600]{1,0:T(8,128)S(1)}, u32[]{:S(2)}, u32[]{:S(2)}) collective-permute-start(f32[16,1600]{1,0:T(8,128)S(1)} %get-tuple-element.70.refs_0_), channel_id=1, source_target_pairs={{0,32},{32,64},{64,96},{96,128},{128,160},{160,192},{192,224},{224... | collective-permute-start | bytes 307208 | tf_op jit(solution)/shard_map/ppermute | solution.py:17
  13.4 9.7 %collective-permute-start.2 = (f32[16,1600]{1,0:T(8,128)S(1)}, f32[16,1600]{1,0:T(8,128)S(1)}, u32[]{:S(2)}, u32[]{:S(2)}) collective-permute-start(f32[16,1600]{1,0:T(8,128)S(1)} %collective-permute-done.refs_1_), channel_id=1, source_target_pairs={{0,32},{32,64},{64,96},{96,128},{128,160},{160,192},{192,224},{224... | collective-permute-start | bytes 307208 | tf_op jit(solution)/shard_map/ppermute | solution.py:17
  13.4 10.9 %collective-permute-start.5 = (f32[16,1600]{1,0:T(8,128)S(1)}, f32[16,1600]{1,0:T(8,128)S(1)}, u32[]{:S(2)}, u32[]{:S(2)}) collective-permute-start(f32[16,1600]{1,0:T(8,128)S(1)} %collective-permute-done.1.refs_7_), channel_id=1, source_target_pairs={{0,224},{32,0},{64,32},{96,64},{128,96},{160,128},{192,160},{224,1... | collective-permute-start | bytes 307208 | tf_op jit(solution)/shard_map/ppermute | solution.py:17
  16.0 8.4 %collective-permute-start.3 = (f32[16,1600]{1,0:T(8,128)S(1)}, f32[16,1600]{1,0:T(8,128)S(1)}, u32[]{:S(2)}, u32[]{:S(2)}) collective-permute-start(f32[16,1600]{1,0:T(8,128)S(1)} %get-tuple-element.70.refs_0_), channel_id=1, source_target_pairs={{0,128},{32,160},{64,192},{96,224},{128,0},{160,32},{192,64},{224,... | collective-permute-start | bytes 307208 | tf_op jit(solution)/shard_map/ppermute | solution.py:17
  29.4 10.4 %collective-permute-start.12 = (f32[64,1856]{1,0:T(8,128)S(1)}, f32[64,1856]{1,0:T(8,128)S(1)}, u32[]{:S(2)}, u32[]{:S(2)}) collective-permute-start(f32[64,1856]{1,0:T(8,128)S(1)} %constant_dynamic-update-slice_fusion.refs_0_), channel_id=1, source_target_pairs={{0,32},{32,64},{64,96},{96,128},{128,160},{160,192},{192,224},{224... | collective-permute-start | bytes 1425416 | tf_op jit(solution)/shard_map/ppermute | solution.py:17
  29.5 10.3 %collective-permute-start.13 = (f32[64,1856]{1,0:T(8,128)S(1)}, f32[64,1856]{1,0:T(8,128)S(1)}, u32[]{:S(2)}, u32[]{:S(2)}) collective-permute-start(f32[64,1856]{1,0:T(8,128)S(1)} %constant_dynamic-update-slice_fusion.refs_0_), channel_id=1, source_target_pairs={{0,224},{32,0},{64,32},{96,64},{128,96},{160,128},{192,160},{224,1... | collective-permute-start | bytes 1425416 | tf_op jit(solution)/shard_map/ppermute | solution.py:17
  32.7 12.9 %collective-permute-start.10 = (f32[8,16,1280]{2,1,0:T(8,128)S(1)}, f32[8,16,1280]{2,1,0:T(8,128)S(1)}, u32[]{:S(2)}, u32[]{:S(2)}) collective-permute-start(f32[8,16,1280]{2,1,0:T(8,128)S(1)} %get-tuple-element.78.refs_0_.refs_9_), channel_id=1, source_target_pairs={{0,8},{8,16},{16,24},{24,0},{1,9},{9,17},{17,25},{25,1},{2,10},{10... | collective-permute-start | bytes 1966088 | tf_op jit(solution)/shard_map/ppermute | solution.py:17
  35.2 19.3 %collective-permute-start.20 = (f32[8,16,1280]{2,1,0:T(8,128)S(1)}, f32[8,16,1280]{2,1,0:T(8,128)S(1)}, u32[]{:S(2)}, u32[]{:S(2)}) collective-permute-start(f32[8,16,1280]{2,1,0:T(8,128)S(1)} %get-tuple-element.78.refs_0_.refs_9_), channel_id=1, source_target_pairs={{0,24},{8,0},{16,8},{24,16},{1,25},{9,1},{17,9},{25,17},{2,26},{10... | collective-permute-start | bytes 1966088 | tf_op jit(solution)/shard_map/ppermute | solution.py:17
  39.8 11.6 %collective-permute-start.14 = (f32[64,1856]{1,0:T(8,128)S(1)}, f32[64,1856]{1,0:T(8,128)S(1)}, u32[]{:S(2)}, u32[]{:S(2)}) collective-permute-start(f32[64,1856]{1,0:T(8,128)S(1)} %collective-permute-done.12.refs_1_), channel_id=1, source_target_pairs={{0,32},{32,64},{64,96},{96,128},{128,160},{160,192},{192,224},{224... | collective-permute-start | bytes 1425416 | tf_op jit(solution)/shard_map/ppermute | solution.py:17
  39.8 11.6 %collective-permute-start.15 = (f32[64,1856]{1,0:T(8,128)S(1)}, f32[64,1856]{1,0:T(8,128)S(1)}, u32[]{:S(2)}, u32[]{:S(2)}) collective-permute-start(f32[64,1856]{1,0:T(8,128)S(1)} %collective-permute-done.13.refs_8_), channel_id=1, source_target_pairs={{0,224},{32,0},{64,32},{96,64},{128,96},{160,128},{192,160},{224,1... | collective-permute-start | bytes 1425416 | tf_op jit(solution)/shard_map/ppermute | solution.py:17
  45.6 11.3 %collective-permute-start.19 = (f32[4,16,1280]{2,1,0:T(8,128)S(1)}, f32[4,16,1280]{2,1,0:T(8,128)S(1)}, u32[]{:S(2)}, u32[]{:S(2)}) collective-permute-start(f32[4,16,1280]{2,1,0:T(8,128)S(1)} %slice.24), channel_id=1, source_target_pairs={{0,8},{8,16},{16,24},{24,0},{1,9},{9,17},{17,25},{25,1},{2,10},{10... | collective-permute-start | bytes 983048 | tf_op jit(solution)/shard_map/ppermute | solution.py:17
  51.4 13.7 %collective-permute-start.17 = (f32[64,1856]{1,0:T(8,128)S(1)}, f32[64,1856]{1,0:T(8,128)S(1)}, u32[]{:S(2)}, u32[]{:S(2)}) collective-permute-start(f32[64,1856]{1,0:T(8,128)S(1)} %collective-permute-done.14.refs_2_), channel_id=1, source_target_pairs={{0,32},{32,64},{64,96},{96,128},{128,160},{160,192},{192,224},{224... | collective-permute-start | bytes 1425416 | tf_op jit(solution)/shard_map/ppermute | solution.py:17
  51.4 13.7 %collective-permute-start.18 = (f32[64,1856]{1,0:T(8,128)S(1)}, f32[64,1856]{1,0:T(8,128)S(1)}, u32[]{:S(2)}, u32[]{:S(2)}) collective-permute-start(f32[64,1856]{1,0:T(8,128)S(1)} %collective-permute-done.15.refs_7_), channel_id=1, source_target_pairs={{0,224},{32,0},{64,32},{96,64},{128,96},{160,128},{192,160},{224,1... | collective-permute-start | bytes 1425416 | tf_op jit(solution)/shard_map/ppermute | solution.py:17
  54.1 11.0 %collective-permute-start.22 = (f32[128,768]{1,0:T(8,128)S(1)}, f32[128,768]{1,0:T(8,128)S(1)}, u32[]{:S(2)}, u32[]{:S(2)}) collective-permute-start(f32[128,768]{1,0:T(8,128)S(1)} %slab.1.b0), channel_id=1, source_target_pairs={{0,8},{8,16},{16,24},{24,0},{1,9},{9,17},{17,25},{25,1},{2,10},{10... | collective-permute-start | bytes 1179656 | tf_op jit(solution)/shard_map/ppermute | solution.py:17
  54.6 10.6 %collective-permute-start.23 = (f32[128,768]{1,0:T(8,128)S(1)}, f32[128,768]{1,0:T(8,128)S(1)}, u32[]{:S(2)}, u32[]{:S(2)}) collective-permute-start(f32[128,768]{1,0:T(8,128)S(1)} %slab.1.b0), channel_id=1, source_target_pairs={{0,24},{8,0},{16,8},{24,16},{1,25},{9,1},{17,9},{25,17},{2,26},{10... | collective-permute-start | bytes 1179656 | tf_op jit(solution)/shard_map/ppermute | solution.py:17
  65.2 26.5 %collective-permute-start.24 = (f32[512,768]{1,0:T(8,128)S(1)}, f32[512,768]{1,0:T(8,128)S(1)}, u32[]{:S(2)}, u32[]{:S(2)}) collective-permute-start(f32[512,768]{1,0:T(8,128)S(1)} %mine.1), channel_id=1, source_target_pairs={{0,1},{1,0},{2,3},{3,2},{4,5},{5,4},{6,7},{7,6},{8,9},{9,8},{10,11... | collective-permute-start | bytes 4718600 | tf_op jit(solution)/shard_map/ppermute | solution.py:21
  76.3 10.1 %collective-permute-start.25 = (f32[32,1856]{1,0:T(8,128)S(1)}, f32[32,1856]{1,0:T(8,128)S(1)}, u32[]{:S(2)}, u32[]{:S(2)}) collective-permute-start(f32[32,1856]{1,0:T(8,128)S(1)} %slice.20), channel_id=1, source_target_pairs={{0,32},{32,64},{64,96},{96,128},{128,160},{160,192},{192,224},{224... | collective-permute-start | bytes 712712 | tf_op jit(solution)/shard_map/ppermute | solution.py:17
  95.1 13.0 %collective-permute-start.34 = (f32[512,128]{1,0:T(8,128)S(1)}, f32[512,128]{1,0:T(8,128)S(1)}, u32[]{:S(2)}, u32[]{:S(2)}) collective-permute-start(f32[512,128]{1,0:T(8,128)S(1)} %get-tuple-element.122.p0), channel_id=1, source_target_pairs={{0,8},{8,16},{16,24},{24,0},{1,9},{9,17},{17,25},{25,1},{2,10},{10... | collective-permute-start | bytes 786440 | tf_op jit(solution)/shard_map/ppermute | solution.py:17
  96.3 14.2 %collective-permute-start.35 = (f32[512,128]{1,0:T(8,128)S(1)}, f32[512,128]{1,0:T(8,128)S(1)}, u32[]{:S(2)}, u32[]{:S(2)}) collective-permute-start(f32[512,128]{1,0:T(8,128)S(1)} %get-tuple-element.122.p0), channel_id=1, source_target_pairs={{0,16},{8,24},{16,0},{24,8},{1,17},{9,25},{17,1},{25,9},{2,18},{10... | collective-permute-start | bytes 786440 | tf_op jit(solution)/shard_map/ppermute | solution.py:17
  98.9 11.6 %collective-permute-start.36 = (f32[512,128]{1,0:T(8,128)S(1)}, f32[512,128]{1,0:T(8,128)S(1)}, u32[]{:S(2)}, u32[]{:S(2)}) collective-permute-start(f32[512,128]{1,0:T(8,128)S(1)} %get-tuple-element.122.p0), channel_id=1, source_target_pairs={{0,24},{8,0},{16,8},{24,16},{1,25},{9,1},{17,9},{25,17},{2,26},{10... | collective-permute-start | bytes 786440 | tf_op jit(solution)/shard_map/ppermute | solution.py:17
  114.8 11.3 %collective-permute-start.42 = (f32[384,128]{1,0:T(8,128)S(1)}, f32[384,128]{1,0:T(8,128)S(1)}, u32[]{:S(2)}, u32[]{:S(2)}) collective-permute-start(f32[384,128]{1,0:T(8,128)S(1)} %rows.1.r0), channel_id=1, source_target_pairs={{0,16},{8,24},{16,0},{24,8},{1,17},{9,25},{17,1},{25,9},{2,18},{10... | collective-permute-start | bytes 589832 | tf_op jit(solution)/shard_map/ppermute | solution.py:17
  116.9 9.2 %collective-permute-start.43 = (f32[384,128]{1,0:T(8,128)S(1)}, f32[384,128]{1,0:T(8,128)S(1)}, u32[]{:S(2)}, u32[]{:S(2)}) collective-permute-start(f32[384,128]{1,0:T(8,128)S(1)} %rows.1.r0), channel_id=1, source_target_pairs={{0,24},{8,0},{16,8},{24,16},{1,25},{9,1},{17,9},{25,17},{2,26},{10... | collective-permute-start | bytes 589832 | tf_op jit(solution)/shard_map/ppermute | solution.py:17
  119.8 8.4 %collective-permute-start.38 = (f32[128,128]{1,0:T(8,128)S(1)}, f32[128,128]{1,0:T(8,128)S(1)}, u32[]{:S(2)}, u32[]{:S(2)}) collective-permute-start(f32[128,128]{1,0:T(8,128)S(1)} %get-tuple-element.119), channel_id=1, source_target_pairs={{0,8},{8,16},{16,24},{24,0},{1,9},{9,17},{17,25},{25,1},{2,10},{10... | collective-permute-start | bytes 196616 | tf_op jit(solution)/shard_map/ppermute | solution.py:17
  120.2 8.7 %collective-permute-start.39 = (f32[128,128]{1,0:T(8,128)S(1)}, f32[128,128]{1,0:T(8,128)S(1)}, u32[]{:S(2)}, u32[]{:S(2)}) collective-permute-start(f32[128,128]{1,0:T(8,128)S(1)} %get-tuple-element.120), channel_id=1, source_target_pairs={{0,16},{8,24},{16,0},{24,8},{1,17},{9,25},{17,1},{25,9},{2,18},{10... | collective-permute-start | bytes 196616 | tf_op jit(solution)/shard_map/ppermute | solution.py:17
  (23 other events, 126.2 us)

commit v4 on v3

--- a/solution.py
+++ b/solution.py
@@ -52,11 +52,7 @@
 
 
 def rows_of_b(refs):
-    found = []
-    for k, first, count, ref in ((0, 0, 8, refs[0]), (1, 0, 8, refs[1]), (2, 0, 4, refs[2]), (2, 4, 4, refs[3]),
-                                 (3, 0, 8, refs[4])):
-        found += [((first + s) * 64 + k * 16, s, ref) for s in range(count)]
-    return found
+    return [(s * 64 + k * 16, s, ref) for k, ref in enumerate(refs) for s in range(8)]
 
 
 def put_parts(mat, rows, columns, value):
@@ -66,21 +62,21 @@
 
 
 def pack_kernel(place, right, off, diag, b_out, *a_outs):
-    b_out[:, 1280:1408] = off[:, 0:128]
-    b_out[:, 1408:1536] = diag[:, 64:192]
-    b_out[:, 1536:1600] = diag[:, 0:64]
+    b_out[:, 1536:1664] = off[:, 0:128]
+    b_out[:, 1664:1792] = diag[:, 64:192]
+    b_out[:, 1792:1856] = diag[:, 0:64]
     b_out[:, 0:768] = diag[:, 192:960]
-    b_out[:, 768:1280] = off[:, 128:640]
+    b_out[:, 768:1536] = off[:, 128:896]
     x, core = place[1], place[3]
     column = 2 * place[2] + core
     for k in range(4):
         out = a_outs[k]
         at = pl.ds(pl.multiple_of(lax.rem(x + k, 4) * 128, 128), 128)
-        out[:, 0:1536] = off[:, 640:2176]
-        out[:, 1536:1664] = right[7 + column, :, at]
+        out[:, 0:1280] = off[:, 896:2176]
+        out[:, 1280:1408] = right[7 + column, :, at]
         for m in (2, 1, 0):
             both = right[2**m - 1 + lax.shift_right_logical(column, 3 - m), :, at]
-            to = 1664 + 64 * (2 - m)
+            to = 1408 + 64 * (2 - m)
             out[:, to:to + 64] = jnp.where(core == 0, both[:, 0:64], both[:, 64:128])
 
 
@@ -88,11 +84,11 @@
     main, low = refs[8], refs[9]
     size = 16
     for first, ref in zip(range(0, 128, 16), refs):
-        main[first // 16, :, :] = ref[:, 0:1280]
-        low[first:first + size, :] = ref[:, 1280:1408]
-        low[128 + first:128 + first + size, :] = ref[:, 1408:1536]
+        main[first // 16, :, :] = ref[:, 0:1536]
+        low[first:first + size, :] = ref[:, 1536:1664]
+        low[128 + first:128 + first + size, :] = ref[:, 1664:1792]
         at = first // 64 * 64
-        low[256 + first % 64:256 + first % 64 + size, at:at + 64] = ref[:, 1536:1600]
+        low[256 + first % 64:256 + first % 64 + size, at:at + 64] = ref[:, 1792:1856]
 
 
 def pair_kernel(own, other, out):
@@ -118,20 +114,21 @@
 
 
 def mine_kernel(*refs):
-    out = refs[5]
-    for start, s, ref in rows_of_b(refs[:5]):
+    out = refs[4]
+    for start, s, ref in rows_of_b(refs[:4]):
         out[start:start + 16, 0:256] = ref[s, :, 0:256]
         out[start:start + 16, 256:768] = ref[s, :, 768:1280]
 
 
 def level3_kernel(place, *refs):
-    a_refs, b_refs = rows_of_a(refs[:9]), rows_of_b(refs[9:14])
-    mat, keep, y3_out, kept_out, given_out, b2t_out, rhs, up = refs[14:]
+    a_refs, b_refs = rows_of_a(refs[:9]), rows_of_b(refs[9:13])
+    mat, keep, y3_out, kept_out, given_out, b2t_out, rhs, up = refs[13:]
     for start, size, ref in a_refs:
-        rhs[start:start + size, 0:320] = ref[:, 1536:1856]
-        put_parts(mat, slice(start, start + size), slice(0, 1536), ref[:, 0:1536])
+        rhs[start:start + size, 0:320] = ref[:, 1280:1600]
+        put_parts(mat, slice(start, start + size), slice(256, 1536), ref[:, 0:1280])
     for start, s, ref in b_refs:
         put_parts(mat, slice(start, start + 16), slice(1536, 2048), ref[s, :, 256:768])
+        put_parts(mat, slice(start, start + 16), slice(0, 256), ref[s, :, 1280:1536])
     rhs[:, 320:384] = jnp.zeros((512, 64), F32)
     b3t = rhs[:, 0:128].T
     b21t = rhs[:, 128:256].T
@@ -274,7 +271,7 @@
     place = jnp.stack([lax.axis_index(a) for a in ("z", "x", "y", "core")]).astype(jnp.int32)
 
     stream_b, *stream_a = call(
-        pack_kernel, "pack", [((16, 1600), F32)] + [((16, 1856), F32)] * 4,
+        pack_kernel, "pack", [((16, 1856), F32)] + [((16, 1600), F32)] * 4,
         place, right_side, off_blocks[0], diag_inverse[0], limit=8)
 
     wait = lax.optimization_barrier
@@ -291,7 +288,7 @@
     b4, *b3, across1, across2, across3 = wait((b4, *b3, *across))
     block_a = jnp.concatenate([stream_a[0], across1, across2, across3], axis=0)
     a1 = both_ways(block_a, block_a, "z")
-    main, low = call(column_blocks_kernel, "column_blocks", [((8, 16, 1280), F32), ((320, 128), F32)],
+    main, low = call(column_blocks_kernel, "column_blocks", [((8, 16, 1536), F32), ((320, 128), F32)],
                      stream_b, b1[0], b2[0], b3[0], b4, b3[1], b2[1], b1[1], scalars=0)
     c1_up, c1_down = both_ways(main, main, "x")
     other = swap(low, "y", 1)
@@ -299,16 +296,17 @@
     a2 = both_ways(a1_up, a1_down, "z")
     (pair,) = call(pair_kernel, "pair", [((128, 128), F32)], low, other, scalars=0)
     far = swap(pair, "y", 2)
-    c2 = both_ways(c1_up[:4], c1_down[4:], "x")
-    a2_up, a2_down, far = wait((*a2, far))
+    c2 = shift(c1_up, "x", 1)
+    a2_up, a2_down, far, c1_down = wait((*a2, far, c1_down))
     a3 = both_ways(a2_up, a2_down, "z")
     (slab,) = call(slab_kernel, "slab", [((128, 768), F32)], low, other, pair, far, scalars=0)
     e1 = both_ways(slab, slab, "x")
-    a3_up, a3_down, c2_up, c2_down, e1_up, e1_down = wait((*a3, *c2, *e1))
+    e1_up, e1_down = e1
+    a3_up, a3_down, e1_down = wait((*a3, e1_down))
     a4 = both_ways(a3_up[:32], a3_down[32:], "z")
     e2 = both_ways(e1_up[:64], e1_down[64:], "x")
-    *a4, e2_up, e2_down = wait((*a4, *e2))
-    blocks_b = [main, c1_up, c2_up, c2_down, c1_down]
+    *a4, c2, e1_up, e2_up, e2_down = wait((*a4, c2, e1_up, *e2))
+    blocks_b = [main, c1_up, c2, c1_down]
     blocks_a = [block_a, a1_up, a2_up, a3_up, a4[0], a4[1], a3_down, a2_down, a1_down]
 
     (mine,) = call(mine_kernel, "mine", [((512, 768), F32)], *blocks_b, scalars=0, limit=6)

time: 131 us -> 129 us (0.985)
  starting transfers between devices: 78 us -> 69 us
  waiting for transfers between devices: 34.8 us -> 41.6 us
    ppermute x9, starting transfers between devices: 24.6 us -> 18.3 us  [swap(): lax.ppermute(value, axis, [(i, i ^ mask) for i in range(SIZES[axis])])]
    ppermute x35 -> x34, waiting for transfers between devices: 27.7 us -> 32.4 us  [shift(): lax.ppermute(value, axis, [(i, (i + by) % size) for i in range(size)])]
    ppermute x35 -> x34, starting transfers between devices: 53.4 us -> 50.7 us  [shift(): lax.ppermute(value, axis, [(i, (i + by) % size) for i in range(size)])]
    ppermute x9, waiting for transfers between devices: 7.07 us -> 9.2 us  [swap(): lax.ppermute(value, axis, [(i, i ^ mask) for i in range(SIZES[axis])])]
  transfers between devices with their start and end apart: 44 -> 43, of which waited for: 17 -> 18; matrix products, arithmetic and copies ran while one was open for 0% -> 0% of each run, Pallas kernels for 6% -> 6%
where the time goes in v4:
time: 129 us
  starting transfers between devices  69 us (53%)
  waiting for transfers between devices  41.6 us (32%)
  Pallas kernels  14 us (11%)
  local copies, waits for them, and re-layouts  2.87 us (2%)
    ppermute x34, starting transfers between devices, shift(): lax.ppermute(value, axis, [(i, (i + by) % size) for i in range(size)])  50.7 us
    ppermute x34, waiting for transfers between devices, shift(): lax.ppermute(value, axis, [(i, (i + by) % size) for i in range(size)])  32.4 us
    ppermute x9, starting transfers between devices, swap(): lax.ppermute(value, axis, [(i, i ^ mask) for i in range(SIZES[axis])])  18.3 us
    pallas_call x15, Pallas kernels, call(): pl.pallas_call(kernel, name=name, out_shape=[jax.ShapeDtypeStruct(shape,...  14 us
    ppermute x9, waiting for transfers between devices, swap(): lax.ppermute(value, axis, [(i, i ^ mask) for i in range(SIZES[axis])])  9.2 us
    unnamed x9, local copies, waits for them, and re-layouts  2.8 us
  transfers between devices with their start and end apart: 43, of which 18 were waited for; matrix products, arithmetic and copies ran while one was open for 0% of the time, Pallas kernels for 6%

profile of v4, /device:TPU:1, one launch (start us, length us, event | category | flops | bytes accessed | tf_op | source)
XLA Modules:
  0.0 128.6 jit_solution(15208696756527453067)
XLA Ops:
  4.2 2.5 %collective-permute-start = (f32[16,1856]{1,0:T(8,128)S(1)}, f32[16,1856]{1,0:T(8,128)S(1)}, u32[]{:S(2)}, u32[]{:S(2)}) collective-permute-start(f32[16,1856]{1,0:T(8,128)S(1)} %get-tuple-element.70.refs_0_), channel_id=1, source_target_pairs={{0,32},{32,64},{64,96},{96,128},{128,160},{160,192},{192,224},{224... | collective-permute-start | bytes 356360 | tf_op jit(solution)/shard_map/ppermute | solution.py:17
  6.7 4.0 %collective-permute-start.1 = (f32[16,1856]{1,0:T(8,128)S(1)}, f32[16,1856]{1,0:T(8,128)S(1)}, u32[]{:S(2)}, u32[]{:S(2)}) collective-permute-start(f32[16,1856]{1,0:T(8,128)S(1)} %get-tuple-element.70.refs_0_), channel_id=1, source_target_pairs={{0,224},{32,0},{64,32},{96,64},{128,96},{160,128},{192,160},{224,1... | collective-permute-start | bytes 356360 | tf_op jit(solution)/shard_map/ppermute | solution.py:17
  10.7 3.0 %collective-permute-done.refs_1_ = f32[16,1856]{1,0:T(8,128)S(1)} collective-permute-done((f32[16,1856]{1,0:T(8,128)S(1)}, f32[16,1856]{1,0:T(8,128)S(1)}, u32[]{:S(2)}, u32[]{:S(2)}) %collective-permute-start) | collective-permute-done | bytes 118816 | tf_op jit(solution)/shard_map/ppermute | solution.py:17
  13.7 2.7 %collective-permute-start.5 = (f32[16,1856]{1,0:T(8,128)S(1)}, f32[16,1856]{1,0:T(8,128)S(1)}, u32[]{:S(2)}, u32[]{:S(2)}) collective-permute-start(f32[16,1856]{1,0:T(8,128)S(1)} %collective-permute-done.1.refs_7_), channel_id=1, source_target_pairs={{0,224},{32,0},{64,32},{96,64},{128,96},{160,128},{192,160},{224,1... | collective-permute-start | bytes 356360 | tf_op jit(solution)/shard_map/ppermute | solution.py:17
  17.6 3.7 %collective-permute-start.3 = (f32[16,1856]{1,0:T(8,128)S(1)}, f32[16,1856]{1,0:T(8,128)S(1)}, u32[]{:S(2)}, u32[]{:S(2)}) collective-permute-start(f32[16,1856]{1,0:T(8,128)S(1)} %get-tuple-element.70.refs_0_), channel_id=1, source_target_pairs={{0,128},{32,160},{64,192},{96,224},{128,0},{160,32},{192,64},{224,... | collective-permute-start | bytes 356360 | tf_op jit(solution)/shard_map/ppermute | solution.py:17
  21.3 2.5 %collective-permute-start.8 = (f32[16,1600]{1,0:T(8,128)S(1)}, f32[16,1600]{1,0:T(8,128)S(1)}, u32[]{:S(2)}, u32[]{:S(2)}) collective-permute-start(f32[16,1600]{1,0:T(8,128)S(1)} %get-tuple-element.73), channel_id=1, source_target_pairs={{0,16},{8,24},{16,0},{24,8},{1,17},{9,25},{17,1},{25,9},{2,18},{10... | collective-permute-start | bytes 307208 | tf_op jit(solution)/shard_map/ppermute | solution.py:17
  24.9 2.7 %collective-permute-start.6 = (f32[16,1856]{1,0:T(8,128)S(1)}, f32[16,1856]{1,0:T(8,128)S(1)}, u32[]{:S(2)}, u32[]{:S(2)}) collective-permute-start(f32[16,1856]{1,0:T(8,128)S(1)} %collective-permute-done.5.refs_6_), channel_id=1, source_target_pairs={{0,224},{32,0},{64,32},{96,64},{128,96},{160,128},{192,160},{224,1... | collective-permute-start | bytes 356360 | tf_op jit(solution)/shard_map/ppermute | solution.py:17
  27.6 2.6 %collective-permute-done.4.refs_3_ = f32[16,1856]{1,0:T(8,128)S(1)} collective-permute-done((f32[16,1856]{1,0:T(8,128)S(1)}, f32[16,1856]{1,0:T(8,128)S(1)}, u32[]{:S(2)}, u32[]{:S(2)}) %collective-permute-start.4) | collective-permute-done | bytes 118816 | tf_op jit(solution)/shard_map/ppermute | solution.py:17
  31.8 2.6 %collective-permute-start.13 = (f32[64,1600]{1,0:T(8,128)S(1)}, f32[64,1600]{1,0:T(8,128)S(1)}, u32[]{:S(2)}, u32[]{:S(2)}) collective-permute-start(f32[64,1600]{1,0:T(8,128)S(1)} %constant_dynamic-update-slice_fusion.refs_0_), channel_id=1, source_target_pairs={{0,224},{32,0},{64,32},{96,64},{128,96},{160,128},{192,160},{224,1... | collective-permute-start | bytes 1228808 | tf_op jit(solution)/shard_map/ppermute | solution.py:17
  37.6 3.2 %collective-permute-done.11.other = f32[320,128]{1,0:T(8,128)S(1)} collective-permute-done((f32[320,128]{1,0:T(8,128)S(1)}, f32[320,128]{1,0:T(8,128)S(1)}, u32[]{:S(2)}, u32[]{:S(2)}) %collective-permute-start.11) | collective-permute-done | bytes 163872 | tf_op jit(solution)/shard_map/ppermute | solution.py:21
  41.4 2.2 %collective-permute-start.15 = (f32[64,1600]{1,0:T(8,128)S(1)}, f32[64,1600]{1,0:T(8,128)S(1)}, u32[]{:S(2)}, u32[]{:S(2)}) collective-permute-start(f32[64,1600]{1,0:T(8,128)S(1)} %collective-permute-done.13.refs_8_), channel_id=1, source_target_pairs={{0,224},{32,0},{64,32},{96,64},{128,96},{160,128},{192,160},{224,1... | collective-permute-start | bytes 1228808 | tf_op jit(solution)/shard_map/ppermute | solution.py:17
  43.6 3.9 %collective-permute-done.10.refs_1_.refs_10_ = f32[8,16,1536]{2,1,0:T(8,128)S(1)} collective-permute-done((f32[8,16,1536]{2,1,0:T(8,128)S(1)}, f32[8,16,1536]{2,1,0:T(8,128)S(1)}, u32[]{:S(2)}, u32[]{:S(2)}) %collective-permute-start.10) | collective-permute-done | bytes 786464 | tf_op jit(solution)/shard_map/ppermute | solution.py:17
  48.1 3.0 %collective-permute-start.16 = (f32[128,128]{1,0:T(8,128)S(1)}, f32[128,128]{1,0:T(8,128)S(1)}, u32[]{:S(2)}, u32[]{:S(2)}) collective-permute-start(f32[128,128]{1,0:T(8,128)S(1)} %pair.1), channel_id=1, source_target_pairs={{0,4},{2,6},{4,0},{6,2},{1,5},{3,7},{5,1},{7,3},{8,12},{10,14},{12... | collective-permute-start | bytes 196616 | tf_op jit(solution)/shard_map/ppermute | solution.py:21
  52.9 2.6 %collective-permute-start.19 = (f32[64,1600]{1,0:T(8,128)S(1)}, f32[64,1600]{1,0:T(8,128)S(1)}, u32[]{:S(2)}, u32[]{:S(2)}) collective-permute-start(f32[64,1600]{1,0:T(8,128)S(1)} %collective-permute-done.15.refs_7_), channel_id=1, source_target_pairs={{0,224},{32,0},{64,32},{96,64},{128,96},{160,128},{192,160},{224,1... | collective-permute-start | bytes 1228808 | tf_op jit(solution)/shard_map/ppermute | solution.py:17
  58.0 5.4 %collective-permute-done.20.b3 = f32[128,768]{1,0:T(8,128)S(1)} collective-permute-done((f32[128,768]{1,0:T(8,128)S(1)}, f32[128,768]{1,0:T(8,128)S(1)}, u32[]{:S(2)}, u32[]{:S(2)}) %collective-permute-start.20) | collective-permute-done | bytes 393248 | tf_op jit(solution)/shard_map/ppermute | solution.py:17
  63.5 2.7 %collective-permute-start.22 = (f32[32,1600]{1,0:T(8,128)S(1)}, f32[32,1600]{1,0:T(8,128)S(1)}, u32[]{:S(2)}, u32[]{:S(2)}) collective-permute-start(f32[32,1600]{1,0:T(8,128)S(1)} %slice.13), channel_id=1, source_target_pairs={{0,224},{32,0},{64,32},{96,64},{128,96},{160,128},{192,160},{224,1... | collective-permute-start | bytes 614408 | tf_op jit(solution)/shard_map/ppermute | solution.py:17
  66.2 5.7 %collective-permute-done.24.b1 = f32[128,768]{1,0:T(8,128)S(1)} collective-permute-done((f32[128,768]{1,0:T(8,128)S(1)}, f32[128,768]{1,0:T(8,128)S(1)}, u32[]{:S(2)}, u32[]{:S(2)}) %collective-permute-start.24) | collective-permute-done | bytes 393248 | tf_op jit(solution)/shard_map/ppermute | solution.py:17
  74.7 3.9 %collective-permute-done.25.b2 = f32[64,768]{1,0:T(8,128)S(1)} collective-permute-done((f32[64,768]{1,0:T(8,128)S(1)}, f32[64,768]{1,0:T(8,128)S(1)}, u32[]{:S(2)}, u32[]{:S(2)}) %collective-permute-start.25) | collective-permute-done | bytes 196640 | tf_op jit(solution)/shard_map/ppermute | solution.py:17
  78.8 6.5 %collective-permute-start.27 = (f32[512,768]{1,0:T(8,128)S(1)}, f32[512,768]{1,0:T(8,128)S(1)}, u32[]{:S(2)}, u32[]{:S(2)}) collective-permute-start(f32[512,768]{1,0:T(8,128)S(1)} %mine.1), channel_id=1, source_target_pairs={{0,1},{1,0},{2,3},{3,2},{4,5},{5,4},{6,7},{7,6},{8,9},{9,8},{10,11... | collective-permute-start | bytes 4718600 | tf_op jit(solution)/shard_map/ppermute | solution.py:21
  85.3 2.3 %level3.1 = (bf16[2,512,2048]{2,1,0:T(8,128)(2,1)S(1)}, f32[256,512]{1,0:T(8,128)S(1)}, f32[512,128]{1,0:T(8,128)S(1)}, f32[64,1536]{1,0:T(8,128)S(1)}, f32[64,1536]{1,0:T(8,128)S(1)}, /*index=5*/f32[64,512]{1,0:T(8,128)S(1)}) custom-call(s32[4]{0:T(128)S(1)} %pad_add_fusion.place, f32[64,1600]{1,0:T(8,128)S(1)} %constant_dynamic-update-slice_fusion.refs_0_, ...), custom_call_target="tpu_custom_call" | custom-call | tf_op jit(solution)/shard_map/level3/pallas_call | solution.py:254
  92.5 4.2 %collective-permute-start.34 = (f32[512,128]{1,0:T(8,128)S(1)}, f32[512,128]{1,0:T(8,128)S(1)}, u32[]{:S(2)}, u32[]{:S(2)}) collective-permute-start(f32[512,128]{1,0:T(8,128)S(1)} %get-tuple-element.122.p0), channel_id=1, source_target_pairs={{0,16},{8,24},{16,0},{24,8},{1,17},{9,25},{17,1},{25,9},{2,18},{10... | collective-permute-start | bytes 786440 | tf_op jit(solution)/shard_map/ppermute | solution.py:17
  99.6 3.0 %collective-permute-start.31 = (f32[64,512]{1,0:T(8,128)S(1)}, f32[64,512]{1,0:T(8,128)S(1)}, u32[]{:S(2)}, u32[]{:S(2)}) collective-permute-start(f32[64,512]{1,0:T(8,128)S(1)} %get-tuple-element.108.up_ref), channel_id=1, source_target_pairs={{0,4},{2,6},{4,0},{6,2},{1,5},{3,7},{5,1},{7,3},{8,12},{10,14},{12... | collective-permute-start | bytes 393224 | tf_op jit(solution)/shard_map/ppermute | solution.py:21
  105.6 2.8 %collective-permute-done.34.p2 = f32[512,128]{1,0:T(8,128)S(1)} collective-permute-done((f32[512,128]{1,0:T(8,128)S(1)}, f32[512,128]{1,0:T(8,128)S(1)}, u32[]{:S(2)}, u32[]{:S(2)}) %collective-permute-start.34) | collective-permute-done | bytes 262176 | tf_op jit(solution)/shard_map/ppermute | solution.py:17
  111.7 3.0 %collective-permute-start.41 = (f32[384,128]{1,0:T(8,128)S(1)}, f32[384,128]{1,0:T(8,128)S(1)}, u32[]{:S(2)}, u32[]{:S(2)}) collective-permute-start(f32[384,128]{1,0:T(8,128)S(1)} %rows.1.r0), channel_id=1, source_target_pairs={{0,16},{8,24},{16,0},{24,8},{1,17},{9,25},{17,1},{25,9},{2,18},{10... | collective-permute-start | bytes 589832 | tf_op jit(solution)/shard_map/ppermute | solution.py:17
  (92 shorter events, 46.9 us)
Async XLA Ops:
  4.2 9.5 %collective-permute-start = (f32[16,1856]{1,0:T(8,128)S(1)}, f32[16,1856]{1,0:T(8,128)S(1)}, u32[]{:S(2)}, u32[]{:S(2)}) collective-permute-start(f32[16,1856]{1,0:T(8,128)S(1)} %get-tuple-element.70.refs_0_), channel_id=1, source_target_pairs={{0,32},{32,64},{64,96},{96,128},{128,160},{160,192},{192,224},{224... | collective-permute-start | bytes 356360 | tf_op jit(solution)/shard_map/ppermute | solution.py:17
  13.7 11.2 %collective-permute-start.2 = (f32[16,1856]{1,0:T(8,128)S(1)}, f32[16,1856]{1,0:T(8,128)S(1)}, u32[]{:S(2)}, u32[]{:S(2)}) collective-permute-start(f32[16,1856]{1,0:T(8,128)S(1)} %collective-permute-done.refs_1_), channel_id=1, source_target_pairs={{0,32},{32,64},{64,96},{96,128},{128,160},{160,192},{192,224},{224... | collective-permute-start | bytes 356360 | tf_op jit(solution)/shard_map/ppermute | solution.py:17
  13.7 11.2 %collective-permute-start.5 = (f32[16,1856]{1,0:T(8,128)S(1)}, f32[16,1856]{1,0:T(8,128)S(1)}, u32[]{:S(2)}, u32[]{:S(2)}) collective-permute-start(f32[16,1856]{1,0:T(8,128)S(1)} %collective-permute-done.1.refs_7_), channel_id=1, source_target_pairs={{0,224},{32,0},{64,32},{96,64},{128,96},{160,128},{192,160},{224,1... | collective-permute-start | bytes 356360 | tf_op jit(solution)/shard_map/ppermute | solution.py:17
  17.6 10.0 %collective-permute-start.3 = (f32[16,1856]{1,0:T(8,128)S(1)}, f32[16,1856]{1,0:T(8,128)S(1)}, u32[]{:S(2)}, u32[]{:S(2)}) collective-permute-start(f32[16,1856]{1,0:T(8,128)S(1)} %get-tuple-element.70.refs_0_), channel_id=1, source_target_pairs={{0,128},{32,160},{64,192},{96,224},{128,0},{160,32},{192,64},{224,... | collective-permute-start | bytes 356360 | tf_op jit(solution)/shard_map/ppermute | solution.py:17
  30.7 16.7 %collective-permute-start.10 = (f32[8,16,1536]{2,1,0:T(8,128)S(1)}, f32[8,16,1536]{2,1,0:T(8,128)S(1)}, u32[]{:S(2)}, u32[]{:S(2)}) collective-permute-start(f32[8,16,1536]{2,1,0:T(8,128)S(1)} %get-tuple-element.78.refs_0_.refs_9_), channel_id=1, source_target_pairs={{0,8},{8,16},{16,24},{24,0},{1,9},{9,17},{17,25},{25,1},{2,10},{10... | collective-permute-start | bytes 2359304 | tf_op jit(solution)/shard_map/ppermute | solution.py:17
  31.7 9.2 %collective-permute-start.12 = (f32[64,1600]{1,0:T(8,128)S(1)}, f32[64,1600]{1,0:T(8,128)S(1)}, u32[]{:S(2)}, u32[]{:S(2)}) collective-permute-start(f32[64,1600]{1,0:T(8,128)S(1)} %constant_dynamic-update-slice_fusion.refs_0_), channel_id=1, source_target_pairs={{0,32},{32,64},{64,96},{96,128},{128,160},{160,192},{192,224},{224... | collective-permute-start | bytes 1228808 | tf_op jit(solution)/shard_map/ppermute | solution.py:17
  31.8 9.1 %collective-permute-start.13 = (f32[64,1600]{1,0:T(8,128)S(1)}, f32[64,1600]{1,0:T(8,128)S(1)}, u32[]{:S(2)}, u32[]{:S(2)}) collective-permute-start(f32[64,1600]{1,0:T(8,128)S(1)} %constant_dynamic-update-slice_fusion.refs_0_), channel_id=1, source_target_pairs={{0,224},{32,0},{64,32},{96,64},{128,96},{160,128},{192,160},{224,1... | collective-permute-start | bytes 1228808 | tf_op jit(solution)/shard_map/ppermute | solution.py:17
  34.4 18.4 %collective-permute-start.17 = (f32[8,16,1536]{2,1,0:T(8,128)S(1)}, f32[8,16,1536]{2,1,0:T(8,128)S(1)}, u32[]{:S(2)}, u32[]{:S(2)}) collective-permute-start(f32[8,16,1536]{2,1,0:T(8,128)S(1)} %get-tuple-element.78.refs_0_.refs_9_), channel_id=1, source_target_pairs={{0,24},{8,0},{16,8},{24,16},{1,25},{9,1},{17,9},{25,17},{2,26},{10... | collective-permute-start | bytes 2359304 | tf_op jit(solution)/shard_map/ppermute | solution.py:17
  40.9 11.9 %collective-permute-start.14 = (f32[64,1600]{1,0:T(8,128)S(1)}, f32[64,1600]{1,0:T(8,128)S(1)}, u32[]{:S(2)}, u32[]{:S(2)}) collective-permute-start(f32[64,1600]{1,0:T(8,128)S(1)} %collective-permute-done.12.refs_1_), channel_id=1, source_target_pairs={{0,32},{32,64},{64,96},{96,128},{128,160},{160,192},{192,224},{224... | collective-permute-start | bytes 1228808 | tf_op jit(solution)/shard_map/ppermute | solution.py:17
  41.4 11.5 %collective-permute-start.15 = (f32[64,1600]{1,0:T(8,128)S(1)}, f32[64,1600]{1,0:T(8,128)S(1)}, u32[]{:S(2)}, u32[]{:S(2)}) collective-permute-start(f32[64,1600]{1,0:T(8,128)S(1)} %collective-permute-done.13.refs_8_), channel_id=1, source_target_pairs={{0,224},{32,0},{64,32},{96,64},{128,96},{160,128},{192,160},{224,1... | collective-permute-start | bytes 1228808 | tf_op jit(solution)/shard_map/ppermute | solution.py:17
  47.5 31.2 %collective-permute-start.23 = (f32[8,16,1536]{2,1,0:T(8,128)S(1)}, f32[8,16,1536]{2,1,0:T(8,128)S(1)}, u32[]{:S(2)}, u32[]{:S(2)}) collective-permute-start(f32[8,16,1536]{2,1,0:T(8,128)S(1)} %collective-permute-done.10.refs_1_.refs_10_), channel_id=1, source_target_pairs={{0,8},{8,16},{16,24},{24,0},{1,9},{9,17},{17,25},{25,1},{2,10},{10... | collective-permute-start | bytes 2359304 | tf_op jit(solution)/shard_map/ppermute | solution.py:17
  52.8 10.5 %collective-permute-start.18 = (f32[64,1600]{1,0:T(8,128)S(1)}, f32[64,1600]{1,0:T(8,128)S(1)}, u32[]{:S(2)}, u32[]{:S(2)}) collective-permute-start(f32[64,1600]{1,0:T(8,128)S(1)} %collective-permute-done.14.refs_2_), channel_id=1, source_target_pairs={{0,32},{32,64},{64,96},{96,128},{128,160},{160,192},{192,224},{224... | collective-permute-start | bytes 1228808 | tf_op jit(solution)/shard_map/ppermute | solution.py:17
  52.9 10.4 %collective-permute-start.19 = (f32[64,1600]{1,0:T(8,128)S(1)}, f32[64,1600]{1,0:T(8,128)S(1)}, u32[]{:S(2)}, u32[]{:S(2)}) collective-permute-start(f32[64,1600]{1,0:T(8,128)S(1)} %collective-permute-done.15.refs_7_), channel_id=1, source_target_pairs={{0,224},{32,0},{64,32},{96,64},{128,96},{160,128},{192,160},{224,1... | collective-permute-start | bytes 1228808 | tf_op jit(solution)/shard_map/ppermute | solution.py:17
  57.8 14.1 %collective-permute-start.24 = (f32[128,768]{1,0:T(8,128)S(1)}, f32[128,768]{1,0:T(8,128)S(1)}, u32[]{:S(2)}, u32[]{:S(2)}) collective-permute-start(f32[128,768]{1,0:T(8,128)S(1)} %slab.1.b0), channel_id=1, source_target_pairs={{0,8},{8,16},{16,24},{24,0},{1,9},{9,17},{17,25},{25,1},{2,10},{10... | collective-permute-start | bytes 1179656 | tf_op jit(solution)/shard_map/ppermute | solution.py:17
  63.4 15.3 %collective-permute-start.21 = (f32[32,1600]{1,0:T(8,128)S(1)}, f32[32,1600]{1,0:T(8,128)S(1)}, u32[]{:S(2)}, u32[]{:S(2)}) collective-permute-start(f32[32,1600]{1,0:T(8,128)S(1)} %slice.12), channel_id=1, source_target_pairs={{0,32},{32,64},{64,96},{96,128},{128,160},{160,192},{192,224},{224... | collective-permute-start | bytes 614408 | tf_op jit(solution)/shard_map/ppermute | solution.py:17
  63.5 15.2 %collective-permute-start.22 = (f32[32,1600]{1,0:T(8,128)S(1)}, f32[32,1600]{1,0:T(8,128)S(1)}, u32[]{:S(2)}, u32[]{:S(2)}) collective-permute-start(f32[32,1600]{1,0:T(8,128)S(1)} %slice.13), channel_id=1, source_target_pairs={{0,224},{32,0},{64,32},{96,64},{128,96},{160,128},{192,160},{224,1... | collective-permute-start | bytes 614408 | tf_op jit(solution)/shard_map/ppermute | solution.py:17
  78.8 10.7 %collective-permute-start.27 = (f32[512,768]{1,0:T(8,128)S(1)}, f32[512,768]{1,0:T(8,128)S(1)}, u32[]{:S(2)}, u32[]{:S(2)}) collective-permute-start(f32[512,768]{1,0:T(8,128)S(1)} %mine.1), channel_id=1, source_target_pairs={{0,1},{1,0},{2,3},{3,2},{4,5},{5,4},{6,7},{7,6},{8,9},{9,8},{10,11... | collective-permute-start | bytes 4718600 | tf_op jit(solution)/shard_map/ppermute | solution.py:21
  92.5 13.0 %collective-permute-start.33 = (f32[512,128]{1,0:T(8,128)S(1)}, f32[512,128]{1,0:T(8,128)S(1)}, u32[]{:S(2)}, u32[]{:S(2)}) collective-permute-start(f32[512,128]{1,0:T(8,128)S(1)} %get-tuple-element.122.p0), channel_id=1, source_target_pairs={{0,8},{8,16},{16,24},{24,0},{1,9},{9,17},{17,25},{25,1},{2,10},{10... | collective-permute-start | bytes 786440 | tf_op jit(solution)/shard_map/ppermute | solution.py:17
  92.5 15.8 %collective-permute-start.34 = (f32[512,128]{1,0:T(8,128)S(1)}, f32[512,128]{1,0:T(8,128)S(1)}, u32[]{:S(2)}, u32[]{:S(2)}) collective-permute-start(f32[512,128]{1,0:T(8,128)S(1)} %get-tuple-element.122.p0), channel_id=1, source_target_pairs={{0,16},{8,24},{16,0},{24,8},{1,17},{9,25},{17,1},{25,9},{2,18},{10... | collective-permute-start | bytes 786440 | tf_op jit(solution)/shard_map/ppermute | solution.py:17
  96.8 11.6 %collective-permute-start.35 = (f32[512,128]{1,0:T(8,128)S(1)}, f32[512,128]{1,0:T(8,128)S(1)}, u32[]{:S(2)}, u32[]{:S(2)}) collective-permute-start(f32[512,128]{1,0:T(8,128)S(1)} %get-tuple-element.122.p0), channel_id=1, source_target_pairs={{0,24},{8,0},{16,8},{24,16},{1,25},{9,1},{17,9},{25,17},{2,26},{10... | collective-permute-start | bytes 786440 | tf_op jit(solution)/shard_map/ppermute | solution.py:17
  111.7 12.2 %collective-permute-start.41 = (f32[384,128]{1,0:T(8,128)S(1)}, f32[384,128]{1,0:T(8,128)S(1)}, u32[]{:S(2)}, u32[]{:S(2)}) collective-permute-start(f32[384,128]{1,0:T(8,128)S(1)} %rows.1.r0), channel_id=1, source_target_pairs={{0,16},{8,24},{16,0},{24,8},{1,17},{9,25},{17,1},{25,9},{2,18},{10... | collective-permute-start | bytes 589832 | tf_op jit(solution)/shard_map/ppermute | solution.py:17
  114.7 9.2 %collective-permute-start.42 = (f32[384,128]{1,0:T(8,128)S(1)}, f32[384,128]{1,0:T(8,128)S(1)}, u32[]{:S(2)}, u32[]{:S(2)}) collective-permute-start(f32[384,128]{1,0:T(8,128)S(1)} %rows.1.r0), channel_id=1, source_target_pairs={{0,24},{8,0},{16,8},{24,16},{1,25},{9,1},{17,9},{25,17},{2,26},{10... | collective-permute-start | bytes 589832 | tf_op jit(solution)/shard_map/ppermute | solution.py:17
  116.5 9.2 %collective-permute-start.37 = (f32[128,128]{1,0:T(8,128)S(1)}, f32[128,128]{1,0:T(8,128)S(1)}, u32[]{:S(2)}, u32[]{:S(2)}) collective-permute-start(f32[128,128]{1,0:T(8,128)S(1)} %get-tuple-element.119), channel_id=1, source_target_pairs={{0,8},{8,16},{16,24},{24,0},{1,9},{9,17},{17,25},{25,1},{2,10},{10... | collective-permute-start | bytes 196616 | tf_op jit(solution)/shard_map/ppermute | solution.py:17
  118.0 8.7 %collective-permute-start.38 = (f32[128,128]{1,0:T(8,128)S(1)}, f32[128,128]{1,0:T(8,128)S(1)}, u32[]{:S(2)}, u32[]{:S(2)}) collective-permute-start(f32[128,128]{1,0:T(8,128)S(1)} %get-tuple-element.120), channel_id=1, source_target_pairs={{0,16},{8,24},{16,0},{24,8},{1,17},{9,25},{17,1},{25,9},{2,18},{10... | collective-permute-start | bytes 196616 | tf_op jit(solution)/shard_map/ppermute | solution.py:17
  (22 other events, 113.7 us)
